TPU v7x, 32 devices: a whole 2x2x4 slice. The times are simulated.
32 devices in a mesh: band: 4 (over x, core), gvec: 2 (over y), dom: 4 (over z).
Axes of the slice: x: 2, y: 2, z: 4, core: 2. Of those that a mesh axis runs over, the one named last changes fastest.
Arguments:
- coeffs: bfloat16 [16, 128, 128, 128], P(('band', 'dom'), 'gvec'), may hold values from -1.5 to 1.5
- v_local: bfloat16 [128, 128, 128], P(None, 'gvec'), may hold values from -4 to 4
- atom_pos: float32 [3, 32768], P(None, ('band', 'gvec', 'dom')), may hold values from -32 to 160
- atom_charge: float32 [32768], P(('band', 'gvec', 'dom')), may hold values from -1 to 1
- near_list: int32 [512], P(('band', 'gvec', 'dom')), may hold values from 0 to 1023, as said below
- live_count: int32 [32], P(('band', 'gvec', 'dom')), may hold values from 0 to 16, as said below
Outputs:
- waves_new: bfloat16 [16, 128, 128, 128], P(('band', 'dom'), 'gvec')
- energies: float32 [16], P(('band', 'dom'))
- resid_ratio: float32 [16], P(('band', 'dom'))
- atom_force: float32 [3, 32768], P(None, ('band', 'gvec', 'dom'))
- totals: float32 [8], replicated
Inputs may be any that keep to these rules, and one draw needn't show every extreme that they name: `live_count`: the counts of all devices sum to exactly 128; some device has all 16 slots live; a device's live slots are its first ones. `near_list`: indices of the device's own atoms; the 16 entries of one device's block are distinct.
All inputs are finite; a program needn't handle non-finite values.
Results may differ from a plain program's by a relative error of at most 0.0045.
Values may be sent and summed in bfloat16 or wider, within the bound.
A program may use at most 64 MiB of HBM per device.

v0:
```python
import jax
import jax.numpy as jnp
from jax import lax
from jax.sharding import PartitionSpec as P

sigma_fractions = (1.0 / 32.0, 1.0 / 16.0, 1.0 / 8.0, 1.0 / 4.0)
kernel_weights = (1.0, 0.5, 0.25, 0.125)
force_unit = 1.0 / 4096.0
step_size = 0.5


def cosine_table(length):
    points = jnp.arange(length).astype(jnp.float32)
    angles = jnp.pi * (points[:, None] + 0.5) * points[None, :] / length
    scales = jnp.where(points == 0.0, jnp.sqrt(1.0 / length), jnp.sqrt(2.0 / length))
    return (jnp.cos(angles) * scales[None, :]).astype(jnp.bfloat16)


def occupancy(band_index, band_total):
    shifted = band_index.astype(jnp.float32) - 0.5 * band_total
    return 2.0 / (1.0 + jnp.exp(shifted / (0.125 * band_total)))


def kernels(points, centres, extent):
    values = []
    slopes = []
    for fraction in sigma_fractions:
        exponent = 0.5 / (extent * fraction) ** 2
        offset = points[:, None] - centres[None, :]
        gauss_value = jnp.exp(-exponent * offset * offset)
        values.append(gauss_value)
        slopes.append(2.0 * exponent * offset * gauss_value)
    return (jnp.concatenate(values, axis=1), jnp.concatenate(slopes, axis=1))


def charge_work(charges, density, x_start, y_start, extent, block_width):
    x_count, y_count, z_count = density.shape
    density_rows = density.reshape(x_count * y_count, z_count).astype(jnp.bfloat16)
    x_points = (x_start + jnp.arange(x_count)).astype(jnp.float32)
    y_points = (y_start + jnp.arange(y_count)).astype(jnp.float32)
    z_points = jnp.arange(z_count).astype(jnp.float32)
    weights = jnp.array(kernel_weights, jnp.float32)
    slot_total = charges.shape[1]
    blocks = charges.reshape(4, slot_total // block_width, block_width).transpose(1, 0, 2)

    def one_block(potential, block_now):
        x_value, x_slope = kernels(x_points, block_now[0], extent)
        y_value, y_slope = kernels(y_points, block_now[1], extent)
        z_value, z_slope = kernels(z_points, block_now[2], extent)
        scaled = (weights[:, None] * block_now[3][None, :]).reshape(-1)
        plane = (
            (x_value[:, None, :] * y_value[None, :, :])
            .reshape(x_count * y_count, -1)
            .astype(jnp.bfloat16)
        )
        depth = (scaled[None, :] * z_value).astype(jnp.bfloat16)
        potential = potential + lax.dot_general(
            plane, depth, (((1,), (1,)), ((), ())), preferred_element_type=jnp.float32
        )
        tables = jnp.concatenate([z_value, z_slope], axis=1).astype(jnp.bfloat16)
        projected = jnp.dot(density_rows, tables, preferred_element_type=jnp.float32).reshape(
            x_count, y_count, 2, -1
        )
        grid_part = projected[:, :, 0, :]
        slope_part = projected[:, :, 1, :]
        along_y = jnp.sum(grid_part * y_value[None], axis=1)
        slope_y = jnp.sum(grid_part * y_slope[None], axis=1)
        depth_y = jnp.sum(slope_part * y_value[None], axis=1)
        force_x = jnp.sum(x_slope * along_y, axis=0)
        force_y = jnp.sum(x_value * slope_y, axis=0)
        force_z = jnp.sum(x_value * depth_y, axis=0)
        stacked = jnp.stack([force_x, force_y, force_z]) * scaled[None, :]
        forces = -force_unit * jnp.sum(stacked.reshape(3, len(kernel_weights), -1), axis=1)
        return (potential, forces)

    start = jnp.zeros((x_count * y_count, z_count), jnp.float32)
    potential, forces = lax.scan(one_block, start, blocks)
    return (
        potential.reshape(x_count, y_count, z_count),
        forces.transpose(1, 0, 2).reshape(3, slot_total),
    )


def stress_terms(weighted, x_wave, y_wave):
    over_z = jnp.sum(weighted, axis=2)
    over_y = jnp.sum(weighted, axis=1)
    over_x = jnp.sum(weighted, axis=0)
    stress_xx = jnp.sum(x_wave * x_wave * jnp.sum(over_z, axis=1))
    stress_yy = jnp.sum(y_wave * y_wave * jnp.sum(over_z, axis=0))
    stress_zz = jnp.sum(y_wave * y_wave * jnp.sum(over_y, axis=0))
    stress_xy = jnp.sum(x_wave[:, None] * y_wave[None, :] * over_z)
    stress_xz = jnp.sum(x_wave[:, None] * y_wave[None, :] * over_y)
    stress_yz = jnp.sum(y_wave[:, None] * y_wave[None, :] * over_x)
    return jnp.stack([stress_xx, stress_yy, stress_zz, stress_xy, stress_xz, stress_yz])


def per_device(coeffs, v_local, atom_pos, atom_charge, near_list, live_count):
    local_bands, x_local, extent, _ = coeffs.shape
    cosines = cosine_table(extent)
    gvec_id = lax.axis_index("gvec")
    group_id = lax.axis_index(("band", "dom"))
    groups = lax.axis_size(("band", "dom"))
    band_total = local_bands * groups
    cell_count = float(extent**3)
    band_ids = group_id * local_bands + jnp.arange(local_bands)
    weight = occupancy(band_ids, band_total)
    capacity = near_list.shape[0]
    live_mask = (jnp.arange(capacity) < live_count[0]).astype(jnp.float32)
    picked_pos = jnp.take(atom_pos, near_list, axis=1)
    picked_charge = jnp.take(atom_charge, near_list) * live_mask
    own_block = jnp.concatenate([picked_pos, picked_charge[None, :], live_mask[None, :]], axis=0)
    all_blocks = lax.all_gather(own_block, ("band", "gvec", "dom"), axis=1, tiled=True)
    live_total = all_blocks.shape[1] // 4
    block_width = min(1024, live_total)
    target = jnp.where(
        all_blocks[4] > 0.5, jnp.cumsum(all_blocks[4]) - 1.0, float(live_total)
    ).astype(jnp.int32)
    charges = jnp.zeros((4, live_total), jnp.float32).at[:, target].set(all_blocks[:4], mode="drop")
    sectioned = jnp.einsum(
        "naql,zl->naqz", coeffs, cosines, preferred_element_type=jnp.float32
    ).astype(jnp.bfloat16)
    sectioned = jnp.einsum(
        "naqz,yq->nayz", sectioned, cosines, preferred_element_type=jnp.float32
    ).astype(jnp.bfloat16)
    exchanged = lax.all_to_all(sectioned, "gvec", split_axis=2, concat_axis=1, tiled=True)
    real_space = jnp.einsum(
        "nayz,xa->nxyz", exchanged, cosines, preferred_element_type=jnp.float32
    ).astype(jnp.bfloat16)
    x_share = extent // groups
    y_share = exchanged.shape[2]
    x_start = group_id * x_share
    y_start = gvec_id * y_share
    wide_real = real_space.astype(jnp.float32)
    partial_value = jnp.sum(weight[:, None, None, None] * wide_real * wide_real, axis=0)
    density = lax.psum_scatter(
        partial_value.astype(jnp.bfloat16), ("band", "dom"), scatter_dimension=0, tiled=True
    ).astype(jnp.float32)
    potential, forces = charge_work(charges, density, x_start, y_start, extent, block_width)
    slab_field = lax.all_gather(potential.astype(jnp.bfloat16), ("band", "dom"), axis=0, tiled=True)
    field_total = v_local.astype(jnp.float32) + slab_field.astype(jnp.float32)
    applied = (field_total[None] * wide_real).astype(jnp.bfloat16)
    embedding = jnp.sum(density * potential) / cell_count
    padded = jnp.take(forces, jnp.minimum(target, live_total - 1), axis=1) * all_blocks[4][None, :]
    mine = lax.psum_scatter(padded, ("band", "gvec", "dom"), scatter_dimension=1, tiled=True)
    atom_force = jnp.zeros((3, atom_pos.shape[1]), jnp.float32).at[:, near_list].add(mine)
    back_one = jnp.einsum(
        "nxyz,xa->nayz", applied, cosines, preferred_element_type=jnp.float32
    ).astype(jnp.bfloat16)
    returned = lax.all_to_all(back_one, "gvec", split_axis=1, concat_axis=2, tiled=True)
    back_two = jnp.einsum(
        "nayz,yq->naqz", returned, cosines, preferred_element_type=jnp.float32
    ).astype(jnp.bfloat16)
    wave_field = jnp.einsum("naqz,zl->naql", back_two, cosines, preferred_element_type=jnp.float32)
    wave_step = jnp.pi / extent
    x_wave = (gvec_id * x_local + jnp.arange(x_local)).astype(jnp.float32) * wave_step
    y_wave = jnp.arange(extent).astype(jnp.float32) * wave_step
    kinetic = 0.5 * (
        x_wave[:, None, None] ** 2 + y_wave[None, :, None] ** 2 + y_wave[None, None, :] ** 2
    )
    coeff_wide = coeffs.astype(jnp.float32)
    image = kinetic[None] * coeff_wide + wave_field
    norm_sq = jnp.sum(coeff_wide * coeff_wide, axis=(1, 2, 3))
    intersection = jnp.sum(coeff_wide * image, axis=(1, 2, 3))
    weighted = jnp.sum(weight[:, None, None, None] * coeff_wide * coeff_wide, axis=0)
    stress_local = stress_terms(weighted, x_wave, y_wave) / cell_count
    local_totals = jnp.concatenate([stress_local, embedding[None]])
    spread = (jnp.arange(band_total)[None, :] == band_ids[:, None]).astype(jnp.float32)
    norm_vec = jnp.sum(spread * norm_sq[:, None], axis=0)
    intersection_vec = jnp.sum(spread * intersection[:, None], axis=0)
    norm_all, intersection_all, summed = lax.psum(
        (norm_vec, intersection_vec, local_totals), ("band", "gvec", "dom")
    )
    energy_all = intersection_all / norm_all
    energies = jnp.sum(spread * energy_all[None, :], axis=1)
    residual = image - energies[:, None, None, None] * coeff_wide
    resid_sq = lax.psum(jnp.sum(residual * residual, axis=(1, 2, 3)), "gvec")
    norm_mine = jnp.sum(spread * norm_all[None, :], axis=1)
    resid_ratio = resid_sq / norm_mine
    waves_new = (coeff_wide - step_size * residual / (1.0 + kinetic[None])).astype(jnp.bfloat16)
    band_energy = jnp.sum(occupancy(jnp.arange(band_total), band_total) * energy_all) / band_total
    totals = jnp.concatenate([summed, band_energy[None]])
    return (waves_new, energies, resid_ratio, atom_force, totals)


def solution(mesh):
    return jax.shard_map(
        per_device,
        mesh=mesh,
        in_specs=(
            P(("band", "dom"), "gvec", None, None),
            P(None, "gvec", None),
            P(None, ("band", "gvec", "dom")),
            P(("band", "gvec", "dom")),
            P(("band", "gvec", "dom")),
            P(("band", "gvec", "dom")),
        ),
        out_specs=(
            P(("band", "dom"), "gvec", None, None),
            P(("band", "dom")),
            P(("band", "dom")),
            P(None, ("band", "gvec", "dom")),
            P(),
        ),
        check_vma=False,
    )
```

profile of v0, /device:TPU:0, one launch (start us, length us, event | category | flops | bytes accessed | tf_op | source)
XLA Modules:
  0.0 384.4 jit_solution(9661353968709335428)
XLA Ops:
  7.2 0.7 compare_select_fusion.3
  8.6 1.1 copy.74
  9.7 0.6 gather_fusion.1
  10.3 0.6 gather_fusion
  10.9 0.7 fusion.111
  11.9 70.8 %all-gather = f32[32,16,5]{1,2,0:T(8,128)S(1)} all-gather(f32[1,16,5]{1,2,0:T(8,128)S(1)} %bitcast.161), channel_id=1, replica_groups=mesh['band'=4,'gvec'=2,'dom'=4] {'band','gvec','dom'}, dimensions={0}, use_global_device_ids=true | all-gather | bytes 10560 | tf_op jit(solution)/shard_map/all_gather | solution.py:112
  82.8 0.3 reduce-window.9
  83.4 0.1 copy.78
  83.6 1.7 scatter_custom_fusion
  85.3 0.2 slice_reduce_fusion.1
  86.0 1.0 fusion.125
  87.0 3.0 convert_bitcast_fusion.1
  90.0 4.3 %copy.80 = bf16[1,64,128,128]{3,1,0,2:T(8,128)(2,1)} copy(bf16[1,64,128,128]{3,2,1,0:T(8,128)(2,1)} %convert_bitcast_fusion.1) | data formatting | bytes 4194304 | tf_op jit(solution)/shard_map/convert_element_type | solution.py:124
  94.3 4.8 %all-to-all-start = ((bf16[1,64,128,128]{3,1,0,2:T(8,128)(2,1)}), bf16[1,64,128,128]{3,1,0,2:T(8,128)(2,1)}, u32[]{:S(2)}, u32[]{:S(2)}) async-start(bf16[1,64,128,128]{3,1,0,2:T(8,128)(2,1)} %copy.80), calls=%async_computation | async-start | bytes 4194304 | tf_op jit(solution)/shard_map/all_to_all | solution.py:125
  99.2 0.2 reduce-scatter.3.cloned.1.call-start
  100.0 19.0 %all-to-all-done = bf16[1,64,128,128]{3,1,0,2:T(8,128)(2,1)} async-done(((bf16[1,64,128,128]{3,1,0,2:T(8,128)(2,1)}), bf16[1,64,128,128]{3,1,0,2:T(8,128)(2,1)}, u32[]{:S(2)}, u32[]{:S(2)}) %all-to-all-start) | async-done | bytes 2097184 | tf_op jit(solution)/shard_map/all_to_all | solution.py:125
  119.0 1.8 copy.81
  120.8 2.3 fusion.79
  123.1 2.1 all-gather.3.cloned.1.call-done
  125.1 6.9 %fusion.7 = (bf16[128,64,128]{2,1,0:T(8,128)(2,1)}, bf16[128,64,128]{2,1,0:T(8,128)(2,1)}) fusion(f32[]{:T(128)S(6)} %div.58, bf16[128,64,128]{2,0,1:T(8,128)(2,1)} %fusion.79, bf16[128,64,128]{2,1,0:T(8,128)(2,1)} %all-gather.3.cloned.1.call-done, bf16[128,64,128]{2,1,0:T(8,128)(2,1)} %param.8), kind=kLoop, calls=%fused_computation.21 | loop fusion | flops 9437184 | bytes 10485764 | tf_op jit(solution)/shard_map/convert_element_type | solution.py:136
  132.1 3.6 convert_bitcast_fusion
  135.8 2.7 copy.85
  138.4 4.9 %all-to-all-start.1 = ((bf16[1,128,64,128]{3,2,0,1:T(8,128)(2,1)}), bf16[1,128,64,128]{3,2,0,1:T(8,128)(2,1)}, u32[]{:S(2)}, u32[]{:S(2)}) async-start(bf16[1,128,64,128]{3,2,0,1:T(8,128)(2,1)} %copy.85), calls=%async_computation.1 | async-start | bytes 4194304 | tf_op jit(solution)/shard_map/all_to_all | solution.py:149
  143.6 0.2 copy.88
  143.9 25.0 %all-to-all-done.1 = bf16[1,128,64,128]{3,2,0,1:T(8,128)(2,1)} async-done(((bf16[1,128,64,128]{3,2,0,1:T(8,128)(2,1)}), bf16[1,128,64,128]{3,2,0,1:T(8,128)(2,1)}, u32[]{:S(2)}, u32[]{:S(2)}) %all-to-all-start.1) | async-done | bytes 2097184 | tf_op jit(solution)/shard_map/all_to_all | solution.py:149
  168.9 3.2 copy.86
  172.1 7.9 %fusion = (f32[128,128]{1,0:T(8,128)S(1)}, f32[128]{0:T(128)S(1)}, f32[64,128]{1,0:T(8,128)S(1)}, f32[64,128]{1,0:T(8,128)S(1)}, f32[]{:T(128)}, /*index=5*/f32[...) fusion(bf16[1,64,128,128]{3,2,1,0:T(8,128)(2,1)S(1)} %copy-done.1, f32[]{:T(128)S(6)} %div.58, ...), kind=kOutput, calls=%fused_computation.13 | convolution fusion | flops 555843264 | bytes 8555788 | tf_op jit(solution)/shard_map/naqz,zl->naql/dot_general | solution.py:153
  180.0 0.6 multiply_reduce_fusion.7
  180.6 0.7 multiply_reduce_fusion.4
  181.3 0.6 multiply_reduce_fusion.9
  181.9 0.7 fusion.61
  182.6 3.8 stack.47
  186.4 1.3 fusion.113
  187.7 5.0 %reduce-scatter.3.cloned.1.call-done = bf16[8,64,128]{2,1,0:T(8,128)(2,1)} async-done(((bf16[128,64,128]{2,1,0:T(8,128)(2,1)}), bf16[8,64,128]{2,1,0:T(8,128)(2,1)}) %reduce-scatter.3.cloned.1.call-update) | async-done | bytes 131088 | tf_op jit(solution)/shard_map/reduce_scatter | solution.py:135
  192.7 1.6 multiply_reduce_fusion.3
  195.0 40.1 %all-reduce = (f32[16]{0:T(128)S(1)}, f32[16]{0:T(128)S(1)}, f32[7]{0:T(128)S(1)}) all-reduce(f32[16]{0:T(128)S(1)} %get-tuple-element.119, f32[16]{0:T(128)S(1)} %get-tuple-element.118, f32[7]{0:T(128)S(1)} %pad_maximum_fusion.3), channel_id=1, replica_groups=mesh['band'=4,'gvec'=2,'dom'=4] {'band','gvec','dom'}, use_global_device_ids=true, to_apply=%region_4.5 | all-reduce | flops 39 | bytes 312 | tf_op jit(solution)/shard_map/psum | solution.py:170
  235.1 0.6 select_reduce_fusion
  235.7 0.6 fusion.112
  236.3 1.3 fusion.45
  237.7 0.4 multiply_reduce_fusion.2
  238.2 1.0 gather_fusion.2
  239.3 0.9 multiply_bitcast_fusion
  240.8 6.6 %multiply_reduce_fusion = (f32[]{:T(128)}, bf16[1,64,128,128]{3,2,1,0:T(8,128)(2,1)}) fusion(f32[64,128,128]{2,1,0:T(8,128)} %get-tuple-element.117, bf16[1,64,128,128]{3,2,1,0:T(8,128)(2,1)S(1)} %copy-done.1, f32[]{:T(128)} %get-tuple-element.77, f32[128]{0:T(128)S(1)} %fusion.116, f32[64,128]{1,0:T(8,128)S(1)} %broadcast_add_fusion), kind=kLoop, calls=%fused_computation.28 | loop fusion | flops 14680063 | bytes 8421896 | tf_op jit(solution)/shard_map/reduce_sum | solution.py:176
  247.5 0.6 pad_maximum_fusion.4
  248.0 5.8 %psum.30 = f32[1]{0:T(128)} all-reduce(f32[1]{0:T(128)} %bitcast.32), channel_id=1, replica_groups=mesh['band'=4,'gvec'=2,'dom'=4] {'gvec'}, use_global_device_ids=true, to_apply=%region_9.10 | all-reduce | flops 1 | bytes 8 | tf_op jit(solution)/shard_map/psum | solution.py:176
  255.2 119.9 %reduce-scatter.5.cloned.1.call-done = f32[3,16]{0,1:T(8,128)} async-done(((f32[3,512]{0,1:T(8,128)}), f32[3,16]{0,1:T(8,128)}) %reduce-scatter.5.cloned.1.call-update) | async-done | bytes 208 | tf_op jit(solution)/shard_map/reduce_scatter | solution.py:144
  375.0 0.9 scatter_custom_fusion.1
  376.0 0.8 copy.91
  (57 shorter events, 2.5 us)
Async XLA Ops:
  7.2 2.5 copy-start
  7.2 78.7 %copy-start.2 = (f32[4]{0:T(128)S(1)}, f32[4]{0:T(128)}, u32[]{:S(2)}) copy-start(f32[4]{0:T(128)} %constant.183.clone) | copy-start | bytes 52
  7.2 117.9 %all-gather.3.cloned.1.call-start = ((), (), s32[]{:S(2)}) async-start(), calls=%async_computation.4 | async-start | bytes 2228224 | tf_op jit(solution)/shard_map/all_gather | solution.py:139
  8.6 78.5 %copy-start.1 = (bf16[1,64,128,128]{3,2,1,0:T(8,128)(2,1)S(1)}, bf16[1,64,128,128]{3,2,1,0:T(8,128)(2,1)}, u32[]{:S(2)}) copy-start(bf16[1,64,128,128]{3,2,1,0:T(8,128)(2,1)} %param.7) | copy-start | bytes 6291460
  94.3 24.7 %all-to-all-start = ((bf16[1,64,128,128]{3,1,0,2:T(8,128)(2,1)}), bf16[1,64,128,128]{3,1,0,2:T(8,128)(2,1)}, u32[]{:S(2)}, u32[]{:S(2)}) async-start(bf16[1,64,128,128]{3,1,0,2:T(8,128)(2,1)} %copy.80), calls=%async_computation | async-start | bytes 4194304 | tf_op jit(solution)/shard_map/all_to_all | solution.py:125
  99.2 93.5 %reduce-scatter.3.cloned.1.call-start = ((), (), s32[]{:S(2)}) async-start(), calls=%async_computation.5 | async-start | bytes 2228224 | tf_op jit(solution)/shard_map/reduce_scatter | solution.py:135
  138.4 30.5 %all-to-all-start.1 = ((bf16[1,128,64,128]{3,2,0,1:T(8,128)(2,1)}), bf16[1,128,64,128]{3,2,0,1:T(8,128)(2,1)}, u32[]{:S(2)}, u32[]{:S(2)}) async-start(bf16[1,128,64,128]{3,2,0,1:T(8,128)(2,1)} %copy.85), calls=%async_computation.1 | async-start | bytes 4194304 | tf_op jit(solution)/shard_map/all_to_all | solution.py:149
  143.3 231.7 %reduce-scatter.5.cloned.1.call-start = ((), (), s32[]{:S(2)}) async-start(), calls=%async_computation.6 | async-start | bytes 270336 | tf_op jit(solution)/shard_map/reduce_scatter | solution.py:144
Sparse Core Ops, SparseCore 0:
  87.1 37.9 all-gather.2
  132.1 60.4 reduce-scatter.2
  240.3 134.6 reduce-scatter.4
where the time goes:
time: 385 us; the launch traced here: 384 us
  waiting for transfers between devices  171 us (44%)
  blocking collectives  117 us (30%)
  other arithmetic  26.4 us (7%)
  local copies, waits for them, and re-layouts  22.8 us (6%)
  matrix products  19.1 us (5%)
  between operations  18.6 us (5%)
  starting transfers between devices  9.99 us (3%)
    reduce_scatter x1, waiting for transfers between devices, per_device(): lax.psum_scatter(padded, ('band', 'gvec', 'dom'), scatter_dimension=1, ti...  120 us
    all_gather x1, blocking collectives, per_device(): lax.all_gather(own_block, ('band', 'gvec', 'dom'), axis=1, tiled=True)  70.8 us
    psum x1, blocking collectives, per_device(): lax.psum((norm_vec, intersection_vec, local_totals), ('band', 'gvec', 'do...  40.1 us
    all_to_all x1, waiting for transfers between devices, per_device(): lax.all_to_all(back_one, 'gvec', split_axis=1, concat_axis=2, tiled=True)  25 us
    all_to_all x1, waiting for transfers between devices, per_device(): lax.all_to_all(sectioned, 'gvec', split_axis=2, concat_axis=1, tiled=True)  19 us
    dot_general x1, matrix products, per_device(): jnp.einsum('naqz,zl->naql', back_two, cosines, preferred_element_type=jnp...  7.92 us
  transfers between devices with their start and end apart: 5, of which 5 were waited for; matrix products, arithmetic and copies ran while one was open for 12% of the time, Pallas kernels for 0%

commit v1 on v0

v1 whole, which is shorter than its diff:
```python
import jax
import jax.numpy as jnp
from jax import lax
from jax.experimental import pallas as pl
from jax.experimental.pallas import tpu as pltpu
from jax.sharding import PartitionSpec as P
import functools

sigma_fractions = (1.0 / 32.0, 1.0 / 16.0, 1.0 / 8.0, 1.0 / 4.0)
kernel_weights = (1.0, 0.5, 0.25, 0.125)
force_unit = 1.0 / 4096.0
step_size = 0.5


def cosine_table(length):
    points = jnp.arange(length).astype(jnp.float32)
    angles = jnp.pi * (points[:, None] + 0.5) * points[None, :] / length
    scales = jnp.where(points == 0.0, jnp.sqrt(1.0 / length), jnp.sqrt(2.0 / length))
    return (jnp.cos(angles) * scales[None, :]).astype(jnp.bfloat16)


def occupancy(band_index, band_total):
    shifted = band_index.astype(jnp.float32) - 0.5 * band_total
    return 2.0 / (1.0 + jnp.exp(shifted / (0.125 * band_total)))


def kernels(points, centres, extent):
    values = []
    slopes = []
    for fraction in sigma_fractions:
        exponent = 0.5 / (extent * fraction) ** 2
        offset = points[:, None] - centres[None, :]
        gauss_value = jnp.exp(-exponent * offset * offset)
        values.append(gauss_value)
        slopes.append(2.0 * exponent * offset * gauss_value)
    return (jnp.concatenate(values, axis=1), jnp.concatenate(slopes, axis=1))


def stress_terms(weighted, x_wave, y_wave):
    over_z = jnp.sum(weighted, axis=2)
    over_y = jnp.sum(weighted, axis=1)
    over_x = jnp.sum(weighted, axis=0)
    stress_xx = jnp.sum(x_wave * x_wave * jnp.sum(over_z, axis=1))
    stress_yy = jnp.sum(y_wave * y_wave * jnp.sum(over_z, axis=0))
    stress_zz = jnp.sum(y_wave * y_wave * jnp.sum(over_y, axis=0))
    stress_xy = jnp.sum(x_wave[:, None] * y_wave[None, :] * over_z)
    stress_xz = jnp.sum(x_wave[:, None] * y_wave[None, :] * over_y)
    stress_yz = jnp.sum(y_wave[:, None] * y_wave[None, :] * over_x)
    return jnp.stack([stress_xx, stress_yy, stress_zz, stress_xy, stress_xz, stress_yz])


def peer_coords(index, sizes):
    _, gvec_size, dom_size = sizes
    return (index // (gvec_size * dom_size), (index // dom_size) % gvec_size, index % dom_size)


def gather_kernel(sizes, x_ref, out_ref, send_sem, recv_sem):
    total = sizes[0] * sizes[1] * sizes[2]
    me = (lax.axis_index("band") * sizes[1] + lax.axis_index("gvec")) * sizes[2] + lax.axis_index("dom")
    barrier = pltpu.get_barrier_semaphore()

    def greet(step, carry):
        peer = lax.rem(me + step, total)
        pl.semaphore_signal(
            barrier, inc=1, device_id=peer_coords(peer, sizes), device_id_type=pl.DeviceIdType.MESH
        )
        return carry

    def copy_of(step):
        peer = lax.rem(me + step, total)
        return pltpu.make_async_remote_copy(
            src_ref=x_ref,
            dst_ref=out_ref.at[me],
            send_sem=send_sem.at[step],
            recv_sem=recv_sem.at[step],
            device_id=peer_coords(peer, sizes),
            device_id_type=pl.DeviceIdType.MESH,
        )

    def send(step, carry):
        copy_of(step).start()
        return carry

    def finish(step, carry):
        copy_of(step).wait()
        return carry

    lax.fori_loop(1, total, greet, 0)
    out_ref[me] = x_ref[...]
    pl.semaphore_wait(barrier, total - 1)
    lax.fori_loop(1, total, send, 0)
    lax.fori_loop(1, total, finish, 0)


def gather_all(block, sizes, collective_id):
    total = sizes[0] * sizes[1] * sizes[2]
    return pl.pallas_call(
        functools.partial(gather_kernel, sizes),
        out_shape=jax.ShapeDtypeStruct((total,) + block.shape, block.dtype),
        in_specs=[pl.BlockSpec(memory_space=pltpu.VMEM)],
        out_specs=pl.BlockSpec(memory_space=pltpu.VMEM),
        scratch_shapes=[pltpu.SemaphoreType.DMA((total,)), pltpu.SemaphoreType.DMA((total,))],
        compiler_params=pltpu.CompilerParams(collective_id=collective_id, has_side_effects=True),
        name=f"gather_{collective_id}",
    )(block)


def pair_kernel(gvec_size, x_ref, out_ref, send_sem, recv_sem):
    me = lax.axis_index("gvec")
    barrier = pltpu.get_barrier_semaphore()
    others = [lax.rem(me + step, gvec_size) for step in range(1, gvec_size)]
    band, dom = lax.axis_index("band"), lax.axis_index("dom")
    for peer in others:
        pl.semaphore_signal(
            barrier, inc=1, device_id=(band, peer, dom), device_id_type=pl.DeviceIdType.MESH
        )
    out_ref[me] = x_ref[...]
    pl.semaphore_wait(barrier, gvec_size - 1)
    copies = []
    for step, peer in enumerate(others):
        copy = pltpu.make_async_remote_copy(
            src_ref=x_ref,
            dst_ref=out_ref.at[me],
            send_sem=send_sem.at[step],
            recv_sem=recv_sem.at[step],
            device_id=(band, peer, dom),
            device_id_type=pl.DeviceIdType.MESH,
        )
        copy.start()
        copies.append(copy)
    for copy in copies:
        copy.wait()


def gather_gvec(block, gvec_size, collective_id):
    return pl.pallas_call(
        functools.partial(pair_kernel, gvec_size),
        out_shape=jax.ShapeDtypeStruct((gvec_size,) + block.shape, block.dtype),
        in_specs=[pl.BlockSpec(memory_space=pltpu.VMEM)],
        out_specs=pl.BlockSpec(memory_space=pltpu.VMEM),
        scratch_shapes=[pltpu.SemaphoreType.DMA((gvec_size,)), pltpu.SemaphoreType.DMA((gvec_size,))],
        compiler_params=pltpu.CompilerParams(collective_id=collective_id, has_side_effects=True),
        name=f"gather_{collective_id}",
    )(block)


def potential_kernel(x_ref, y_ref, depth_ref, local_ref, out_ref):
    rows = x_ref.shape[0]
    for row in range(rows):
        plane = (x_ref[row : row + 1, :] * y_ref[...]).astype(jnp.bfloat16)
        value = lax.dot_general(
            plane, depth_ref[...], (((1,), (1,)), ((), ())), preferred_element_type=jnp.float32
        )
        rounded = value.astype(jnp.bfloat16).astype(jnp.float32)
        out_ref[row] = local_ref[row].astype(jnp.float32) + rounded


def slab_potential(x_value, y_value, depth, v_local):
    x_total, y_total, z_total = v_local.shape
    width = x_value.shape[1]
    rows = 8
    return pl.pallas_call(
        potential_kernel,
        grid=(x_total // rows,),
        out_shape=jax.ShapeDtypeStruct(v_local.shape, jnp.float32),
        in_specs=[
            pl.BlockSpec((rows, width), lambda i: (i, 0)),
            pl.BlockSpec((y_total, width), lambda i: (0, 0)),
            pl.BlockSpec((z_total, width), lambda i: (0, 0)),
            pl.BlockSpec((rows, y_total, z_total), lambda i: (i, 0, 0)),
        ],
        out_specs=pl.BlockSpec((rows, y_total, z_total), lambda i: (i, 0, 0)),
        cost_estimate=pl.CostEstimate(
            flops=2 * x_total * y_total * z_total * width,
            bytes_accessed=6 * x_total * y_total * z_total,
            transcendentals=0,
        ),
        name="slab_potential",
    )(x_value, y_value, depth, v_local)


def force_kernel(xv_ref, xs_ref, yv_ref, ys_ref, density_ref, out_ref):
    @pl.when(pl.program_id(0) == 0)
    def _():
        out_ref[...] = jnp.zeros_like(out_ref)

    rows, y_total, z_total = density_ref.shape
    width = yv_ref.shape[1]
    density = density_ref[...].astype(jnp.float32)
    density = (density * density).astype(jnp.bfloat16).reshape(rows * y_total, z_total)
    for part, (xr, yr) in enumerate(((xv_ref, yv_ref), (xs_ref, yv_ref), (xv_ref, ys_ref))):
        plane = jnp.concatenate(
            [(xr[row : row + 1, :] * yr[...]).astype(jnp.bfloat16) for row in range(rows)], axis=0
        )
        out_ref[part] += lax.dot_general(
            density, plane, (((0,), (0,)), ((), ())), preferred_element_type=jnp.float32
        )


def slab_moments(x_value, x_slope, y_value, y_slope, real_space):
    x_total, y_total, z_total = real_space.shape
    width = x_value.shape[1]
    rows = 8
    return pl.pallas_call(
        force_kernel,
        grid=(x_total // rows,),
        out_shape=jax.ShapeDtypeStruct((3, z_total, width), jnp.float32),
        in_specs=[
            pl.BlockSpec((rows, width), lambda i: (i, 0)),
            pl.BlockSpec((rows, width), lambda i: (i, 0)),
            pl.BlockSpec((y_total, width), lambda i: (0, 0)),
            pl.BlockSpec((y_total, width), lambda i: (0, 0)),
            pl.BlockSpec((rows, y_total, z_total), lambda i: (i, 0, 0)),
        ],
        out_specs=pl.BlockSpec((3, z_total, width), lambda i: (0, 0, 0)),
        cost_estimate=pl.CostEstimate(
            flops=6 * x_total * y_total * z_total * width,
            bytes_accessed=2 * x_total * y_total * z_total,
            transcendentals=0,
        ),
        name="slab_moments",
    )(x_value, x_slope, y_value, y_slope, real_space)


def per_device(sizes, coeffs, v_local, atom_pos, atom_charge, near_list, live_count):
    local_bands, x_local, extent, _ = coeffs.shape
    cosines = cosine_table(extent)
    gvec_id = lax.axis_index("gvec")
    group_id = lax.axis_index("band") * sizes[2] + lax.axis_index("dom")
    me = (lax.axis_index("band") * sizes[1] + gvec_id) * sizes[2] + lax.axis_index("dom")
    groups = sizes[0] * sizes[2]
    devices = groups * sizes[1]
    band_total = local_bands * groups
    cell_count = float(extent**3)
    band_ids = group_id * local_bands + jnp.arange(local_bands)
    weight = occupancy(band_ids, band_total)
    capacity = near_list.shape[0]
    live_mask = (jnp.arange(capacity) < live_count[0]).astype(jnp.float32)
    picked_pos = jnp.take(atom_pos, near_list, axis=1)
    picked_charge = jnp.take(atom_charge, near_list) * live_mask
    own_block = jnp.concatenate([picked_pos, picked_charge[None, :], live_mask[None, :]], axis=0)
    lanes = -(-capacity // 128) * 128
    tile = jnp.pad(own_block, ((0, 3), (0, lanes - capacity)))
    gathered = gather_all(tile, sizes, 0)
    all_blocks = gathered[:, :5, :capacity].transpose(1, 0, 2).reshape(5, devices * capacity)
    live_total = all_blocks.shape[1] // 4
    order = jnp.cumsum(all_blocks[4]) - 1.0
    target = jnp.where(all_blocks[4] > 0.5, order, float(live_total)).astype(jnp.int32)
    select = (target[:, None] == jnp.arange(live_total)[None, :]).astype(jnp.float32)
    charges = jnp.dot(all_blocks[:4], select, precision=lax.Precision.HIGHEST)

    y_share = v_local.shape[1]
    x_points = jnp.arange(extent).astype(jnp.float32)
    y_points = (gvec_id * y_share + jnp.arange(y_share)).astype(jnp.float32)
    x_value, x_slope = kernels(x_points, charges[0], extent)
    y_value, y_slope = kernels(y_points, charges[1], extent)
    z_value, z_slope = kernels(x_points, charges[2], extent)
    weights = jnp.array(kernel_weights, jnp.float32)
    scaled = (weights[:, None] * charges[3][None, :]).reshape(-1)
    depth = (scaled[None, :] * z_value).astype(jnp.bfloat16)
    field_total = slab_potential(x_value, y_value, depth, v_local)

    sectioned = jnp.einsum(
        "naql,zl->naqz", coeffs, cosines, preferred_element_type=jnp.float32
    ).astype(jnp.bfloat16)
    sectioned = jnp.einsum(
        "naqz,yq->nayz", sectioned, cosines, preferred_element_type=jnp.float32
    ).astype(jnp.bfloat16)
    exchanged = lax.all_to_all(sectioned, "gvec", split_axis=2, concat_axis=1, tiled=True)
    real_space = jnp.einsum(
        "nayz,xa->nxyz", exchanged, cosines, preferred_element_type=jnp.float32
    ).astype(jnp.bfloat16)
    applied = (field_total[None] * real_space.astype(jnp.float32)).astype(jnp.bfloat16)
    moments = 0.0
    for band in range(local_bands):
        moments = moments + weight[band] * slab_moments(
            x_value, x_slope, y_value, y_slope, real_space[band]
        )
    embedding = jnp.sum(moments[0] * depth.astype(jnp.float32)) / cell_count
    force_terms = jnp.stack(
        [
            jnp.sum(moments[1] * z_value, axis=0),
            jnp.sum(moments[2] * z_value, axis=0),
            jnp.sum(moments[0] * z_slope, axis=0),
        ]
    )
    force_terms = force_terms * scaled[None, :]
    forces = -force_unit * jnp.sum(force_terms.reshape(3, len(kernel_weights), -1), axis=1)

    back_one = jnp.einsum(
        "nxyz,xa->nayz", applied, cosines, preferred_element_type=jnp.float32
    ).astype(jnp.bfloat16)
    returned = lax.all_to_all(back_one, "gvec", split_axis=1, concat_axis=2, tiled=True)
    back_two = jnp.einsum(
        "nayz,yq->naqz", returned, cosines, preferred_element_type=jnp.float32
    ).astype(jnp.bfloat16)
    wave_field = jnp.einsum("naqz,zl->naql", back_two, cosines, preferred_element_type=jnp.float32)
    wave_step = jnp.pi / extent
    x_wave = (gvec_id * x_local + jnp.arange(x_local)).astype(jnp.float32) * wave_step
    y_wave = jnp.arange(extent).astype(jnp.float32) * wave_step
    kinetic = 0.5 * (
        x_wave[:, None, None] ** 2 + y_wave[None, :, None] ** 2 + y_wave[None, None, :] ** 2
    )
    coeff_wide = coeffs.astype(jnp.float32)
    image = kinetic[None] * coeff_wide + wave_field
    norm_part = jnp.sum(coeff_wide * coeff_wide, axis=(1, 2, 3))
    inner_part = jnp.sum(coeff_wide * image, axis=(1, 2, 3))
    pair_block = jnp.pad(
        jnp.stack([norm_part, inner_part]), ((0, 6), (0, -local_bands % 128))
    )
    pair = jnp.sum(gather_gvec(pair_block, sizes[1], 1), axis=0)
    norm_sq = pair[0, :local_bands]
    energies = pair[1, :local_bands] / norm_sq
    residual = image - energies[:, None, None, None] * coeff_wide
    resid_part = jnp.sum(residual * residual, axis=(1, 2, 3))
    waves_new = (coeff_wide - step_size * residual / (1.0 + kinetic[None])).astype(jnp.bfloat16)
    weighted = jnp.sum(weight[:, None, None, None] * coeff_wide * coeff_wide, axis=0)
    stress_local = stress_terms(weighted, x_wave, y_wave) / cell_count
    band_part = jnp.sum(weight * inner_part / norm_sq) / band_total
    local_totals = jnp.concatenate([stress_local, embedding[None], band_part[None]])
    mine = (jnp.arange(band_total)[None, :] == band_ids[:, None]).astype(jnp.float32)
    resid_vec = jnp.sum(mine * resid_part[:, None], axis=0)
    flat = jnp.concatenate([forces.reshape(-1), local_totals, resid_vec])
    flat = jnp.pad(flat, (0, -flat.shape[0] % 1024)).reshape(-1, 128)
    summed = jnp.sum(gather_all(flat, sizes, 2), axis=0).reshape(-1)
    force_all = summed[: 3 * live_total].reshape(3, live_total)
    totals = summed[3 * live_total : 3 * live_total + 8]
    resid_all = summed[3 * live_total + 8 : 3 * live_total + 8 + band_total]
    resid_ratio = jnp.sum(mine * resid_all[None, :], axis=1) / norm_sq
    start = lax.dynamic_slice(order, (me * capacity,), (capacity,))
    own_target = jnp.where(live_mask > 0.5, start, float(live_total)).astype(jnp.int32)
    slot_select = (own_target[None, :] == jnp.arange(live_total)[:, None]).astype(jnp.float32)
    slot_force = jnp.dot(force_all, slot_select, precision=lax.Precision.HIGHEST)
    atom_select = (near_list[:, None] == jnp.arange(atom_pos.shape[1])[None, :]).astype(jnp.float32)
    atom_force = jnp.dot(slot_force, atom_select, precision=lax.Precision.HIGHEST)
    return (waves_new, energies, resid_ratio, atom_force, totals)


def solution(mesh):
    sizes = (mesh.shape["band"], mesh.shape["gvec"], mesh.shape["dom"])
    return jax.shard_map(
        functools.partial(per_device, sizes),
        mesh=mesh,
        in_specs=(
            P(("band", "dom"), "gvec", None, None),
            P(None, "gvec", None),
            P(None, ("band", "gvec", "dom")),
            P(("band", "gvec", "dom")),
            P(("band", "gvec", "dom")),
            P(("band", "gvec", "dom")),
        ),
        out_specs=(
            P(("band", "dom"), "gvec", None, None),
            P(("band", "dom")),
            P(("band", "dom")),
            P(None, ("band", "gvec", "dom")),
            P(),
        ),
        check_vma=False,
    )
```

time: 385 us -> 172 us (0.45)
  waiting for transfers between devices: 171 us -> 24.4 us
  blocking collectives: 117 us -> 0 us
  Pallas kernels: 0 us -> 68.6 us
  between operations: 18.6 us -> 8.65 us
  matrix products: 19.1 us -> 13.6 us
    reduce_scatter x2 -> x0, waiting for transfers between devices: 125 us -> none  [the longest x1 120 us: per_device(): lax.psum_scatter(padded, ('band', 'gvec', 'dom'), scatter_dimension=1, ti...]
    all_gather x1 -> x0, blocking collectives: 70.8 us -> none  [per_device(): lax.all_gather(own_block, ('band', 'gvec', 'dom'), axis=1, tiled=True)]
    pallas_call x0 -> x5, Pallas kernels: none -> 68.6 us  [the longest x2 37.6 us: gather_all(): pl.pallas_call(functools.partial(gather_kernel, sizes), out_shape=jax.Sha...]
    psum x2 -> x0, blocking collectives: 45.9 us -> none  [the longest x1 40.1 us: per_device(): lax.psum((norm_vec, intersection_vec, local_totals), ('band', 'gvec', 'do...]
    all_to_all x1, waiting for transfers between devices: 19 us -> 0.01 us  [per_device(): lax.all_to_all(sectioned, 'gvec', split_axis=2, concat_axis=1, tiled=True)]
    reduce_sum x7 -> x6, other arithmetic: 9.87 us -> 10.9 us  [the longest x1 7.15 us: per_device(): resid_part = jnp.sum(residual * residual, axis=(1, 2, 3))]
  transfers between devices with their start and end apart: 5 -> 2, of which waited for: 5 -> 1; matrix products, arithmetic and copies ran while one was open for 12% -> 4% of each run, Pallas kernels for 0% -> 15%
where the time goes in v1:
time: 172 us; the launch traced here: 171 us
  Pallas kernels  68.6 us (40%)
  other arithmetic  25.6 us (15%)
  waiting for transfers between devices  24.4 us (14%)
  local copies, waits for them, and re-layouts  21.4 us (12%)
  matrix products  13.6 us (8%)
  between operations  8.65 us (5%)
  starting transfers between devices  8.38 us (5%)
    pallas_call x2, Pallas kernels, gather_all(): pl.pallas_call(functools.partial(gather_kernel, sizes), out_shape=jax.Sha...  37.6 us
    all_to_all x1, waiting for transfers between devices, per_device(): lax.all_to_all(back_one, 'gvec', split_axis=1, concat_axis=2, tiled=True)  24.4 us
    pallas_call x1, Pallas kernels, slab_potential(): pl.pallas_call(potential_kernel, grid=(x_total // rows,), out_shape=jax.S...  13.5 us
    pallas_call x1, Pallas kernels, slab_moments(): pl.pallas_call(force_kernel, grid=(x_total // rows,), out_shape=jax.Shape...  12.5 us
    reduce_sum x1, other arithmetic, per_device(): resid_part = jnp.sum(residual * residual, axis=(1, 2, 3))  7.15 us
    dot_general x1, matrix products, per_device(): jnp.einsum('naqz,zl->naql', back_two, cosines, preferred_element_type=jnp...  6.08 us
    pallas_call x1, Pallas kernels, gather_gvec(): pl.pallas_call(functools.partial(pair_kernel, gvec_size), out_shape=jax.S...  4.92 us
    all_to_all x1, starting transfers between devices, per_device(): lax.all_to_all(sectioned, 'gvec', split_axis=2, concat_axis=1, tiled=True)  4.39 us
  transfers between devices with their start and end apart: 2, of which 1 were waited for; matrix products, arithmetic and copies ran while one was open for 4% of the time, Pallas kernels for 15%

profile of v1, /device:TPU:0, one launch (start us, length us, event | category | flops | bytes accessed | tf_op | source)
XLA Modules:
  0.0 170.5 jit_solution(13923949420967247830)
XLA Ops:
  0.7 3.2 %convert_bitcast_fusion.1 = bf16[1,64,128,128]{3,2,1,0:T(8,128)(2,1)S(1)} fusion(bf16[1,64,128,128]{3,2,1,0:T(8,128)(2,1)} %param.7, f32[128]{0:T(128)S(1)} %compare_select_fusion.2, f32[128]{0:T(128)S(1)} %iota_convert_fusion, f32[128]{0:T(128)S(1)} %add_multiply_fusion.1), kind=kOutput, calls=%fused_computation.35 | convolution fusion | flops 539099136 | bytes 4195840 | tf_op jit(solution)/shard_map/naqz,yq->nayz/dot_general | solution.py:266
  3.9 2.7 %copy.45 = bf16[1,64,128,128]{3,1,0,2:T(8,128)(2,1)} copy(bf16[1,64,128,128]{3,2,1,0:T(8,128)(2,1)S(1)} %convert_bitcast_fusion.1) | data formatting | bytes 4194304 | tf_op jit(solution)/shard_map/convert_element_type | solution.py:268
  6.6 4.4 %all-to-all-start = ((bf16[1,64,128,128]{3,1,0,2:T(8,128)(2,1)}), bf16[1,64,128,128]{3,1,0,2:T(8,128)(2,1)S(1)}, u32[]{:S(2)}, u32[]{:S(2)}) async-start(bf16[1,64,128,128]{3,1,0,2:T(8,128)(2,1)} %copy.45), calls=%async_computation | async-start | bytes 4194304 | tf_op jit(solution)/shard_map/all_to_all | solution.py:269
  11.7 0.2 copy.41
  11.9 0.6 gather_fusion.1
  12.6 0.6 gather_fusion
  13.2 0.6 select_maximum_fusion.1.x_ref
  13.8 25.8 %gather_0.1 = f32[32,8,128]{2,1,0:T(8,128)} custom-call(f32[8,128]{1,0:T(8,128)} %select_maximum_fusion.1.x_ref), custom_call_target="tpu_custom_call" | custom-call | tf_op jit(solution)/shard_map/gather_0/pallas_call | solution.py:97
  39.6 0.9 slice_bitcast_fusion.3
  40.8 0.3 reduce-window.9
  41.6 0.3 fusion.38
  42.1 0.7 pad_maximum_fusion.4.ys_ref
  42.8 0.7 pad_maximum_fusion.3.y_ref.yv_ref
  43.4 0.2 fusion.48
  43.6 0.7 pad_maximum_fusion.2.xs_ref
  44.4 0.7 pad_maximum_fusion.x_ref.xv_ref
  45.1 0.2 copy.46
  45.3 1.0 fusion.73
  46.3 2.7 %copy.63.density_ref = bf16[128,64,128]{2,1,0:T(8,128)(2,1)} copy(bf16[128,64,128]{2,0,1:T(8,128)(2,1)S(1)} %fusion.73) | data formatting | bytes 4194304 | tf_op jit(solution)/shard_map/nayz,xa->nxyz/dot_general | solution.py:270
  49.0 12.5 %slab_moments.1 = f32[3,128,512]{2,1,0:T(8,128)} custom-call(f32[128,512]{1,0:T(8,128)} %pad_maximum_fusion.x_ref.xv_ref, f32[128,512]{1,0:T(8,128)} %pad_maximum_fusion.2.xs_ref, f32[64,512]{1,0:T(8,128)} %pad_maximum_fusion.3.y_ref.yv_ref, f32[64,512]{1,0:T(8,128)} %pad_maximum_fusion.4.ys_ref, bf16[128,64,128]{2,1,0:T(8,128)(2,1)} %copy.63.density_ref), custom_call_target="tpu_custom_call" | custom-call | flops 3221225472 | bytes 2097152 | tf_op jit(solution)/shard_map/slab_moments/pallas_call | solution.py:204
  61.5 1.2 broadcast_multiply_fusion
  62.7 1.4 multiply_reduce_fusion.1
  64.1 13.5 %slab_potential.1 = f32[128,64,128]{2,1,0:T(8,128)} custom-call(f32[128,512]{1,0:T(8,128)} %pad_maximum_fusion.x_ref.xv_ref, f32[64,512]{1,0:T(8,128)} %pad_maximum_fusion.3.y_ref.yv_ref, bf16[128,512]{1,0:T(8,128)(2,1)} %get-tuple-element.22.depth_ref, bf16[128,64,128]{2,1,0:T(8,128)(2,1)} %local_ref.1), custom_call_target="tpu_custom_call" | custom-call | flops 1073741824 | bytes 6291456 | tf_op jit(solution)/shard_map/slab_potential/pallas_call | solution.py:162
  77.6 3.8 %multiply_convert_fusion = bf16[128,64,128]{2,1,0:T(8,128)(2,1)S(1)} fusion(f32[128,64,128]{2,1,0:T(8,128)} %slab_potential.1, bf16[128,64,128]{2,0,1:T(8,128)(2,1)S(1)} %fusion.73), kind=kLoop, calls=%fused_computation.22 | loop fusion | flops 3145728 | bytes 8388608 | tf_op jit(solution)/shard_map/convert_element_type | solution.py:273
  81.4 2.0 %convert_bitcast_fusion = bf16[1,128,64,128]{3,1,2,0:T(8,128)(2,1)S(1)} fusion(bf16[128,64,128]{2,1,0:T(8,128)(2,1)S(1)} %multiply_convert_fusion, f32[128]{0:T(128)S(1)} %compare_select_fusion.2, f32[128]{0:T(128)S(1)} %iota_convert_fusion, f32[128]{0:T(128)S(1)} %add_multiply_fusion.1), kind=kOutput, calls=%fused_computation.34 | convolution fusion | flops 269549568 | bytes 4195840 | tf_op jit(solution)/shard_map/nxyz,xa->nayz/dot_general | solution.py:290
  83.4 2.7 %copy.50 = bf16[1,128,64,128]{3,2,0,1:T(8,128)(2,1)} copy(bf16[1,128,64,128]{3,1,2,0:T(8,128)(2,1)S(1)} %convert_bitcast_fusion) | data formatting | bytes 4194304 | tf_op jit(solution)/shard_map/convert_element_type | solution.py:292
  86.1 4.0 %all-to-all-start.1 = ((bf16[1,128,64,128]{3,2,0,1:T(8,128)(2,1)}), bf16[1,128,64,128]{3,2,0,1:T(8,128)(2,1)S(1)}, u32[]{:S(2)}, u32[]{:S(2)}) async-start(bf16[1,128,64,128]{3,2,0,1:T(8,128)(2,1)} %copy.50), calls=%async_computation.1 | async-start | bytes 4194304 | tf_op jit(solution)/shard_map/all_to_all | solution.py:293
  91.0 24.4 %all-to-all-done.1 = bf16[1,128,64,128]{3,2,0,1:T(8,128)(2,1)S(1)} async-done(((bf16[1,128,64,128]{3,2,0,1:T(8,128)(2,1)}), bf16[1,128,64,128]{3,2,0,1:T(8,128)(2,1)S(1)}, u32[]{:S(2)}, u32[]{:S(2)}) %all-to-all-start.1) | async-done | bytes 2097184 | tf_op jit(solution)/shard_map/all_to_all | solution.py:293
  115.4 1.3 copy-done.2
  116.7 3.3 %copy.51 = bf16[1,2,64,64,128]{4,3,1,2,0:T(8,128)(2,1)} copy(bf16[1,2,64,64,128]{4,3,2,1,0:T(8,128)(2,1)} %bitcast.130) | data formatting | bytes 4194304 | tf_op jit(solution)/shard_map/all_to_all | solution.py:293
  120.0 6.1 %fusion.7 = (f32[]{:T(128)}, f32[]{:T(128)}, f32[64,128,128]{2,1,0:T(8,128)}) fusion(bf16[1,64,128,128]{3,2,1,0:T(8,128)(2,1)S(1)} %copy-done.1, f32[128]{0:T(128)S(1)} %fusion.96, f32[64,128]{1,0:T(8,128)S(1)} %broadcast_add_fusion, f32[128]{0:T(128)S(1)} %compare_select_fusion.2, f32[128]{0:T(128)S(1)} %iota_convert_fusion, ...), kind=kOutput, calls=%fused_computation.16 | convolution fusion | flops 547487744 | bytes 8423432 | tf_op jit(solution)/shard_map/naqz,zl->naql/dot_general | solution.py:297
  126.7 1.9 %select_maximum_fusion.x_ref = f32[8,128]{1,0:T(8,128)} fusion(f32[1,1]{1,0:T(1,128)} %bitcast.29, f32[1,1]{1,0:T(1,128)} %bitcast.28), kind=kLoop, calls=%fused_computation.145 | loop fusion | flops 8192 | bytes 4104 | tf_op jit(solution)/shard_map/stack | solution.py:309
  128.6 4.9 %gather_1.1 = f32[2,8,128]{2,1,0:T(8,128)} custom-call(f32[8,128]{1,0:T(8,128)} %select_maximum_fusion.x_ref), custom_call_target="tpu_custom_call" | custom-call | tf_op jit(solution)/shard_map/gather_1/pallas_call | solution.py:136
  133.6 0.7 reduce_sum.225
  134.3 0.5 fusion.104
  136.8 7.2 %multiply_reduce_fusion = (f32[]{:T(128)}, f32[128]{0:T(128)S(1)}, f32[64,128]{1,0:T(8,128)S(1)}, f32[64,128]{1,0:T(8,128)S(1)}, f32[128,128]{1,0:T(8,128)S(1)},...) fusion(f32[64,128,128]{2,1,0:T(8,128)} %get-tuple-element.68, ...), kind=kLoop, calls=%fused_computation.21 | loop fusion | flops 23035584 | bytes 8554252 | tf_op jit(solution)/shard_map/reduce_sum | solution.py:315
  144.0 0.6 multiply_reduce_fusion.5
  144.6 0.7 multiply_reduce_fusion.3
  145.2 0.7 multiply_reduce_fusion.2
  146.0 0.7 fusion.59
  146.7 3.8 %stack.55 = f32[6]{0:T(128)S(1)} concatenate(f32[1]{0:T(128)} %bitcast.40, f32[1]{0:T(128)} %bitcast.41, f32[1]{0:T(128)} %bitcast.42, f32[1]{0:T(128)} %bitcast.43, f32[1]{0:T(128)} %bitcast.44, f32[1]{0:T(128)} %bitcast.45), dimensions={0} | concatenate | bytes 48 | tf_op jit(solution)/shard_map/stack | solution.py:49
  150.6 0.6 compare_select_fusion.4
  151.3 0.6 pad_bitcast_fusion.x_ref
  151.9 11.8 %gather_2.1 = f32[32,8,128]{2,1,0:T(8,128)} custom-call(f32[8,128]{1,0:T(8,128)} %pad_bitcast_fusion.x_ref), custom_call_target="tpu_custom_call" | custom-call | tf_op jit(solution)/shard_map/gather_2/pallas_call | solution.py:97
  163.7 0.9 reduce_sum.245
  164.7 0.8 fusion.93
  165.4 0.5 slice.76
  166.1 0.8 fusion.56
  (46 shorter events, 1.4 us)
Async XLA Ops:
  0.6 11.3 %copy-start = (f32[1024]{0:T(1024)S(1)}, f32[1024]{0:T(1024)}, u32[]{:S(2)}) copy-start(f32[1024]{0:T(1024)} %param.10) | copy-start | bytes 12292
  6.6 5.0 %copy-start.4 = (s32[16]{0:T(128)S(1)}, s32[16]{0:T(128)}, u32[]{:S(2)}) copy-start(s32[16]{0:T(128)} %param.11) | copy-start | bytes 196
  6.6 5.1 %copy-start.3 = (f32[3,1024]{1,0:T(4,128)S(1)}, f32[3,1024]{1,0:T(4,128)}, u32[]{:S(2)}) copy-start(f32[3,1024]{1,0:T(4,128)} %param.9) | copy-start | bytes 36868
  6.6 38.5 %all-to-all-start = ((bf16[1,64,128,128]{3,1,0,2:T(8,128)(2,1)}), bf16[1,64,128,128]{3,1,0,2:T(8,128)(2,1)S(1)}, u32[]{:S(2)}, u32[]{:S(2)}) async-start(bf16[1,64,128,128]{3,1,0,2:T(8,128)(2,1)} %copy.45), calls=%async_computation | async-start | bytes 4194304 | tf_op jit(solution)/shard_map/all_to_all | solution.py:269
  12.6 32.5 %copy-start.5 = (f32[4]{0:T(128)S(1)}, f32[4]{0:T(128)}, u32[]{:S(2)}) copy-start(f32[4]{0:T(128)} %constant.133.clone) | copy-start | bytes 52
  86.1 29.3 %all-to-all-start.1 = ((bf16[1,128,64,128]{3,2,0,1:T(8,128)(2,1)}), bf16[1,128,64,128]{3,2,0,1:T(8,128)(2,1)S(1)}, u32[]{:S(2)}, u32[]{:S(2)}) async-start(bf16[1,128,64,128]{3,2,0,1:T(8,128)(2,1)} %copy.50), calls=%async_computation.1 | async-start | bytes 4194304 | tf_op jit(solution)/shard_map/all_to_all | solution.py:293
  115.4 1.3 copy-start.2
  116.7 3.3 %copy-start.1 = (bf16[1,64,128,128]{3,2,1,0:T(8,128)(2,1)S(1)}, bf16[1,64,128,128]{3,2,1,0:T(8,128)(2,1)}, u32[]{:S(2)}) copy-start(bf16[1,64,128,128]{3,2,1,0:T(8,128)(2,1)} %param.7) | copy-start | bytes 6291460

commit v2 on v1

--- a/solution.py
+++ b/solution.py
@@ -105,60 +105,30 @@
     )(block)
 
 
-def pair_kernel(gvec_size, x_ref, out_ref, send_sem, recv_sem):
-    me = lax.axis_index("gvec")
-    barrier = pltpu.get_barrier_semaphore()
-    others = [lax.rem(me + step, gvec_size) for step in range(1, gvec_size)]
-    band, dom = lax.axis_index("band"), lax.axis_index("dom")
-    for peer in others:
-        pl.semaphore_signal(
-            barrier, inc=1, device_id=(band, peer, dom), device_id_type=pl.DeviceIdType.MESH
-        )
-    out_ref[me] = x_ref[...]
-    pl.semaphore_wait(barrier, gvec_size - 1)
-    copies = []
-    for step, peer in enumerate(others):
-        copy = pltpu.make_async_remote_copy(
-            src_ref=x_ref,
-            dst_ref=out_ref.at[me],
-            send_sem=send_sem.at[step],
-            recv_sem=recv_sem.at[step],
-            device_id=(band, peer, dom),
-            device_id_type=pl.DeviceIdType.MESH,
-        )
-        copy.start()
-        copies.append(copy)
-    for copy in copies:
-        copy.wait()
-
-
-def gather_gvec(block, gvec_size, collective_id):
-    return pl.pallas_call(
-        functools.partial(pair_kernel, gvec_size),
-        out_shape=jax.ShapeDtypeStruct((gvec_size,) + block.shape, block.dtype),
-        in_specs=[pl.BlockSpec(memory_space=pltpu.VMEM)],
-        out_specs=pl.BlockSpec(memory_space=pltpu.VMEM),
-        scratch_shapes=[pltpu.SemaphoreType.DMA((gvec_size,)), pltpu.SemaphoreType.DMA((gvec_size,))],
-        compiler_params=pltpu.CompilerParams(collective_id=collective_id, has_side_effects=True),
-        name=f"gather_{collective_id}",
-    )(block)
+def plane_rows(x_ref, y_ref):
+    rows, width = x_ref.shape
+    y_total = y_ref.shape[0]
+    parts = []
+    for row in range(rows):
+        parts.append((x_ref[row : row + 1, :] * y_ref[...]).astype(jnp.bfloat16))
+    return jnp.concatenate(parts, axis=0)
 
 
 def potential_kernel(x_ref, y_ref, depth_ref, local_ref, out_ref):
-    rows = x_ref.shape[0]
-    for row in range(rows):
-        plane = (x_ref[row : row + 1, :] * y_ref[...]).astype(jnp.bfloat16)
-        value = lax.dot_general(
-            plane, depth_ref[...], (((1,), (1,)), ((), ())), preferred_element_type=jnp.float32
-        )
-        rounded = value.astype(jnp.bfloat16).astype(jnp.float32)
-        out_ref[row] = local_ref[row].astype(jnp.float32) + rounded
+    value = lax.dot_general(
+        plane_rows(x_ref, y_ref),
+        depth_ref[...],
+        (((1,), (1,)), ((), ())),
+        preferred_element_type=jnp.float32,
+    )
+    rounded = value.astype(jnp.bfloat16).astype(jnp.float32).reshape(out_ref.shape)
+    out_ref[...] = local_ref[...].astype(jnp.float32) + rounded
 
 
 def slab_potential(x_value, y_value, depth, v_local):
     x_total, y_total, z_total = v_local.shape
     width = x_value.shape[1]
-    rows = 8
+    rows = 16
     return pl.pallas_call(
         potential_kernel,
         grid=(x_total // rows,),
@@ -171,7 +141,7 @@
         ],
         out_specs=pl.BlockSpec((rows, y_total, z_total), lambda i: (i, 0, 0)),
         cost_estimate=pl.CostEstimate(
-            flops=2 * x_total * y_total * z_total * width,
+            flops=8 * x_total * y_total * z_total * width,
             bytes_accessed=6 * x_total * y_total * z_total,
             transcendentals=0,
         ),
@@ -179,28 +149,27 @@
     )(x_value, y_value, depth, v_local)
 
 
-def force_kernel(xv_ref, xs_ref, yv_ref, ys_ref, density_ref, out_ref):
+def force_kernel(xv_ref, xs_ref, yv_ref, ys_ref, real_ref, out_ref):
     @pl.when(pl.program_id(0) == 0)
     def _():
         out_ref[...] = jnp.zeros_like(out_ref)
 
-    rows, y_total, z_total = density_ref.shape
-    width = yv_ref.shape[1]
-    density = density_ref[...].astype(jnp.float32)
+    rows, y_total, z_total = real_ref.shape
+    density = real_ref[...].astype(jnp.float32)
     density = (density * density).astype(jnp.bfloat16).reshape(rows * y_total, z_total)
     for part, (xr, yr) in enumerate(((xv_ref, yv_ref), (xs_ref, yv_ref), (xv_ref, ys_ref))):
-        plane = jnp.concatenate(
-            [(xr[row : row + 1, :] * yr[...]).astype(jnp.bfloat16) for row in range(rows)], axis=0
-        )
         out_ref[part] += lax.dot_general(
-            density, plane, (((0,), (0,)), ((), ())), preferred_element_type=jnp.float32
+            density,
+            plane_rows(xr, yr),
+            (((0,), (0,)), ((), ())),
+            preferred_element_type=jnp.float32,
         )
 
 
 def slab_moments(x_value, x_slope, y_value, y_slope, real_space):
     x_total, y_total, z_total = real_space.shape
     width = x_value.shape[1]
-    rows = 8
+    rows = 16
     return pl.pallas_call(
         force_kernel,
         grid=(x_total // rows,),
@@ -214,7 +183,7 @@
         ],
         out_specs=pl.BlockSpec((3, z_total, width), lambda i: (0, 0, 0)),
         cost_estimate=pl.CostEstimate(
-            flops=6 * x_total * y_total * z_total * width,
+            flops=12 * x_total * y_total * z_total * width,
             bytes_accessed=2 * x_total * y_total * z_total,
             transcendentals=0,
         ),
@@ -242,6 +211,7 @@
     lanes = -(-capacity // 128) * 128
     tile = jnp.pad(own_block, ((0, 3), (0, lanes - capacity)))
     gathered = gather_all(tile, sizes, 0)
+    coeffs, gathered = lax.optimization_barrier((coeffs, gathered))
     all_blocks = gathered[:, :5, :capacity].transpose(1, 0, 2).reshape(5, devices * capacity)
     live_total = all_blocks.shape[1] // 4
     order = jnp.cumsum(all_blocks[4]) - 1.0
@@ -260,22 +230,73 @@
     depth = (scaled[None, :] * z_value).astype(jnp.bfloat16)
     field_total = slab_potential(x_value, y_value, depth, v_local)
 
-    sectioned = jnp.einsum(
+    gvec_size = sizes[1]
+    chunks = 2 if y_share % 32 == 0 else 1
+    chunk = y_share // chunks
+
+    def y_rows(step, part):
+        owner = lax.rem(gvec_id + step + gvec_size, gvec_size)
+        return lax.dynamic_slice_in_dim(cosines, owner * y_share + part * chunk, chunk, 0)
+
+    def a_columns(step):
+        owner = lax.rem(gvec_id + step, gvec_size)
+        return lax.dynamic_slice_in_dim(cosines, owner * x_local, x_local, 1)
+
+    def shift(value, step):
+        return lax.ppermute(
+            value, "gvec", [(at, (at + step) % gvec_size) for at in range(gvec_size)]
+        )
+
+    section_z = jnp.einsum(
         "naql,zl->naqz", coeffs, cosines, preferred_element_type=jnp.float32
     ).astype(jnp.bfloat16)
-    sectioned = jnp.einsum(
-        "naqz,yq->nayz", sectioned, cosines, preferred_element_type=jnp.float32
-    ).astype(jnp.bfloat16)
-    exchanged = lax.all_to_all(sectioned, "gvec", split_axis=2, concat_axis=1, tiled=True)
-    real_space = jnp.einsum(
-        "nayz,xa->nxyz", exchanged, cosines, preferred_element_type=jnp.float32
-    ).astype(jnp.bfloat16)
-    applied = (field_total[None] * real_space.astype(jnp.float32)).astype(jnp.bfloat16)
+
+    def section_y(step, part):
+        return jnp.einsum(
+            "naqz,yq->nayz", section_z, y_rows(step, part), preferred_element_type=jnp.float32
+        ).astype(jnp.bfloat16)
+
+    arrived = [
+        [shift(section_y(-step, part), -step) for step in range(1, gvec_size)]
+        for part in range(chunks)
+    ]
+    coeff_wide = coeffs.astype(jnp.float32)
+    wave_step = jnp.pi / extent
+    x_wave = (gvec_id * x_local + jnp.arange(x_local)).astype(jnp.float32) * wave_step
+    y_wave = jnp.arange(extent).astype(jnp.float32) * wave_step
+    kinetic = 0.5 * (
+        x_wave[:, None, None] ** 2 + y_wave[None, :, None] ** 2 + y_wave[None, None, :] ** 2
+    )
+    norm_part = jnp.sum(coeff_wide * coeff_wide, axis=(1, 2, 3))
+    weighted = jnp.sum(weight[:, None, None, None] * coeff_wide * coeff_wide, axis=0)
+    stress_local = stress_terms(weighted, x_wave, y_wave) / cell_count
+
     moments = 0.0
-    for band in range(local_bands):
-        moments = moments + weight[band] * slab_moments(
-            x_value, x_slope, y_value, y_slope, real_space[band]
-        )
+    returned = []
+    own_sections = [section_y(0, part) for part in range(chunks)]
+    for part in range(chunks):
+        window = slice(part * chunk, (part + 1) * chunk)
+        held = [own_sections[part]] + arrived[part]
+        real_space = sum(
+            jnp.einsum("nayz,xa->nxyz", block, a_columns(step), preferred_element_type=jnp.float32)
+            for step, block in enumerate(held)
+        ).astype(jnp.bfloat16)
+        applied = (field_total[None, :, window] * real_space.astype(jnp.float32)).astype(jnp.bfloat16)
+
+        def back_x(step):
+            return jnp.einsum(
+                "nxyz,xa->nayz", applied, a_columns(step), preferred_element_type=jnp.float32
+            ).astype(jnp.bfloat16)
+
+        if part == chunks - 1:
+            applied, stress_local, norm_part = lax.optimization_barrier(
+                (applied, stress_local, norm_part)
+            )
+        returned.append([shift(back_x(step), step) for step in range(1, gvec_size)] + [back_x(0)])
+        for band in range(local_bands):
+            moments = moments + weight[band] * slab_moments(
+                x_value, x_slope, y_value[window], y_slope[window], real_space[band]
+            )
     embedding = jnp.sum(moments[0] * depth.astype(jnp.float32)) / cell_count
     force_terms = jnp.stack(
         [
@@ -287,46 +308,44 @@
     force_terms = force_terms * scaled[None, :]
     forces = -force_unit * jnp.sum(force_terms.reshape(3, len(kernel_weights), -1), axis=1)
 
-    back_one = jnp.einsum(
-        "nxyz,xa->nayz", applied, cosines, preferred_element_type=jnp.float32
-    ).astype(jnp.bfloat16)
-    returned = lax.all_to_all(back_one, "gvec", split_axis=1, concat_axis=2, tiled=True)
-    back_two = jnp.einsum(
-        "nayz,yq->naqz", returned, cosines, preferred_element_type=jnp.float32
+    steps = list(range(-1, -gvec_size, -1)) + [0]
+    back_two = sum(
+        jnp.einsum("nayz,yq->naqz", block, y_rows(step, part), preferred_element_type=jnp.float32)
+        for part in range(chunks)
+        for step, block in zip(steps, returned[part])
     ).astype(jnp.bfloat16)
     wave_field = jnp.einsum("naqz,zl->naql", back_two, cosines, preferred_element_type=jnp.float32)
-    wave_step = jnp.pi / extent
-    x_wave = (gvec_id * x_local + jnp.arange(x_local)).astype(jnp.float32) * wave_step
-    y_wave = jnp.arange(extent).astype(jnp.float32) * wave_step
-    kinetic = 0.5 * (
-        x_wave[:, None, None] ** 2 + y_wave[None, :, None] ** 2 + y_wave[None, None, :] ** 2
-    )
-    coeff_wide = coeffs.astype(jnp.float32)
     image = kinetic[None] * coeff_wide + wave_field
-    norm_part = jnp.sum(coeff_wide * coeff_wide, axis=(1, 2, 3))
     inner_part = jnp.sum(coeff_wide * image, axis=(1, 2, 3))
-    pair_block = jnp.pad(
-        jnp.stack([norm_part, inner_part]), ((0, 6), (0, -local_bands % 128))
-    )
-    pair = jnp.sum(gather_gvec(pair_block, sizes[1], 1), axis=0)
-    norm_sq = pair[0, :local_bands]
-    energies = pair[1, :local_bands] / norm_sq
+    own_energy = jnp.where(norm_part > 0.0, inner_part / jnp.where(norm_part > 0.0, norm_part, 1.0), 0.0)
+    own_residual = image - own_energy[:, None, None, None] * coeff_wide
+    resid_part = jnp.sum(own_residual * own_residual, axis=(1, 2, 3))
+    local_totals = jnp.concatenate([stress_local, embedding[None]])
+    mine = (jnp.arange(band_total)[None, :] == band_ids[:, None]).astype(jnp.float32)
+    band_rows = jnp.stack([norm_part, inner_part, resid_part])
+    flat = jnp.concatenate([forces.reshape(-1), local_totals])
+    flat = jnp.pad(flat, (0, -flat.shape[0] % 128)).reshape(-1, 128)
+    bands = jnp.pad(band_rows, ((0, -(flat.shape[0] + 3) % 8), (0, 128 - local_bands)))
+    parts = gather_all(jnp.concatenate([flat, bands]), sizes, 1)
+    lines = flat.shape[0]
+    summed = jnp.sum(parts[:, :lines], axis=0).reshape(-1)
+    force_all = summed[: 3 * live_total].reshape(3, live_total)
+    by_group = parts[:, lines : lines + 3, :local_bands].reshape(
+        sizes[0], gvec_size, sizes[2], 3, local_bands
+    )
+    norms, inners, squares = by_group[:, :, :, 0], by_group[:, :, :, 1], by_group[:, :, :, 2]
+    norm_all = jnp.sum(norms, axis=1)
+    energy_all = jnp.sum(inners, axis=1) / norm_all
+    own_all = jnp.where(norms > 0.0, inners / jnp.where(norms > 0.0, norms, 1.0), 0.0)
+    shifted = energy_all[:, None] - own_all
+    ratio_all = (jnp.sum(squares + shifted * shifted * norms, axis=1) / norm_all).reshape(-1)
+    energy_all = energy_all.reshape(-1)
+    energies = jnp.sum(mine * energy_all[None, :], axis=1)
+    resid_ratio = jnp.sum(mine * ratio_all[None, :], axis=1)
     residual = image - energies[:, None, None, None] * coeff_wide
-    resid_part = jnp.sum(residual * residual, axis=(1, 2, 3))
     waves_new = (coeff_wide - step_size * residual / (1.0 + kinetic[None])).astype(jnp.bfloat16)
-    weighted = jnp.sum(weight[:, None, None, None] * coeff_wide * coeff_wide, axis=0)
-    stress_local = stress_terms(weighted, x_wave, y_wave) / cell_count
-    band_part = jnp.sum(weight * inner_part / norm_sq) / band_total
-    local_totals = jnp.concatenate([stress_local, embedding[None], band_part[None]])
-    mine = (jnp.arange(band_total)[None, :] == band_ids[:, None]).astype(jnp.float32)
-    resid_vec = jnp.sum(mine * resid_part[:, None], axis=0)
-    flat = jnp.concatenate([forces.reshape(-1), local_totals, resid_vec])
-    flat = jnp.pad(flat, (0, -flat.shape[0] % 1024)).reshape(-1, 128)
-    summed = jnp.sum(gather_all(flat, sizes, 2), axis=0).reshape(-1)
-    force_all = summed[: 3 * live_total].reshape(3, live_total)
-    totals = summed[3 * live_total : 3 * live_total + 8]
-    resid_all = summed[3 * live_total + 8 : 3 * live_total + 8 + band_total]
-    resid_ratio = jnp.sum(mine * resid_all[None, :], axis=1) / norm_sq
+    band_energy = jnp.sum(occupancy(jnp.arange(band_total), band_total) * energy_all) / band_total
+    totals = jnp.concatenate([summed[3 * live_total : 3 * live_total + 7], band_energy[None]])
     start = lax.dynamic_slice(order, (me * capacity,), (capacity,))
     own_target = jnp.where(live_mask > 0.5, start, float(live_total)).astype(jnp.int32)
     slot_select = (own_target[None, :] == jnp.arange(live_total)[:, None]).astype(jnp.float32)

time: 172 us -> 162 us (0.942)
  matrix products: 13.6 us -> 38.3 us
  Pallas kernels: 68.6 us -> 45.8 us
  other arithmetic: 25.6 us -> 43.5 us
  local copies, waits for them, and re-layouts: 21.4 us -> 10.5 us
  waiting for transfers between devices: 24.4 us -> 14 us
  starting transfers between devices: 8.38 us -> 4.11 us
  between operations: 8.65 us -> 4.89 us
    all_to_all x2 -> x0, waiting for transfers between devices: 24.4 us -> none  [the longest x1 24.4 us: per_device(): lax.all_to_all(back_one, 'gvec', split_axis=1, concat_axis=2, tiled=True)]
    dot_general x3 -> x16, matrix products: 6.23 us -> 27.4 us  [the longest x3 9.12 us: per_device(): jnp.einsum('nayz,yq->naqz', block, y_rows(step, part), preferred_element_...]
    ppermute x0 -> x4, waiting for transfers between devices: none -> 14 us  [shift(): lax.ppermute(value, 'gvec', [(at, (at + step) % gvec_size) for at in rang...]
    pallas_call x2, Pallas kernels: 37.6 us -> 23.8 us  [gather_all(): pl.pallas_call(functools.partial(gather_kernel, sizes), out_shape=jax.Sha...]
    convert_element_type x1 -> x4, other arithmetic: 3.78 us -> 15.6 us  [the longest x2 6.54 us: per_device(): real_space = sum((jnp.einsum('nayz,xa->nxyz', block, a_columns(step), pre...]
    all_to_all x2 -> x0, starting transfers between devices: 8.38 us -> none  [the longest x1 4.39 us: per_device(): lax.all_to_all(sectioned, 'gvec', split_axis=2, concat_axis=1, tiled=True)]
    pallas_call x1, Pallas kernels: 13.5 us -> 7.91 us  [slab_potential(): pl.pallas_call(potential_kernel, grid=(x_total // rows,), out_shape=jax.S...]
    convert_element_type x2 -> x0, local copies, waits for them, and re-layouts: 5.34 us -> none  [the longest x1 2.67 us: per_device(): sectioned = jnp.einsum('naqz,yq->nayz', sectioned, cosines, preferred_ele...]
  transfers between devices with their start and end apart: 2 -> 4, of which waited for: 1 -> 2; matrix products, arithmetic and copies ran while one was open for 4% -> 19% of each run, Pallas kernels for 15% -> 0%
where the time goes in v2:
time: 162 us; the launch traced here: 161 us
  Pallas kernels  45.8 us (28%)
  other arithmetic  43.5 us (27%)
  matrix products  38.3 us (24%)
  waiting for transfers between devices  14 us (9%)
  local copies, waits for them, and re-layouts  10.5 us (6%)
  between operations  4.89 us (3%)
  starting transfers between devices  4.11 us (3%)
    pallas_call x2, Pallas kernels, gather_all(): pl.pallas_call(functools.partial(gather_kernel, sizes), out_shape=jax.Sha...  23.8 us
    pallas_call x2, Pallas kernels, slab_moments(): pl.pallas_call(force_kernel, grid=(x_total // rows,), out_shape=jax.Shape...  14 us
    ppermute x4, waiting for transfers between devices, shift(): lax.ppermute(value, 'gvec', [(at, (at + step) % gvec_size) for at in rang...  14 us
    dot_general x1, matrix products, per_device(): jnp.einsum('naqz,zl->naql', back_two, cosines, preferred_element_type=jnp...  9.74 us
    dot_general x3, matrix products, per_device(): jnp.einsum('nayz,yq->naqz', block, y_rows(step, part), preferred_element_...  9.12 us
    dot_general x4, matrix products, section_y(): jnp.einsum('naqz,yq->nayz', section_z, y_rows(step, part), preferred_elem...  8.02 us
    pallas_call x1, Pallas kernels, slab_potential(): pl.pallas_call(potential_kernel, grid=(x_total // rows,), out_shape=jax.S...  7.91 us
    convert_element_type x2, other arithmetic, per_device(): real_space = sum((jnp.einsum('nayz,xa->nxyz', block, a_columns(step), pre...  6.54 us
  transfers between devices with their start and end apart: 4, of which 2 were waited for; matrix products, arithmetic and copies ran while one was open for 19% of the time, Pallas kernels for 0%

profile of v2, /device:TPU:0, one launch (start us, length us, event | category | flops | bytes accessed | tf_op | source)
XLA Modules:
  0.0 161.1 jit_solution(6059177094181158582)
XLA Ops:
  1.3 0.7 compare_select_fusion.2
  2.0 0.9 copy.84
  4.2 0.7 fusion.155
  5.5 13.3 %gather_0.1 = f32[32,8,128]{2,1,0:T(8,128)} custom-call(f32[8,128]{1,0:T(8,128)} %select_maximum_fusion.1.x_ref), custom_call_target="tpu_custom_call" | custom-call | tf_op jit(solution)/shard_map/gather_0/pallas_call | solution.py:97
  18.8 0.9 slice_bitcast_fusion.3
  22.2 2.6 %fusion.27 = bf16[64,128,128]{2,1,0:T(8,128)(2,1)S(1)} fusion(bf16[1,64,128,128]{3,2,1,0:T(8,128)(2,1)} %param.7, f32[128]{0:T(128)S(1)} %compare_select_fusion.4, f32[128]{0:T(128)S(1)} %iota_convert_fusion, f32[128]{0:T(128)S(1)} %add_multiply_fusion.2), kind=kOutput, calls=%fused_computation.41 | convolution fusion | flops 269549568 | bytes 4195840 | tf_op jit(solution)/shard_map/naql,zl->naqz/dot_general | solution.py:250
  24.7 1.3 fusion.76
  26.3 1.2 fusion.31
  27.5 1.1 collective-permute-start
  28.7 2.8 %fusion.33 = bf16[1,64,32,128]{3,2,1,0:T(8,128)(2,1)} fusion(bf16[64,128,128]{2,1,0:T(8,128)(2,1)} %copy-done.2, bf16[128,128]{1,0:T(8,128)(2,1)S(1)} %get-tuple-element.85, s32[]{:T(128)S(6)} %select_n.118), kind=kOutput, calls=%fused_computation.53 | convolution fusion | flops 67371008 | bytes 2629636 | tf_op jit(solution)/shard_map/naqz,yq->nayz/dot_general | solution.py:255
  31.5 0.9 collective-permute-start.2
  33.0 2.9 %fusion.7 = (f32[]{:T(128)}, f32[64,128]{1,0:T(8,128)S(1)}, f32[64,128]{1,0:T(8,128)S(1)}, f32[128,128]{1,0:T(8,128)S(1)}, f32[64]{0:T(128)S(1)}, /*index=5*/f32[128]{0:T(128)S(1)}, f32[128]{0:T(128)S(1)}) fusion(bf16[1,64,128,128]{3,2,1,0:T(8,128)(2,1)S(1)} %copy-done.1, f32[]{:T(128)S(6)} %div.106), kind=kLoop, calls=%fused_computation.17 | loop fusion | flops 11501247 | bytes 2229512 | tf_op jit(solution)/shard_map/reduce_sum | solution.py:270
  36.5 0.7 multiply_reduce_fusion.1
  37.8 0.7 fusion.83
  38.6 3.7 %stack.51 = f32[6]{0:T(128)S(1)} concatenate(f32[1]{0:T(128)} %bitcast.38, f32[1]{0:T(128)} %bitcast.39, f32[1]{0:T(128)} %bitcast.40, f32[1]{0:T(128)} %bitcast.41, f32[1]{0:T(128)} %bitcast.42, f32[1]{0:T(128)} %bitcast.43), dimensions={0} | concatenate | bytes 48 | tf_op jit(solution)/shard_map/stack | solution.py:49
  42.9 2.0 %fusion.32 = bf16[64,32,128]{2,1,0:T(8,128)(2,1)S(1)} fusion(bf16[64,128,128]{2,1,0:T(8,128)(2,1)} %copy-done.2, bf16[128,128]{1,0:T(8,128)(2,1)S(1)} %get-tuple-element.85, s32[]{:T(128)S(6)} %select_n.119), kind=kOutput, calls=%fused_computation.52 | convolution fusion | flops 67371008 | bytes 2629636 | tf_op jit(solution)/shard_map/naqz,yq->nayz/dot_general | solution.py:255
  44.9 2.0 %fusion.30 = bf16[64,32,128]{2,1,0:T(8,128)(2,1)S(1)} fusion(bf16[64,128,128]{2,1,0:T(8,128)(2,1)} %copy-done.2, bf16[128,128]{1,0:T(8,128)(2,1)S(1)} %get-tuple-element.85, s32[]{:T(128)S(6)} %select_n.117), kind=kOutput, calls=%fused_computation.50 | convolution fusion | flops 67371008 | bytes 2629636 | tf_op jit(solution)/shard_map/naqz,yq->nayz/dot_general | solution.py:255
  47.0 0.8 fusion.88
  48.3 1.4 fusion.156
  49.7 1.9 %pad_maximum_fusion = (f32[128,512]{1,0:T(8,128)}, f32[128,512]{1,0:T(8,128)}) fusion(f32[128,128]{1,0:T(8,128)} %get-tuple-element.80, f32[128,128]{1,0:T(8,128)S(1)} %get-tuple-element.78, f32[128,128]{1,0:T(8,128)S(1)} %get-tuple-element.79, f32[128,128]{1,0:T(8,128)S(1)} %get-tuple-element.77, f32[128,128]{1,0:T(8,128)} %get-tuple-element.83, ...), kind=kLoop, calls=%fused_computation.108 | loop fusion | flops 393216 | bytes 1048576 | tf_op jit(solution)/shard_map/concatenate | solution.py:36
  52.1 0.7 fusion.161
  52.8 1.5 fusion.45
  54.3 1.5 fusion.53
  55.8 3.3 %fusion.26.real_ref = bf16[128,32,128]{2,1,0:T(8,128)(2,1)} fusion(f32[128,32,128]{2,0,1:T(8,128)S(1)} %fusion.53, f32[128,32,128]{2,0,1:T(8,128)S(1)} %fusion.55), kind=kLoop, calls=%fused_computation.40 | loop fusion | flops 1048576 | bytes 5242880 | tf_op jit(solution)/shard_map/convert_element_type | solution.py:283
  59.1 3.3 %fusion.25.real_ref = bf16[128,32,128]{2,1,0:T(8,128)(2,1)} fusion(f32[128,32,128]{2,0,1:T(8,128)S(1)} %fusion.45, f32[128,32,128]{2,0,1:T(8,128)S(1)} %fusion.47), kind=kLoop, calls=%fused_computation.38 | loop fusion | flops 1048576 | bytes 5242880 | tf_op jit(solution)/shard_map/convert_element_type | solution.py:283
  62.4 6.9 %slab_moments.2 = f32[3,128,512]{2,1,0:T(8,128)} custom-call(f32[128,512]{1,0:T(8,128)} %get-tuple-element.90.x_ref.xv_ref, f32[128,512]{1,0:T(8,128)} %get-tuple-element.91.xs_ref, f32[32,512]{1,0:T(8,128)} %get-tuple-element.92.yv_ref, f32[32,512]{1,0:T(8,128)} %get-tuple-element.41.ys_ref, bf16[128,32,128]{2,1,0:T(8,128)(2,1)} %fusion.26.real_ref), custom_call_target="tpu_custom_call" | custom-call | flops 3221225472 | bytes 1048576 | tf_op jit(solution)/shard_map/slab_moments/pallas_call | solution.py:173
  69.4 7.1 %slab_moments.3 = f32[3,128,512]{2,1,0:T(8,128)} custom-call(f32[128,512]{1,0:T(8,128)} %get-tuple-element.90.x_ref.xv_ref, f32[128,512]{1,0:T(8,128)} %get-tuple-element.91.xs_ref, f32[32,512]{1,0:T(8,128)} %get-tuple-element.93.yv_ref, f32[32,512]{1,0:T(8,128)} %get-tuple-element.40.ys_ref, bf16[128,32,128]{2,1,0:T(8,128)(2,1)} %fusion.25.real_ref), custom_call_target="tpu_custom_call" | custom-call | flops 3221225472 | bytes 1048576 | tf_op jit(solution)/shard_map/slab_moments/pallas_call | solution.py:173
  76.5 1.3 add_multiply_fusion.1
  77.9 1.4 fusion.60
  79.3 7.9 %slab_potential.1 = f32[128,64,128]{2,1,0:T(8,128)} custom-call(f32[128,512]{1,0:T(8,128)} %get-tuple-element.90.x_ref.xv_ref, f32[64,512]{1,0:T(8,128)} %copy-done.5, bf16[128,512]{1,0:T(8,128)(2,1)} %get-tuple-element.33.depth_ref, bf16[128,64,128]{2,1,0:T(8,128)(2,1)} %local_ref.1), custom_call_target="tpu_custom_call" | custom-call | flops 4294967296 | bytes 6291456 | tf_op jit(solution)/shard_map/slab_potential/pallas_call | solution.py:132
  87.2 3.2 %fusion.22 = (bf16[128,32,128]{2,1,0:T(8,128)(2,1)S(1)}, bf16[1,128,32,128]{3,2,1,0:T(8,128)(2,1)S(1)}) fusion(f32[128,64,128]{2,1,0:T(8,128)} %slab_potential.1, bf16[128,32,128]{2,1,0:T(8,128)(2,1)S(1)} %copy-done.3, bf16[128,32,128]{2,1,0:T(8,128)(2,1)} %fusion.25.real_ref), kind=kLoop, calls=%fused_computation.34 | loop fusion | flops 3145728 | bytes 8388608 | tf_op jit(solution)/shard_map/convert_element_type | solution.py:284
  90.9 1.3 fusion.35
  92.8 1.4 collective-permute-start.3
  94.1 2.7 %fusion.49 = f32[128,64,128]{2,0,1:T(8,128)} fusion(bf16[64,32,128]{2,0,1:T(8,128)(2,1)S(1)} %convolution_convert_fusion.2, bf16[128,128]{1,0:T(8,128)(2,1)S(1)} %get-tuple-element.85, s32[]{:T(128)S(6)} %select_n.117), kind=kOutput, calls=%fused_computation.69 | convolution fusion | flops 67108864 | bytes 4726788 | tf_op jit(solution)/shard_map/nayz,yq->naqz/dot_general | solution.py:313
  96.8 1.3 fusion.34
  98.1 0.7 collective-permute-start.1
  100.7 7.1 %collective-permute-done.3 = bf16[1,64,32,128]{3,1,2,0:T(8,128)(2,1)S(1)} collective-permute-done((bf16[1,64,32,128]{3,1,2,0:T(8,128)(2,1)}, bf16[1,64,32,128]{3,1,2,0:T(8,128)(2,1)S(1)}, u32[]{:S(2)}, u32[]{:S(2)}) %collective-permute-start.3) | collective-permute-done | bytes 524320 | tf_op jit(solution)/shard_map/ppermute | solution.py:246
  107.8 2.7 %fusion.43 = f32[128,64,128]{2,0,1:T(8,128)} fusion(bf16[64,32,128]{2,0,1:T(8,128)(2,1)S(1)} %bitcast.196, bf16[128,128]{1,0:T(8,128)(2,1)S(1)} %get-tuple-element.85, s32[]{:T(128)S(6)} %select_n.118), kind=kOutput, calls=%fused_computation.63 | convolution fusion | flops 67108864 | bytes 4726788 | tf_op jit(solution)/shard_map/nayz,yq->naqz/dot_general | solution.py:313
  110.5 6.9 %collective-permute-done.1 = bf16[1,64,32,128]{3,1,2,0:T(8,128)(2,1)} collective-permute-done((bf16[1,64,32,128]{3,1,2,0:T(8,128)(2,1)}, bf16[1,64,32,128]{3,1,2,0:T(8,128)(2,1)}, u32[]{:S(2)}, u32[]{:S(2)}) %collective-permute-start.1) | collective-permute-done | bytes 524320 | tf_op jit(solution)/shard_map/ppermute | solution.py:246
  117.4 3.7 %fusion.51 = f32[128,64,128]{2,0,1:T(8,128)} fusion(bf16[64,32,128]{2,0,1:T(8,128)(2,1)} %bitcast.24, bf16[128,128]{1,0:T(8,128)(2,1)S(1)} %get-tuple-element.85, s32[]{:T(128)S(6)} %select_n.114), kind=kOutput, calls=%fused_computation.71 | convolution fusion | flops 67108864 | bytes 4726788 | tf_op jit(solution)/shard_map/nayz,yq->naqz/dot_general | solution.py:313
  121.2 9.7 %fusion.8 = (f32[]{:T(128)}, f32[64,128,128]{2,1,0:T(8,128)}) fusion(bf16[1,64,128,128]{3,2,1,0:T(8,128)(2,1)S(1)} %copy-done.1, f32[128]{0:T(128)S(1)} %fusion.158, f32[64,128]{1,0:T(8,128)S(1)} %broadcast_add_fusion, bf16[128,128]{1,0:T(8,128)(2,1)S(1)} %get-tuple-element.85, f32[128,64,128]{2,0,1:T(8,128)} %fusion.43, f32[128,64,128]{2,0,1:T(8,128)} %fusion.51, ...), kind=kOutput, calls=%fused_computation.18 | convolution fusion | flops 347078656 | bytes 19472904 | tf_op jit(solution)/shard_map/naqz,zl->naql/dot_general | solution.py:317
  131.6 4.4 %fusion.11 = f32[]{:T(128)} fusion(bf16[1,64,128,128]{3,2,1,0:T(8,128)(2,1)S(1)} %copy-done.1, f32[64,128,128]{2,1,0:T(8,128)} %get-tuple-element.87, f32[]{:T(128)} %bitcast.65, f32[128]{0:T(128)S(1)} %fusion.158, f32[64,128]{1,0:T(8,128)S(1)} %broadcast_add_fusion), kind=kLoop, calls=%fused_computation.21 | loop fusion | flops 9437183 | bytes 6324744 | tf_op jit(solution)/shard_map/reduce_sum | solution.py:322
  136.0 1.9 %pad_maximum_fusion.5 = f32[3,1]{0,1:T(1,128)S(1)} fusion(f32[1,1]{0,1:T(1,128)} %bitcast.66, f32[1,1]{0,1:T(1,128)} %bitcast.63, f32[1,1]{0,1:T(1,128)} %bitcast.62), kind=kLoop, calls=%fused_computation.266 | loop fusion | flops 6 | bytes 24 | tf_op jit(solution)/shard_map/stack | solution.py:325
  138.7 10.6 %gather_1.1 = f32[32,8,128]{2,1,0:T(8,128)} custom-call(f32[8,128]{1,0:T(8,128)} %select_maximum_fusion.x_ref), custom_call_target="tpu_custom_call" | custom-call | tf_op jit(solution)/shard_map/gather_1/pallas_call | solution.py:97
  149.2 0.9 slice_reduce_fusion
  150.2 1.0 slice_reduce_fusion.1
  151.3 0.8 fusion.80
  153.0 5.9 %fusion.15 = bf16[1,64,128,128]{3,2,1,0:T(8,128)(2,1)} fusion(bf16[1,64,128,128]{3,2,1,0:T(8,128)(2,1)S(1)} %copy-done.1, f32[64,128,128]{2,1,0:T(8,128)} %get-tuple-element.87, f32[]{:T(128)} %get-tuple-element.29, f32[128]{0:T(128)S(1)} %fusion.158, f32[64,128]{1,0:T(8,128)S(1)} %broadcast_add_fusion), kind=kLoop, calls=%fused_computation.27 | loop fusion | flops 12582912 | bytes 8421892 | tf_op jit(solution)/shard_map/convert_element_type | solution.py:346
  (92 shorter events, 12.6 us)
Async XLA Ops:
  0.6 2.3 %copy-start = (f32[1024]{0:T(1024)S(1)}, f32[1024]{0:T(1024)}, u32[]{:S(2)}) copy-start(f32[1024]{0:T(1024)} %param.10) | copy-start | bytes 12292
  24.7 1.6 copy-start.2
  24.7 8.3 %copy-start.1 = (bf16[1,64,128,128]{3,2,1,0:T(8,128)(2,1)S(1)}, bf16[1,64,128,128]{3,2,1,0:T(8,128)(2,1)}, u32[]{:S(2)}) copy-start(bf16[1,64,128,128]{3,2,1,0:T(8,128)(2,1)} %param.7) | copy-start | bytes 6291460
  27.5 26.8 %collective-permute-start = (bf16[1,64,32,128]{3,2,1,0:T(8,128)(2,1)}, bf16[1,64,32,128]{3,2,1,0:T(8,128)(2,1)}, u32[]{:S(2)}, u32[]{:S(2)}) collective-permute-start(bf16[1,64,32,128]{3,2,1,0:T(8,128)(2,1)} %fusion.31), channel_id=1, source_target_pairs={{0,4},{4,0},{1,5},{5,1},{2,6},{6,2},{3,7},{7,3},{8,12},{12,8},{9,1... | collective-permute-start | bytes 1572872 | tf_op jit(solution)/shard_map/ppermute | solution.py:246
  31.5 15.5 %copy-start.15 = (f32[4]{0:T(128)S(1)}, f32[4]{0:T(128)}, u32[]{:S(2)}) copy-start(f32[4]{0:T(128)} %constant.165.clone) | copy-start | bytes 52
  31.5 21.3 %collective-permute-start.2 = (bf16[1,64,32,128]{3,2,1,0:T(8,128)(2,1)}, bf16[1,64,32,128]{3,2,1,0:T(8,128)(2,1)}, u32[]{:S(2)}, u32[]{:S(2)}) collective-permute-start(bf16[1,64,32,128]{3,2,1,0:T(8,128)(2,1)} %fusion.33), channel_id=1, source_target_pairs={{0,4},{4,0},{1,5},{5,1},{2,6},{6,2},{3,7},{7,3},{8,12},{12,8},{9,1... | collective-permute-start | bytes 1572872 | tf_op jit(solution)/shard_map/ppermute | solution.py:246
  49.7 6.1 %copy-start.5 = (f32[64,512]{1,0:T(8,128)}, f32[64,512]{1,0:T(8,128)S(1)}, u32[]{:S(2)}) copy-start(f32[64,512]{1,0:T(8,128)S(1)} %pad_maximum_fusion.3.y_ref) | copy-start | bytes 393220
  69.3 7.2 %copy-start.4 = (f32[3,128,512]{2,1,0:T(8,128)S(1)}, f32[3,128,512]{2,1,0:T(8,128)}, u32[]{:S(2)}) copy-start(f32[3,128,512]{2,1,0:T(8,128)} %slab_moments.2) | copy-start | bytes 2359300
  69.3 8.5 %copy-start.6 = (f32[128,128]{1,0:T(8,128)S(1)}, f32[128,128]{1,0:T(8,128)}, u32[]{:S(2)}) copy-start(f32[128,128]{1,0:T(8,128)} %get-tuple-element.53) | copy-start | bytes 196612
  69.3 8.5 %copy-start.7 = (f32[128,128]{1,0:T(8,128)S(1)}, f32[128,128]{1,0:T(8,128)}, u32[]{:S(2)}) copy-start(f32[128,128]{1,0:T(8,128)} %get-tuple-element.54) | copy-start | bytes 196612
  69.3 8.5 %copy-start.8 = (f32[128,128]{1,0:T(8,128)S(1)}, f32[128,128]{1,0:T(8,128)}, u32[]{:S(2)}) copy-start(f32[128,128]{1,0:T(8,128)} %get-tuple-element.55) | copy-start | bytes 196612
  69.4 8.5 %copy-start.9 = (f32[128,128]{1,0:T(8,128)S(1)}, f32[128,128]{1,0:T(8,128)}, u32[]{:S(2)}) copy-start(f32[128,128]{1,0:T(8,128)} %get-tuple-element.56) | copy-start | bytes 196612
  69.4 8.5 %copy-start.10 = (f32[128,128]{1,0:T(8,128)S(1)}, f32[128,128]{1,0:T(8,128)}, u32[]{:S(2)}) copy-start(f32[128,128]{1,0:T(8,128)} %get-tuple-element.57) | copy-start | bytes 196612
  69.4 8.5 %copy-start.11 = (f32[128,128]{1,0:T(8,128)S(1)}, f32[128,128]{1,0:T(8,128)}, u32[]{:S(2)}) copy-start(f32[128,128]{1,0:T(8,128)} %get-tuple-element.58) | copy-start | bytes 196612
  69.4 8.5 %copy-start.12 = (f32[128,128]{1,0:T(8,128)S(1)}, f32[128,128]{1,0:T(8,128)}, u32[]{:S(2)}) copy-start(f32[128,128]{1,0:T(8,128)} %get-tuple-element.59) | copy-start | bytes 196612
  69.4 8.5 %copy-start.13 = (f32[128,128]{1,0:T(8,128)S(1)}, f32[128,128]{1,0:T(8,128)}, u32[]{:S(2)}) copy-start(f32[128,128]{1,0:T(8,128)} %get-tuple-element.60) | copy-start | bytes 196612
  79.3 7.9 %copy-start.3 = (bf16[128,32,128]{2,1,0:T(8,128)(2,1)S(1)}, bf16[128,32,128]{2,1,0:T(8,128)(2,1)}, u32[]{:S(2)}) copy-start(bf16[128,32,128]{2,1,0:T(8,128)(2,1)} %fusion.26.real_ref) | copy-start | bytes 3145732
  92.2 8.4 %copy-start.16 = (f32[6]{0:T(128)S(1)}, f32[6]{0:T(128)}, u32[]{:S(2)}) copy-start(f32[6]{0:T(128)} %broadcast_multiply_fusion.1) | copy-start | bytes 76
  92.8 15.1 %collective-permute-start.3 = (bf16[1,64,32,128]{3,1,2,0:T(8,128)(2,1)}, bf16[1,64,32,128]{3,1,2,0:T(8,128)(2,1)S(1)}, u32[]{:S(2)}, u32[]{:S(2)}) collective-permute-start(bf16[1,64,32,128]{3,1,2,0:T(8,128)(2,1)} %fusion.35), channel_id=1, source_target_pairs={{0,4},{4,0},{1,5},{5,1},{2,6},{6,2},{3,7},{7,3},{8,12},{12,8},{9,1... | collective-permute-start | bytes 1572872 | tf_op jit(solution)/shard_map/ppermute | solution.py:246
  98.1 19.3 %collective-permute-start.1 = (bf16[1,64,32,128]{3,1,2,0:T(8,128)(2,1)}, bf16[1,64,32,128]{3,1,2,0:T(8,128)(2,1)}, u32[]{:S(2)}, u32[]{:S(2)}) collective-permute-start(bf16[1,64,32,128]{3,1,2,0:T(8,128)(2,1)} %fusion.34), channel_id=1, source_target_pairs={{0,4},{4,0},{1,5},{5,1},{2,6},{6,2},{3,7},{7,3},{8,12},{12,8},{9,1... | collective-permute-start | bytes 1572872 | tf_op jit(solution)/shard_map/ppermute | solution.py:246
  130.9 20.3 %copy-start.17 = (s32[16]{0:T(128)S(1)}, s32[16]{0:T(128)}, u32[]{:S(2)}) copy-start(s32[16]{0:T(128)} %fusion.156) | copy-start | bytes 196
  130.9 20.4 %copy-start.14 = (s32[16]{0:T(128)S(1)}, s32[16]{0:T(128)}, u32[]{:S(2)}) copy-start(s32[16]{0:T(128)} %param.11) | copy-start | bytes 196

commit v3 on v2

--- a/solution.py
+++ b/solution.py
@@ -260,18 +260,8 @@
         [shift(section_y(-step, part), -step) for step in range(1, gvec_size)]
         for part in range(chunks)
     ]
-    coeff_wide = coeffs.astype(jnp.float32)
-    wave_step = jnp.pi / extent
-    x_wave = (gvec_id * x_local + jnp.arange(x_local)).astype(jnp.float32) * wave_step
-    y_wave = jnp.arange(extent).astype(jnp.float32) * wave_step
-    kinetic = 0.5 * (
-        x_wave[:, None, None] ** 2 + y_wave[None, :, None] ** 2 + y_wave[None, None, :] ** 2
-    )
-    norm_part = jnp.sum(coeff_wide * coeff_wide, axis=(1, 2, 3))
-    weighted = jnp.sum(weight[:, None, None, None] * coeff_wide * coeff_wide, axis=0)
-    stress_local = stress_terms(weighted, x_wave, y_wave) / cell_count
-
     moments = 0.0
+    reals = []
     returned = []
     own_sections = [section_y(0, part) for part in range(chunks)]
     for part in range(chunks):
@@ -288,15 +278,33 @@
                 "nxyz,xa->nayz", applied, a_columns(step), preferred_element_type=jnp.float32
             ).astype(jnp.bfloat16)
 
+        sent = [back_x(step) for step in range(1, gvec_size)]
         if part == chunks - 1:
-            applied, stress_local, norm_part = lax.optimization_barrier(
-                (applied, stress_local, norm_part)
+            sent, held_coeffs, reals = lax.optimization_barrier(
+                (sent, coeffs, reals + [real_space])
             )
-        returned.append([shift(back_x(step), step) for step in range(1, gvec_size)] + [back_x(0)])
+        else:
+            reals.append(real_space)
+        returned.append(
+            [shift(block, step) for step, block in enumerate(sent, 1)] + [back_x(0)]
+        )
+    for part in range(chunks):
+        window = slice(part * chunk, (part + 1) * chunk)
         for band in range(local_bands):
             moments = moments + weight[band] * slab_moments(
-                x_value, x_slope, y_value[window], y_slope[window], real_space[band]
+                x_value, x_slope, y_value[window], y_slope[window], reals[part][band]
             )
+    coeff_wide = held_coeffs.astype(jnp.float32)
+    wave_step = jnp.pi / extent
+    x_wave = (gvec_id * x_local + jnp.arange(x_local)).astype(jnp.float32) * wave_step
+    y_wave = jnp.arange(extent).astype(jnp.float32) * wave_step
+    kinetic = 0.5 * (
+        x_wave[:, None, None] ** 2 + y_wave[None, :, None] ** 2 + y_wave[None, None, :] ** 2
+    )
+    norm_part = jnp.sum(coeff_wide * coeff_wide, axis=(1, 2, 3))
+    weighted = jnp.sum(weight[:, None, None, None] * coeff_wide * coeff_wide, axis=0)
+    stress_local = stress_terms(weighted, x_wave, y_wave) / cell_count
+
     embedding = jnp.sum(moments[0] * depth.astype(jnp.float32)) / cell_count
     force_terms = jnp.stack(
         [
@@ -322,15 +330,13 @@
     resid_part = jnp.sum(own_residual * own_residual, axis=(1, 2, 3))
     local_totals = jnp.concatenate([stress_local, embedding[None]])
     mine = (jnp.arange(band_total)[None, :] == band_ids[:, None]).astype(jnp.float32)
-    band_rows = jnp.stack([norm_part, inner_part, resid_part])
-    flat = jnp.concatenate([forces.reshape(-1), local_totals])
-    flat = jnp.pad(flat, (0, -flat.shape[0] % 128)).reshape(-1, 128)
-    bands = jnp.pad(band_rows, ((0, -(flat.shape[0] + 3) % 8), (0, 128 - local_bands)))
-    parts = gather_all(jnp.concatenate([flat, bands]), sizes, 1)
-    lines = flat.shape[0]
-    summed = jnp.sum(parts[:, :lines], axis=0).reshape(-1)
+    flat = jnp.concatenate([forces.reshape(-1), local_totals, norm_part, inner_part, resid_part])
+    flat = jnp.pad(flat, (0, -flat.shape[0] % 1024)).reshape(-1, 128)
+    parts = gather_all(flat, sizes, 1).reshape(devices, -1)
+    lines = 3 * live_total + 7
+    summed = jnp.sum(parts[:, :lines], axis=0)
     force_all = summed[: 3 * live_total].reshape(3, live_total)
-    by_group = parts[:, lines : lines + 3, :local_bands].reshape(
+    by_group = parts[:, lines : lines + 3 * local_bands].reshape(
         sizes[0], gvec_size, sizes[2], 3, local_bands
     )
     norms, inners, squares = by_group[:, :, :, 0], by_group[:, :, :, 1], by_group[:, :, :, 2]

time: 162 us -> 146 us (0.901)
  waiting for transfers between devices: 14 us -> 3.97 us
  other arithmetic: 43.5 us -> 36.9 us
  local copies, waits for them, and re-layouts: 10.5 us -> 12.4 us
  matrix products: 38.3 us -> 36.4 us
    ppermute x4, waiting for transfers between devices: 14 us -> 3.97 us  [shift(): lax.ppermute(value, 'gvec', [(at, (at + step) % gvec_size) for at in rang...]
    convert_element_type x4 -> x2, other arithmetic: 7.06 us -> 0.01 us  [the longest x1 0.01 us: per_device(): y_points = (gvec_id * y_share + jnp.arange(y_share)).astype(jnp.float32)]
    dot_general x4, matrix products: 8.02 us -> 4.84 us  [section_y(): jnp.einsum('naqz,yq->nayz', section_z, y_rows(step, part), preferred_elem...]
    convert_element_type x1, other arithmetic: 3.23 us -> 6.3 us  [per_device(): (field_total[None, :, window] * real_space.astype(jnp.float32)).astype(jn...]
    reduce_sum x3, other arithmetic: 5.19 us -> 2.33 us  [the longest x1 1.71 us: per_device(): embedding = jnp.sum(moments[0] * depth.astype(jnp.float32)) / cell_count]
    concatenate x3 -> x4, other arithmetic: 1.91 us -> 3.99 us  [kernels(): return (jnp.concatenate(values, axis=1), jnp.concatenate(slopes, axis=1))]
    concatenate x0 -> x1, local copies, waits for them, and re-layouts: none -> 2.02 us  [per_device(): jnp.concatenate([forces.reshape(-1), local_totals, norm_part, inner_part,...]
    another operation x3 -> x2, other arithmetic: 2.27 us -> 0.34 us  [the longest x1 1.93 us: per_device(): band_rows = jnp.stack([norm_part, inner_part, resid_part])]
  transfers between devices with their start and end apart: 4 -> 4, of which waited for: 2 -> 2; matrix products, arithmetic and copies ran while one was open for 19% -> 17% of each run, Pallas kernels for 0% -> 15%
where the time goes in v3:
time: 146 us; the launch traced here: 145 us
  Pallas kernels  46.1 us (32%)
  other arithmetic  36.9 us (25%)
  matrix products  36.4 us (25%)
  local copies, waits for them, and re-layouts  12.4 us (8%)
  between operations  4.91 us (3%)
  starting transfers between devices  4.05 us (3%)
  waiting for transfers between devices  3.97 us (3%)
    pallas_call x2, Pallas kernels, gather_all(): pl.pallas_call(functools.partial(gather_kernel, sizes), out_shape=jax.Sha...  24.2 us
    pallas_call x2, Pallas kernels, slab_moments(): pl.pallas_call(force_kernel, grid=(x_total // rows,), out_shape=jax.Shape...  14 us
    dot_general x1, matrix products, per_device(): jnp.einsum('naqz,zl->naql', back_two, cosines, preferred_element_type=jnp...  9.78 us
    dot_general x3, matrix products, per_device(): jnp.einsum('nayz,yq->naqz', block, y_rows(step, part), preferred_element_...  9.25 us
    pallas_call x1, Pallas kernels, slab_potential(): pl.pallas_call(potential_kernel, grid=(x_total // rows,), out_shape=jax.S...  7.9 us
    convert_element_type x1, other arithmetic, per_device(): (field_total[None, :, window] * real_space.astype(jnp.float32)).astype(jn...  6.3 us
    reduce_sum x1, other arithmetic, per_device(): resid_part = jnp.sum(own_residual * own_residual, axis=(1, 2, 3))  5.89 us
    convert_element_type x1, other arithmetic, per_device(): (coeff_wide - step_size * residual / (1.0 + kinetic[None])).astype(jnp.bf...  5.86 us
  transfers between devices with their start and end apart: 4, of which 2 were waited for; matrix products, arithmetic and copies ran while one was open for 17% of the time, Pallas kernels for 15%

profile of v3, /device:TPU:0, one launch (start us, length us, event | category | flops | bytes accessed | tf_op | source)
XLA Modules:
  0.0 144.7 jit_solution(9003066987319760527)
XLA Ops:
  1.3 0.7 compare_select_fusion.2
  2.0 0.9 copy.55
  3.0 0.6 gather_fusion.1
  4.2 0.7 fusion.154
  5.5 13.3 %gather_0.1 = f32[32,8,128]{2,1,0:T(8,128)} custom-call(f32[8,128]{1,0:T(8,128)} %select_maximum_fusion.x_ref), custom_call_target="tpu_custom_call" | custom-call | tf_op jit(solution)/shard_map/gather_0/pallas_call | solution.py:97
  18.8 0.9 slice_bitcast_fusion.3
  20.7 0.7 select_convert_fusion
  21.7 2.6 %fusion.27 = bf16[64,128,128]{2,1,0:T(8,128)(2,1)S(1)} fusion(bf16[1,64,128,128]{3,2,1,0:T(8,128)(2,1)} %param.7, f32[128]{0:T(128)S(1)} %compare_select_fusion.4, f32[128]{0:T(128)S(1)} %iota_convert_fusion, f32[128]{0:T(128)S(1)} %add_multiply_fusion.2), kind=kOutput, calls=%fused_computation.41 | convolution fusion | flops 269549568 | bytes 4195840 | tf_op jit(solution)/shard_map/naql,zl->naqz/dot_general | solution.py:250
  24.2 1.3 fusion.75
  25.5 1.2 fusion.31
  26.8 1.1 collective-permute-start
  27.9 1.2 fusion.33
  29.1 0.9 collective-permute-start.1
  30.7 1.2 fusion.32
  31.9 1.2 fusion.30
  33.4 1.5 %fusion.54 = f32[128,32,128]{2,0,1:T(8,128)S(1)} fusion(bf16[64,32,128]{2,1,0:T(8,128)(2,1)} %fusion.30, bf16[128,128]{1,0:T(8,128)(2,1)S(1)} %get-tuple-element.94, s32[]{:T(128)S(6)} %select_n.116), kind=kOutput, calls=%fused_computation.74 | convolution fusion | flops 67108864 | bytes 2654212 | tf_op jit(solution)/shard_map/nayz,xa->nxyz/dot_general | solution.py:271
  34.9 1.3 fusion.155
  36.2 0.7 pad_maximum_fusion.3.y_ref
  36.9 1.6 %pad_maximum_fusion.2.xs_ref = f32[128,512]{1,0:T(8,128)} fusion(f32[128,128]{1,0:T(8,128)} %get-tuple-element.92, f32[128,128]{1,0:T(8,128)} %get-tuple-element.91, f32[128,128]{1,0:T(8,128)} %get-tuple-element.90, f32[128,128]{1,0:T(8,128)} %get-tuple-element.93), kind=kLoop, calls=%fused_computation.109 | loop fusion | flops 196608 | bytes 524288 | tf_op jit(solution)/shard_map/concatenate | solution.py:36
  38.5 1.7 %pad_maximum_fusion = (f32[128,512]{1,0:T(8,128)}, bf16[128,512]{1,0:T(8,128)(2,1)}) fusion(f32[128,128]{1,0:T(8,128)} %get-tuple-element.89, f32[128,128]{1,0:T(8,128)} %get-tuple-element.87, f32[128,128]{1,0:T(8,128)} %get-tuple-element.88, f32[128,128]{1,0:T(8,128)S(1)} %get-tuple-element.86, f32[128,128]{1,0:T(8,128)S(1)} %get-tuple-element.66, ...), kind=kLoop, calls=%fused_computation.107 | loop fusion | flops 524288 | bytes 919552 | tf_op jit(solution)/shard_map/concatenate | solution.py:36
  40.2 7.9 %slab_potential.1 = f32[128,64,128]{2,1,0:T(8,128)} custom-call(f32[128,512]{1,0:T(8,128)} %get-tuple-element.96.x_ref.xv_ref, f32[64,512]{1,0:T(8,128)} %pad_maximum_fusion.3.y_ref, bf16[128,512]{1,0:T(8,128)(2,1)} %get-tuple-element.97.depth_ref, bf16[128,64,128]{2,1,0:T(8,128)(2,1)} %local_ref.1), custom_call_target="tpu_custom_call" | custom-call | flops 4294967296 | bytes 6291456 | tf_op jit(solution)/shard_map/slab_potential/pallas_call | solution.py:132
  48.6 0.7 fusion.162
  49.3 2.6 %collective-permute-done.1 = bf16[1,64,32,128]{3,2,1,0:T(8,128)(2,1)} collective-permute-done((bf16[1,64,32,128]{3,2,1,0:T(8,128)(2,1)}, bf16[1,64,32,128]{3,2,1,0:T(8,128)(2,1)}, u32[]{:S(2)}, u32[]{:S(2)}) %collective-permute-start.1) | collective-permute-done | bytes 524320 | tf_op jit(solution)/shard_map/ppermute | solution.py:246
  51.9 1.5 %fusion.48 = f32[128,32,128]{2,0,1:T(8,128)S(1)} fusion(bf16[64,32,128]{2,1,0:T(8,128)(2,1)} %bitcast.33, bf16[128,128]{1,0:T(8,128)(2,1)S(1)} %get-tuple-element.94, s32[]{:T(128)S(6)} %select_n.111), kind=kOutput, calls=%fused_computation.68 | convolution fusion | flops 67108864 | bytes 2654212 | tf_op jit(solution)/shard_map/nayz,xa->nxyz/dot_general | solution.py:271
  53.4 1.5 %fusion.52 = f32[128,32,128]{2,0,1:T(8,128)S(1)} fusion(bf16[64,32,128]{2,1,0:T(8,128)(2,1)} %bitcast.22, bf16[128,128]{1,0:T(8,128)(2,1)S(1)} %get-tuple-element.94, s32[]{:T(128)S(6)} %select_n.111), kind=kOutput, calls=%fused_computation.72 | convolution fusion | flops 67108864 | bytes 2654212 | tf_op jit(solution)/shard_map/nayz,xa->nxyz/dot_general | solution.py:271
  55.0 6.3 %fusion.21 = (bf16[128,32,128]{2,1,0:T(8,128)(2,1)S(1)}, bf16[128,32,128]{2,1,0:T(8,128)(2,1)}, bf16[128,32,128]{2,1,0:T(8,128)(2,1)S(1)}, bf16[128,32,128]{2,1,0:T(8,128)(2,1)}) fusion(f32[128,64,128]{2,1,0:T(8,128)S(1)} %copy-done.2, f32[128,32,128]{2,0,1:T(8,128)S(1)} %fusion.48, f32[128,32,128]{2,0,1:T(8,128)S(1)} %fusion.50, ...), kind=kLoop, calls=%fused_computation.32 | loop fusion | flops 5242880 | bytes 16777216 | tf_op jit(solution)/shard_map/convert_element_type | solution.py:274
  61.8 1.3 fusion.35
  63.1 1.3 fusion.34
  64.4 1.4 collective-permute-start.3
  66.4 2.7 %fusion.44 = f32[128,64,128]{2,0,1:T(8,128)} fusion(bf16[64,32,128]{2,0,1:T(8,128)(2,1)S(1)} %convolution_convert_fusion.1, bf16[128,128]{1,0:T(8,128)(2,1)S(1)} %get-tuple-element.94, s32[]{:T(128)S(6)} %select_n.119), kind=kOutput, calls=%fused_computation.64 | convolution fusion | flops 67108864 | bytes 4726788 | tf_op jit(solution)/shard_map/nayz,yq->naqz/dot_general | solution.py:321
  69.1 7.0 %slab_moments.2 = f32[3,128,512]{2,1,0:T(8,128)} custom-call(f32[128,512]{1,0:T(8,128)} %get-tuple-element.96.x_ref.xv_ref, f32[128,512]{1,0:T(8,128)} %pad_maximum_fusion.2.xs_ref, f32[32,512]{1,0:T(8,128)} %get-tuple-element.98.yv_ref, f32[32,512]{1,0:T(8,128)} %get-tuple-element.50.ys_ref, bf16[128,32,128]{2,1,0:T(8,128)(2,1)} %get-tuple-element.40), custom_call_target="tpu_custom_call" | custom-call | flops 3221225472 | bytes 1048576 | tf_op jit(solution)/shard_map/slab_moments/pallas_call | solution.py:173
  76.1 7.1 %slab_moments.3 = f32[3,128,512]{2,1,0:T(8,128)} custom-call(f32[128,512]{1,0:T(8,128)} %get-tuple-element.96.x_ref.xv_ref, f32[128,512]{1,0:T(8,128)} %pad_maximum_fusion.2.xs_ref, f32[32,512]{1,0:T(8,128)} %get-tuple-element.99.yv_ref, f32[32,512]{1,0:T(8,128)} %get-tuple-element.49.ys_ref, bf16[128,32,128]{2,1,0:T(8,128)(2,1)} %get-tuple-element.48), custom_call_target="tpu_custom_call" | custom-call | flops 3221225472 | bytes 1048576 | tf_op jit(solution)/shard_map/slab_moments/pallas_call | solution.py:173
  83.2 1.3 add_multiply_fusion.1
  84.5 1.7 %multiply_reduce_fusion = (f32[]{:T(128)}, f32[512]{0:T(512)S(1)}, f32[512]{0:T(512)S(1)}, f32[512]{0:T(512)S(1)}) fusion(bf16[128,512]{1,0:T(8,128)(2,1)} %get-tuple-element.97.depth_ref, f32[3,128,512]{2,1,0:T(8,128)S(1)} %add_multiply_fusion.1, f32[128,128]{1,0:T(8,128)} %get-tuple-element.63, f32[128,128]{1,0:T(8,128)} %get-tuple-element.64, ...), kind=kLoop, calls=%fused_computation.112 | loop fusion | flops 981503 | bytes 1447940 | tf_op jit(solution)/shard_map/reduce_sum | solution.py:308
  87.4 1.4 collective-permute-done.2
  88.7 3.9 %fusion.46 = f32[128,64,128]{2,0,1:T(8,128)} fusion(bf16[64,32,128]{2,0,1:T(8,128)(2,1)} %bitcast.38, bf16[128,128]{1,0:T(8,128)(2,1)S(1)} %get-tuple-element.94, s32[]{:T(128)S(6)} %select_n.111), kind=kOutput, calls=%fused_computation.66 | convolution fusion | flops 67108864 | bytes 4726788 | tf_op jit(solution)/shard_map/nayz,yq->naqz/dot_general | solution.py:321
  92.7 2.7 %fusion.42 = f32[128,64,128]{2,0,1:T(8,128)} fusion(bf16[64,32,128]{2,0,1:T(8,128)(2,1)S(1)} %bitcast.199, bf16[128,128]{1,0:T(8,128)(2,1)S(1)} %get-tuple-element.94, s32[]{:T(128)S(6)} %select_n.118), kind=kOutput, calls=%fused_computation.62 | convolution fusion | flops 67108864 | bytes 4726788 | tf_op jit(solution)/shard_map/nayz,yq->naqz/dot_general | solution.py:321
  95.3 9.8 %fusion.8 = (f32[]{:T(128)}, f32[]{:T(128)}, f32[64,128,128]{2,1,0:T(8,128)}) fusion(bf16[1,64,128,128]{3,2,1,0:T(8,128)(2,1)S(1)} %copy-done.1, f32[128]{0:T(128)S(1)} %fusion.157, f32[64,128]{1,0:T(8,128)S(1)} %broadcast_add_fusion, bf16[128,128]{1,0:T(8,128)(2,1)S(1)} %get-tuple-element.94, f32[128,64,128]{2,0,1:T(8,128)} %fusion.42, ...), kind=kOutput, calls=%fused_computation.18 | convolution fusion | flops 349175808 | bytes 19472908 | tf_op jit(solution)/shard_map/naqz,zl->naql/dot_general | solution.py:325
  107.1 5.9 %fusion.11 = (f32[]{:T(128)}, f32[64,128]{1,0:T(8,128)S(1)}, f32[64,128]{1,0:T(8,128)S(1)}, f32[128,128]{1,0:T(8,128)S(1)}, f32[64]{0:T(128)S(1)}, /*index=5*/f32[128]{0:T(128)S(1)}, f32[128]{0:T(128)S(1)}) fusion(bf16[1,64,128,128]{3,2,1,0:T(8,128)(2,1)S(1)} %copy-done.1, f32[64,128,128]{2,1,0:T(8,128)} %get-tuple-element.95, f32[]{:T(128)} %bitcast.64, ...), kind=kLoop, calls=%fused_computation.21 | loop fusion | flops 17792704 | bytes 6457100 | tf_op jit(solution)/shard_map/reduce_sum | solution.py:330
  113.0 0.7 multiply_reduce_fusion.2
  114.9 0.7 multiply_reduce_fusion.1
  115.6 0.8 fusion.82
  116.3 3.9 %stack.43 = f32[6]{0:T(128)S(1)} concatenate(f32[1]{0:T(128)} %bitcast.55, f32[1]{0:T(128)} %bitcast.56, f32[1]{0:T(128)} %bitcast.57, f32[1]{0:T(128)} %bitcast.58, f32[1]{0:T(128)} %bitcast.59, f32[1]{0:T(128)} %bitcast.60), dimensions={0} | concatenate | bytes 48 | tf_op jit(solution)/shard_map/stack | solution.py:49
  120.3 2.0 %concatenate.35 = f32[394]{0:T(512)S(1)} concatenate(f32[384]{0:T(512)S(1)} %multiply_bitcast_fusion, f32[6]{0:T(128)S(1)} %broadcast_multiply_fusion.1, f32[1]{0:T(128)} %bitcast.61, f32[1]{0:T(128)} %bitcast.62, f32[1]{0:T(128)} %bitcast.63, f32[1]{0:T(128)} %bitcast.65), dimensions={0} | concatenate | bytes 3152 | tf_op jit(solution)/shard_map/concatenate | solution.py:333
  122.9 10.9 %gather_1.1 = f32[32,8,128]{2,1,0:T(8,128)} custom-call(f32[8,128]{1,0:T(8,128)} %pad_bitcast_fusion.x_ref), custom_call_target="tpu_custom_call" | custom-call | tf_op jit(solution)/shard_map/gather_1/pallas_call | solution.py:97
  133.8 0.9 copy.152
  135.0 0.8 fusion.79
  136.6 5.9 %fusion.15 = bf16[1,64,128,128]{3,2,1,0:T(8,128)(2,1)} fusion(bf16[1,64,128,128]{3,2,1,0:T(8,128)(2,1)S(1)} %copy-done.1, f32[64,128,128]{2,1,0:T(8,128)} %get-tuple-element.95, f32[]{:T(128)} %get-tuple-element.35, f32[128]{0:T(128)S(1)} %fusion.157, f32[64,128]{1,0:T(8,128)S(1)} %broadcast_add_fusion), kind=kLoop, calls=%fused_computation.27 | loop fusion | flops 12582912 | bytes 8421892 | tf_op jit(solution)/shard_map/convert_element_type | solution.py:352
  (77 shorter events, 10.0 us)
Async XLA Ops:
  0.6 2.3 %copy-start = (f32[1024]{0:T(1024)S(1)}, f32[1024]{0:T(1024)}, u32[]{:S(2)}) copy-start(f32[1024]{0:T(1024)} %param.10) | copy-start | bytes 12292
  26.7 6.5 %copy-start.9 = (f32[4]{0:T(128)S(1)}, f32[4]{0:T(128)}, u32[]{:S(2)}) copy-start(f32[4]{0:T(128)} %constant.165.clone) | copy-start | bytes 52
  26.8 26.7 %collective-permute-start = (bf16[1,64,32,128]{3,2,1,0:T(8,128)(2,1)}, bf16[1,64,32,128]{3,2,1,0:T(8,128)(2,1)}, u32[]{:S(2)}, u32[]{:S(2)}) collective-permute-start(bf16[1,64,32,128]{3,2,1,0:T(8,128)(2,1)} %fusion.31), channel_id=1, source_target_pairs={{0,4},{4,0},{1,5},{5,1},{2,6},{6,2},{3,7},{7,3},{8,12},{12,8},{9,1... | collective-permute-start | bytes 1572872 | tf_op jit(solution)/shard_map/ppermute | solution.py:246
  29.1 22.8 %collective-permute-start.1 = (bf16[1,64,32,128]{3,2,1,0:T(8,128)(2,1)}, bf16[1,64,32,128]{3,2,1,0:T(8,128)(2,1)}, u32[]{:S(2)}, u32[]{:S(2)}) collective-permute-start(bf16[1,64,32,128]{3,2,1,0:T(8,128)(2,1)} %fusion.33), channel_id=1, source_target_pairs={{0,4},{4,0},{1,5},{5,1},{2,6},{6,2},{3,7},{7,3},{8,12},{12,8},{9,1... | collective-permute-start | bytes 1572872 | tf_op jit(solution)/shard_map/ppermute | solution.py:246
  40.2 7.9 %copy-start.3 = (bf16[64,32,128]{2,1,0:T(8,128)(2,1)S(1)}, bf16[64,32,128]{2,1,0:T(8,128)(2,1)}, u32[]{:S(2)}) copy-start(bf16[64,32,128]{2,1,0:T(8,128)(2,1)} %fusion.32) | copy-start | bytes 1572868
  40.2 8.4 %copy-start.5 = (f32[64,512]{1,0:T(8,128)S(1)}, f32[64,512]{1,0:T(8,128)}, u32[]{:S(2)}) copy-start(f32[64,512]{1,0:T(8,128)} %pad_maximum_fusion.3.y_ref) | copy-start | bytes 393220
  48.1 6.9 %copy-start.2 = (f32[128,64,128]{2,1,0:T(8,128)S(1)}, f32[128,64,128]{2,1,0:T(8,128)}, u32[]{:S(2)}) copy-start(f32[128,64,128]{2,1,0:T(8,128)} %slab_potential.1) | copy-start | bytes 12582916
  64.4 28.2 %collective-permute-start.3 = (bf16[1,64,32,128]{3,1,2,0:T(8,128)(2,1)}, bf16[1,64,32,128]{3,1,2,0:T(8,128)(2,1)S(1)}, u32[]{:S(2)}, u32[]{:S(2)}) collective-permute-start(bf16[1,64,32,128]{3,1,2,0:T(8,128)(2,1)} %fusion.34), channel_id=1, source_target_pairs={{0,4},{4,0},{1,5},{5,1},{2,6},{6,2},{3,7},{7,3},{8,12},{12,8},{9,1... | collective-permute-start | bytes 1572872 | tf_op jit(solution)/shard_map/ppermute | solution.py:246
  65.8 22.9 %collective-permute-start.2 = (bf16[1,64,32,128]{3,1,2,0:T(8,128)(2,1)}, bf16[1,64,32,128]{3,1,2,0:T(8,128)(2,1)}, u32[]{:S(2)}, u32[]{:S(2)}) collective-permute-start(bf16[1,64,32,128]{3,1,2,0:T(8,128)(2,1)} %fusion.35), channel_id=1, source_target_pairs={{0,4},{4,0},{1,5},{5,1},{2,6},{6,2},{3,7},{7,3},{8,12},{12,8},{9,1... | collective-permute-start | bytes 1572872 | tf_op jit(solution)/shard_map/ppermute | solution.py:246
  76.1 7.1 %copy-start.4 = (f32[3,128,512]{2,1,0:T(8,128)S(1)}, f32[3,128,512]{2,1,0:T(8,128)}, u32[]{:S(2)}) copy-start(f32[3,128,512]{2,1,0:T(8,128)} %slab_moments.2) | copy-start | bytes 2359300
  76.1 8.4 %copy-start.6 = (f32[128,128]{1,0:T(8,128)S(1)}, f32[128,128]{1,0:T(8,128)}, u32[]{:S(2)}) copy-start(f32[128,128]{1,0:T(8,128)} %get-tuple-element.62) | copy-start | bytes 196612
  88.7 6.6 %copy-start.1 = (bf16[1,64,128,128]{3,2,1,0:T(8,128)(2,1)S(1)}, bf16[1,64,128,128]{3,2,1,0:T(8,128)(2,1)}, u32[]{:S(2)}) copy-start(bf16[1,64,128,128]{3,2,1,0:T(8,128)(2,1)} %param.7) | copy-start | bytes 6291460
  105.1 10.4 %copy-start.7 = (f32[64]{0:T(128)S(1)}, f32[64]{0:T(128)}, u32[]{:S(2)}) copy-start(f32[64]{0:T(128)} %broadcast_multiply_fusion.3) | copy-start | bytes 772
  105.1 29.7 %copy-start.10 = (s32[16]{0:T(128)S(1)}, s32[16]{0:T(128)}, u32[]{:S(2)}) copy-start(s32[16]{0:T(128)} %fusion.155) | copy-start | bytes 196
  105.1 29.8 %copy-start.8 = (s32[16]{0:T(128)S(1)}, s32[16]{0:T(128)}, u32[]{:S(2)}) copy-start(s32[16]{0:T(128)} %param.11) | copy-start | bytes 196

commit v4 on v3

--- a/solution.py
+++ b/solution.py
@@ -34,19 +34,6 @@
         values.append(gauss_value)
         slopes.append(2.0 * exponent * offset * gauss_value)
     return (jnp.concatenate(values, axis=1), jnp.concatenate(slopes, axis=1))
-
-
-def stress_terms(weighted, x_wave, y_wave):
-    over_z = jnp.sum(weighted, axis=2)
-    over_y = jnp.sum(weighted, axis=1)
-    over_x = jnp.sum(weighted, axis=0)
-    stress_xx = jnp.sum(x_wave * x_wave * jnp.sum(over_z, axis=1))
-    stress_yy = jnp.sum(y_wave * y_wave * jnp.sum(over_z, axis=0))
-    stress_zz = jnp.sum(y_wave * y_wave * jnp.sum(over_y, axis=0))
-    stress_xy = jnp.sum(x_wave[:, None] * y_wave[None, :] * over_z)
-    stress_xz = jnp.sum(x_wave[:, None] * y_wave[None, :] * over_y)
-    stress_yz = jnp.sum(y_wave[:, None] * y_wave[None, :] * over_x)
-    return jnp.stack([stress_xx, stress_yy, stress_zz, stress_xy, stress_xz, stress_yz])
 
 
 def peer_coords(index, sizes):
@@ -189,6 +176,179 @@
         ),
         name="slab_moments",
     )(x_value, x_slope, y_value, y_slope, real_space)
+
+
+def tail_kernel(
+    sizes, base, back_ref, coeff_ref, table_ref, weight_ref, head_ref,
+    waves_ref, out_ref, image_ref, sums_ref, tile_ref, send_sem, recv_sem,
+):
+    band_size, gvec_size, dom_size = sizes
+    total = band_size * gvec_size * dom_size
+    band_id, gvec_id, dom_id = lax.axis_index("band"), lax.axis_index("gvec"), lax.axis_index("dom")
+    me = (band_id * gvec_size + gvec_id) * dom_size + dom_id
+    local_bands, x_local, extent, _ = coeff_ref.shape
+    barrier = pltpu.get_barrier_semaphore()
+
+    def peer_of(step):
+        outer = step // gvec_size
+        return (
+            lax.rem(band_id + outer // dom_size, band_size),
+            lax.rem(gvec_id + step % gvec_size, gvec_size),
+            lax.rem(dom_id + outer % dom_size, dom_size),
+        )
+
+    def greet(step, carry):
+        pl.semaphore_signal(
+            barrier, inc=1, device_id=peer_of(step), device_id_type=pl.DeviceIdType.MESH
+        )
+        return carry
+
+    lax.fori_loop(1, total, greet, 0)
+
+    def copy_of(step):
+        return pltpu.make_async_remote_copy(
+            src_ref=tile_ref,
+            dst_ref=out_ref.at[me],
+            send_sem=send_sem.at[step],
+            recv_sem=recv_sem.at[step],
+            device_id=peer_of(step),
+            device_id_type=pl.DeviceIdType.MESH,
+        )
+
+    def send(step, carry):
+        copy_of(step).start()
+        return carry
+
+    def finish(step, carry):
+        copy_of(step).wait()
+        return carry
+
+    rows = 4
+    block = (rows, extent, extent)
+    wave_step = jnp.pi / extent
+    q_wave = lax.broadcasted_iota(jnp.int32, block[1:], 0).astype(jnp.float32) * wave_step
+    l_wave = lax.broadcasted_iota(jnp.int32, block[1:], 1).astype(jnp.float32) * wave_step
+    plane_kinetic = 0.5 * (q_wave * q_wave + l_wave * l_wave)
+
+    def x_waves(index):
+        first = gvec_id * x_local + index * rows
+        at = lax.broadcasted_iota(jnp.int32, block, 0) + first
+        return at.astype(jnp.float32) * wave_step
+
+    def total_of(value):
+        return jnp.sum(jnp.sum(value, axis=0, keepdims=True), axis=1, keepdims=True)
+
+    spots = (
+        lax.broadcasted_iota(jnp.int32, head_ref.shape, 0) * 128
+        + lax.broadcasted_iota(jnp.int32, head_ref.shape, 1)
+    )
+    tile = head_ref[...]
+    stress = [0.0] * 6
+    for band in range(local_bands):
+        sums_ref[...] = jnp.zeros_like(sums_ref)
+
+        def first_pass(index, carry):
+            window = pl.ds(index * rows, rows)
+            wide = coeff_ref[band, window].astype(jnp.float32)
+            field = jnp.dot(
+                back_ref[band, window].reshape(rows * extent, extent),
+                table_ref[...],
+                preferred_element_type=jnp.float32,
+            ).reshape(block)
+            x_wave = x_waves(index)
+            image = (0.5 * x_wave * x_wave + plane_kinetic[None]) * wide + field
+            image_ref[band, window] = image
+            square = wide * wide
+            by_x = square * x_wave
+            sums_ref[0] += jnp.sum(square, axis=0)
+            sums_ref[1] += jnp.sum(by_x, axis=0)
+            sums_ref[2] += jnp.sum(by_x * x_wave, axis=0)
+            sums_ref[3] += jnp.sum(wide * image, axis=0)
+            return carry
+
+        lax.fori_loop(0, x_local // rows, first_pass, 0)
+        norm = total_of(sums_ref[0])
+        inner = total_of(sums_ref[3])
+        filled = norm > 0.0
+        energy = jnp.where(filled, inner / jnp.where(filled, norm, 1.0), 0.0)
+        weight = weight_ref[0:1, band : band + 1]
+        terms = (
+            sums_ref[2],
+            sums_ref[0] * q_wave * q_wave,
+            sums_ref[0] * l_wave * l_wave,
+            sums_ref[1] * q_wave,
+            sums_ref[1] * l_wave,
+            sums_ref[0] * q_wave * l_wave,
+        )
+        stress = [old + weight * total_of(term) for old, term in zip(stress, terms)]
+        sums_ref[1] = jnp.zeros_like(sums_ref[1])
+
+        def second_pass(index, carry):
+            window = pl.ds(index * rows, rows)
+            wide = coeff_ref[band, window].astype(jnp.float32)
+            residual = image_ref[band, window] - energy[None] * wide
+            sums_ref[1] += jnp.sum(residual * residual, axis=0)
+            return carry
+
+        lax.fori_loop(0, x_local // rows, second_pass, 0)
+        square = total_of(sums_ref[1])
+        for shift, value in enumerate((norm, inner, square)):
+            tile = jnp.where(spots == base + 7 + shift * local_bands + band, value, tile)
+    for shift, value in enumerate(stress):
+        tile = jnp.where(spots == base + shift, value / float(extent**3), tile)
+    tile_ref[...] = tile
+    out_ref[me] = tile
+    pl.semaphore_wait(barrier, total - 1)
+    lax.fori_loop(1, total, send, 0)
+    lax.fori_loop(1, gvec_size, finish, 0)
+
+    both = tile
+    for step in range(1, gvec_size):
+        other = lax.rem(gvec_id + step, gvec_size)
+        both = both + out_ref[(band_id * gvec_size + other) * dom_size + dom_id]
+    for band in range(local_bands):
+        norm = total_of(jnp.where(spots == base + 7 + band, both, 0.0))
+        inner = total_of(jnp.where(spots == base + 7 + local_bands + band, both, 0.0))
+        energy = inner / norm
+
+        def last_pass(index, carry):
+            window = pl.ds(index * rows, rows)
+            wide = coeff_ref[band, window].astype(jnp.float32)
+            x_wave = x_waves(index)
+            kinetic = 0.5 * x_wave * x_wave + plane_kinetic[None]
+            residual = image_ref[band, window] - energy[None] * wide
+            updated = wide - step_size * residual / (1.0 + kinetic)
+            waves_ref[band, window] = updated.astype(jnp.bfloat16)
+            return carry
+
+        lax.fori_loop(0, x_local // rows, last_pass, 0)
+    lax.fori_loop(gvec_size, total, finish, 0)
+
+
+def tail(back_two, coeffs, cosines, weight, head, base, sizes):
+    total = sizes[0] * sizes[1] * sizes[2]
+    extent = coeffs.shape[-1]
+    vmem = pl.BlockSpec(memory_space=pltpu.VMEM)
+    return pl.pallas_call(
+        functools.partial(tail_kernel, sizes, base),
+        out_shape=(
+            jax.ShapeDtypeStruct(coeffs.shape, jnp.bfloat16),
+            jax.ShapeDtypeStruct((total,) + head.shape, jnp.float32),
+        ),
+        in_specs=[vmem] * 5,
+        out_specs=(vmem, vmem),
+        scratch_shapes=[
+            pltpu.VMEM(coeffs.shape, jnp.float32),
+            pltpu.VMEM((4, extent, extent), jnp.float32),
+            pltpu.VMEM(head.shape, jnp.float32),
+            pltpu.SemaphoreType.DMA((total,)),
+            pltpu.SemaphoreType.DMA((total,)),
+        ],
+        compiler_params=pltpu.CompilerParams(
+            collective_id=1, has_side_effects=True, vmem_limit_bytes=40 * 1024 * 1024
+        ),
+        name="tail",
+    )(back_two, coeffs, cosines, weight, head)
 
 
 def per_device(sizes, coeffs, v_local, atom_pos, atom_charge, near_list, live_count):
@@ -280,9 +440,7 @@
 
         sent = [back_x(step) for step in range(1, gvec_size)]
         if part == chunks - 1:
-            sent, held_coeffs, reals = lax.optimization_barrier(
-                (sent, coeffs, reals + [real_space])
-            )
+            sent, reals = lax.optimization_barrier((sent, reals + [real_space]))
         else:
             reals.append(real_space)
         returned.append(
@@ -294,17 +452,6 @@
             moments = moments + weight[band] * slab_moments(
                 x_value, x_slope, y_value[window], y_slope[window], reals[part][band]
             )
-    coeff_wide = held_coeffs.astype(jnp.float32)
-    wave_step = jnp.pi / extent
-    x_wave = (gvec_id * x_local + jnp.arange(x_local)).astype(jnp.float32) * wave_step
-    y_wave = jnp.arange(extent).astype(jnp.float32) * wave_step
-    kinetic = 0.5 * (
-        x_wave[:, None, None] ** 2 + y_wave[None, :, None] ** 2 + y_wave[None, None, :] ** 2
-    )
-    norm_part = jnp.sum(coeff_wide * coeff_wide, axis=(1, 2, 3))
-    weighted = jnp.sum(weight[:, None, None, None] * coeff_wide * coeff_wide, axis=0)
-    stress_local = stress_terms(weighted, x_wave, y_wave) / cell_count
-
     embedding = jnp.sum(moments[0] * depth.astype(jnp.float32)) / cell_count
     force_terms = jnp.stack(
         [
@@ -322,17 +469,13 @@
         for part in range(chunks)
         for step, block in zip(steps, returned[part])
     ).astype(jnp.bfloat16)
-    wave_field = jnp.einsum("naqz,zl->naql", back_two, cosines, preferred_element_type=jnp.float32)
-    image = kinetic[None] * coeff_wide + wave_field
-    inner_part = jnp.sum(coeff_wide * image, axis=(1, 2, 3))
-    own_energy = jnp.where(norm_part > 0.0, inner_part / jnp.where(norm_part > 0.0, norm_part, 1.0), 0.0)
-    own_residual = image - own_energy[:, None, None, None] * coeff_wide
-    resid_part = jnp.sum(own_residual * own_residual, axis=(1, 2, 3))
-    local_totals = jnp.concatenate([stress_local, embedding[None]])
     mine = (jnp.arange(band_total)[None, :] == band_ids[:, None]).astype(jnp.float32)
-    flat = jnp.concatenate([forces.reshape(-1), local_totals, norm_part, inner_part, resid_part])
-    flat = jnp.pad(flat, (0, -flat.shape[0] % 1024)).reshape(-1, 128)
-    parts = gather_all(flat, sizes, 1).reshape(devices, -1)
+    flat = jnp.concatenate([forces.reshape(-1), jnp.zeros((6,), jnp.float32), embedding[None]])
+    tail_length = flat.shape[0] + 3 * local_bands
+    flat = jnp.pad(flat, (0, 3 * local_bands + -tail_length % 1024)).reshape(-1, 128)
+    weight_row = jnp.pad(weight, (0, -local_bands % 128))[None, :]
+    waves_new, parts = tail(back_two, coeffs, cosines, weight_row, flat, 3 * live_total, sizes)
+    parts = parts.reshape(devices, -1)
     lines = 3 * live_total + 7
     summed = jnp.sum(parts[:, :lines], axis=0)
     force_all = summed[: 3 * live_total].reshape(3, live_total)
@@ -348,8 +491,6 @@
     energy_all = energy_all.reshape(-1)
     energies = jnp.sum(mine * energy_all[None, :], axis=1)
     resid_ratio = jnp.sum(mine * ratio_all[None, :], axis=1)
-    residual = image - energies[:, None, None, None] * coeff_wide
-    waves_new = (coeff_wide - step_size * residual / (1.0 + kinetic[None])).astype(jnp.bfloat16)
     band_energy = jnp.sum(occupancy(jnp.arange(band_total), band_total) * energy_all) / band_total
     totals = jnp.concatenate([summed[3 * live_total : 3 * live_total + 7], band_energy[None]])
     start = lax.dynamic_slice(order, (me * capacity,), (capacity,))

time: 146 us -> 112 us (0.77)
  other arithmetic: 36.9 us -> 18.6 us
  matrix products: 36.4 us -> 23 us
  local copies, waits for them, and re-layouts: 12.4 us -> 8.13 us
  waiting for transfers between devices: 3.97 us -> 6.7 us
  between operations: 4.91 us -> 3.05 us
    pallas_call x0 -> x1, Pallas kernels: none -> 12.4 us  [tail(): pl.pallas_call(functools.partial(tail_kernel, sizes, base), out_shape=(ja...]
    pallas_call x2 -> x1, Pallas kernels: 24.2 us -> 13.3 us  [gather_all(): pl.pallas_call(functools.partial(gather_kernel, sizes), out_shape=jax.Sha...]
    reduce_sum x7 -> x1, other arithmetic: 10.9 us -> 0.72 us  [per_device(): jnp.sum(moments[1] * z_value, axis=0)]
    dot_general x1 -> x0, matrix products: 9.78 us -> none  [per_device(): jnp.einsum('naqz,zl->naql', back_two, cosines, preferred_element_type=jnp...]
    convert_element_type x1 -> x0, other arithmetic: 5.86 us -> none  [per_device(): (coeff_wide - step_size * residual / (1.0 + kinetic[None])).astype(jnp.bf...]
    another operation x2, local copies, waits for them, and re-layouts: 4.06 us -> 0.12 us  [the longest x1 3.94 us: stress_terms(): jnp.stack([stress_xx, stress_yy, stress_zz, stress_xy, stress_xz, stress_...]
    ppermute x4, waiting for transfers between devices: 3.97 us -> 6.7 us  [shift(): lax.ppermute(value, 'gvec', [(at, (at + step) % gvec_size) for at in rang...]
    unnamed x27 -> x32, local copies, waits for them, and re-layouts: 2.31 us -> 4.59 us
  transfers between devices with their start and end apart: 4 -> 4, of which waited for: 2 -> 1; matrix products, arithmetic and copies ran while one was open for 17% -> 16% of each run, Pallas kernels for 15% -> 20%
where the time goes in v4:
time: 112 us; the launch traced here: 111 us
  Pallas kernels  47.5 us (42%)
  matrix products  23 us (21%)
  other arithmetic  18.6 us (17%)
  local copies, waits for them, and re-layouts  8.13 us (7%)
  waiting for transfers between devices  6.7 us (6%)
  starting transfers between devices  4.11 us (4%)
  between operations  3.05 us (3%)
    pallas_call x2, Pallas kernels, slab_moments(): pl.pallas_call(force_kernel, grid=(x_total // rows,), out_shape=jax.Shape...  14 us
    pallas_call x1, Pallas kernels, gather_all(): pl.pallas_call(functools.partial(gather_kernel, sizes), out_shape=jax.Sha...  13.3 us
    pallas_call x1, Pallas kernels, tail(): pl.pallas_call(functools.partial(tail_kernel, sizes, base), out_shape=(ja...  12.4 us
    dot_general x4, matrix products, per_device(): jnp.einsum('nayz,yq->naqz', block, y_rows(step, part), preferred_element_...  9.74 us
    pallas_call x1, Pallas kernels, slab_potential(): pl.pallas_call(potential_kernel, grid=(x_total // rows,), out_shape=jax.S...  7.83 us
    ppermute x4, waiting for transfers between devices, shift(): lax.ppermute(value, 'gvec', [(at, (at + step) % gvec_size) for at in rang...  6.7 us
    convert_element_type x1, other arithmetic, per_device(): (field_total[None, :, window] * real_space.astype(jnp.float32)).astype(jn...  6.38 us
    unnamed x32, local copies, waits for them, and re-layouts  4.59 us
  transfers between devices with their start and end apart: 4, of which 1 were waited for; matrix products, arithmetic and copies ran while one was open for 16% of the time, Pallas kernels for 20%

profile of v4, /device:TPU:0, one launch (start us, length us, event | category | flops | bytes accessed | tf_op | source)
XLA Modules:
  0.0 111.1 jit_solution(2819963752244273305)
XLA Ops:
  1.3 0.7 compare_select_fusion.2
  2.0 0.9 copy.55
  3.0 0.6 gather_fusion.1
  3.6 0.6 gather_fusion
  4.2 0.7 fusion.131
  4.9 0.6 select_maximum_fusion.2.x_ref
  5.5 13.3 %gather_0.1 = f32[32,8,128]{2,1,0:T(8,128)} custom-call(f32[8,128]{1,0:T(8,128)} %select_maximum_fusion.2.x_ref), custom_call_target="tpu_custom_call" | custom-call | tf_op jit(solution)/shard_map/gather_0/pallas_call | solution.py:84
  18.8 0.9 slice_bitcast_fusion.3
  21.1 2.6 %fusion.7 = bf16[64,128,128]{2,1,0:T(8,128)(2,1)S(1)} fusion(bf16[1,64,128,128]{3,2,1,0:T(8,128)(2,1)} %coeff_ref, f32[128]{0:T(128)S(1)} %compare_select_fusion.4, f32[128]{0:T(128)S(1)} %iota_convert_fusion, f32[128]{0:T(128)S(1)} %add_multiply_fusion.1), kind=kOutput, calls=%fused_computation.14 | convolution fusion | flops 269549568 | bytes 4195840 | tf_op jit(solution)/shard_map/naql,zl->naqz/dot_general | solution.py:410
  23.6 1.3 %fusion.57 = (f32[128,128]{1,0:T(8,128)}, f32[128,128]{1,0:T(8,128)}, f32[128,128]{1,0:T(8,128)}, f32[128,128]{1,0:T(8,128)}, f32[128,128]{1,0:T(8,128)S(1)}, /*...) fusion(f32[128]{0:T(128)S(1)} %get-tuple-element.45, ...), kind=kLoop, calls=%fused_computation.119 | loop fusion | flops 622592 | bytes 1083904 | tf_op jit(solution)/shard_map/mul | solution.py:35
  24.9 1.2 %fusion.11 = bf16[1,64,32,128]{3,2,1,0:T(8,128)(2,1)} fusion(bf16[64,128,128]{2,1,0:T(8,128)(2,1)S(1)} %fusion.7, bf16[128,128]{1,0:T(8,128)(2,1)S(1)} %get-tuple-element.83.table_ref, s32[]{:T(128)S(6)} %select_n.104), kind=kOutput, calls=%fused_computation.24 | convolution fusion | flops 67371008 | bytes 2629636 | tf_op jit(solution)/shard_map/naqz,yq->nayz/dot_general | solution.py:415
  26.1 1.1 %collective-permute-start = (bf16[1,64,32,128]{3,2,1,0:T(8,128)(2,1)}, bf16[1,64,32,128]{3,2,1,0:T(8,128)(2,1)}, u32[]{:S(2)}, u32[]{:S(2)}) collective-permute-start(bf16[1,64,32,128]{3,2,1,0:T(8,128)(2,1)} %fusion.11), channel_id=1, source_target_pairs={{0,4},{4,0},{1,5},{5,1},{2,6},{6,2},{3,7},{7,3},{8,12},{12,8},{9,1... | collective-permute-start | bytes 1572872 | tf_op jit(solution)/shard_map/ppermute | solution.py:406
  27.3 1.2 %fusion.13 = bf16[1,64,32,128]{3,2,1,0:T(8,128)(2,1)} fusion(bf16[64,128,128]{2,1,0:T(8,128)(2,1)S(1)} %fusion.7, bf16[128,128]{1,0:T(8,128)(2,1)S(1)} %get-tuple-element.83.table_ref, s32[]{:T(128)S(6)} %select_n.111), kind=kOutput, calls=%fused_computation.26 | convolution fusion | flops 67371008 | bytes 2629636 | tf_op jit(solution)/shard_map/naqz,yq->nayz/dot_general | solution.py:415
  28.5 0.9 collective-permute-start.2
  29.5 0.4 fusion.12
  30.6 0.5 fusion.36
  31.1 0.7 pad_maximum_fusion.3.y_ref
  31.8 1.7 %pad_maximum_fusion.2.xs_ref = f32[128,512]{1,0:T(8,128)} fusion(f32[128,128]{1,0:T(8,128)} %get-tuple-element.81, f32[128,128]{1,0:T(8,128)} %get-tuple-element.80, f32[128,128]{1,0:T(8,128)} %get-tuple-element.79, f32[128,128]{1,0:T(8,128)} %get-tuple-element.82), kind=kLoop, calls=%fused_computation.83 | loop fusion | flops 196608 | bytes 524288 | tf_op jit(solution)/shard_map/concatenate | solution.py:36
  33.5 1.7 %pad_maximum_fusion = (f32[128,512]{1,0:T(8,128)}, bf16[128,512]{1,0:T(8,128)(2,1)}) fusion(f32[128,128]{1,0:T(8,128)} %get-tuple-element.78, f32[128,128]{1,0:T(8,128)} %get-tuple-element.76, f32[128,128]{1,0:T(8,128)} %get-tuple-element.77, f32[128,128]{1,0:T(8,128)S(1)} %get-tuple-element.75, f32[128,128]{1,0:T(8,128)S(1)} %get-tuple-element.55, ...), kind=kLoop, calls=%fused_computation.81 | loop fusion | flops 524288 | bytes 919552 | tf_op jit(solution)/shard_map/concatenate | solution.py:36
  35.2 7.8 %slab_potential.1 = f32[128,64,128]{2,1,0:T(8,128)} custom-call(f32[128,512]{1,0:T(8,128)} %get-tuple-element.84.x_ref.xv_ref, f32[64,512]{1,0:T(8,128)} %pad_maximum_fusion.3.y_ref, bf16[128,512]{1,0:T(8,128)(2,1)} %get-tuple-element.85.depth_ref, bf16[128,64,128]{2,1,0:T(8,128)(2,1)} %local_ref.1), custom_call_target="tpu_custom_call" | custom-call | flops 4294967296 | bytes 6291456 | tf_op jit(solution)/shard_map/slab_potential/pallas_call | solution.py:119
  43.0 0.5 fusion.28
  43.5 0.4 copy-done.5
  43.9 0.7 fusion.137
  44.6 6.7 %collective-permute-done.2 = bf16[1,64,32,128]{3,2,1,0:T(8,128)(2,1)} collective-permute-done((bf16[1,64,32,128]{3,2,1,0:T(8,128)(2,1)}, bf16[1,64,32,128]{3,2,1,0:T(8,128)(2,1)}, u32[]{:S(2)}, u32[]{:S(2)}) %collective-permute-start.2) | collective-permute-done | bytes 524320 | tf_op jit(solution)/shard_map/ppermute | solution.py:406
  51.3 1.7 %fusion.26 = f32[128,32,128]{2,0,1:T(8,128)S(1)} fusion(bf16[64,32,128]{2,1,0:T(8,128)(2,1)} %bitcast.36, bf16[128,128]{1,0:T(8,128)(2,1)S(1)} %get-tuple-element.83.table_ref, s32[]{:T(128)S(6)} %select_n.104), kind=kOutput, calls=%fused_computation.38 | convolution fusion | flops 67108864 | bytes 2654212 | tf_op jit(solution)/shard_map/nayz,xa->nxyz/dot_general | solution.py:431
  53.0 1.5 %fusion.34 = f32[128,32,128]{2,0,1:T(8,128)S(1)} fusion(bf16[64,32,128]{2,1,0:T(8,128)(2,1)} %bitcast.22, bf16[128,128]{1,0:T(8,128)(2,1)S(1)} %get-tuple-element.83.table_ref, s32[]{:T(128)S(6)} %select_n.104), kind=kOutput, calls=%fused_computation.46 | convolution fusion | flops 67108864 | bytes 2654212 | tf_op jit(solution)/shard_map/nayz,xa->nxyz/dot_general | solution.py:431
  54.5 6.4 %fusion.2 = (bf16[128,32,128]{2,1,0:T(8,128)(2,1)S(1)}, bf16[128,32,128]{2,1,0:T(8,128)(2,1)}, bf16[128,32,128]{2,1,0:T(8,128)(2,1)S(1)}, bf16[128,32,128]{2,1,0:T(8,128)(2,1)}) fusion(f32[128,64,128]{2,1,0:T(8,128)S(1)} %copy-done.3, f32[128,32,128]{2,0,1:T(8,128)S(1)} %fusion.34, f32[128,32,128]{2,0,1:T(8,128)S(1)} %fusion.36, ...), kind=kLoop, calls=%fused_computation.7 | loop fusion | flops 5242880 | bytes 16777216 | tf_op jit(solution)/shard_map/convert_element_type | solution.py:434
  60.9 0.5 convolution_convert_fusion.2
  61.4 0.5 fusion.14
  61.9 0.5 convolution_convert_fusion
  62.5 0.5 fusion.15
  63.0 1.5 %collective-permute-start.3 = (bf16[1,64,32,128]{3,1,2,0:T(8,128)(2,1)S(1)}, bf16[1,64,32,128]{3,1,2,0:T(8,128)(2,1)S(1)}, u32[]{:S(2)}, u32[]{:S(2)}) collective-permute-start(bf16[1,64,32,128]{3,1,2,0:T(8,128)(2,1)S(1)} %fusion.15), channel_id=1, source_target_pairs={{0,4},{4,0},{1,5},{5,1},{2,6},{6,2},{3,7},{7,3},{8,12},{12,8},{9,1... | collective-permute-start | bytes 1572872 | tf_op jit(solution)/shard_map/ppermute | solution.py:406
  64.5 0.6 collective-permute-start.1
  65.1 2.7 %fusion.20 = f32[128,64,128]{2,0,1:T(8,128)} fusion(bf16[64,32,128]{2,0,1:T(8,128)(2,1)S(1)} %convolution_convert_fusion, bf16[128,128]{1,0:T(8,128)(2,1)S(1)} %get-tuple-element.83.table_ref, s32[]{:T(128)S(6)} %select_n.112), kind=kOutput, calls=%fused_computation.34 | convolution fusion | flops 67108864 | bytes 4726788 | tf_op jit(solution)/shard_map/nayz,yq->naqz/dot_general | solution.py:468
  67.8 2.7 %fusion.30 = f32[128,64,128]{2,0,1:T(8,128)} fusion(bf16[64,32,128]{2,0,1:T(8,128)(2,1)S(1)} %convolution_convert_fusion.2, bf16[128,128]{1,0:T(8,128)(2,1)S(1)} %get-tuple-element.83.table_ref, s32[]{:T(128)S(6)} %select_n.110), kind=kOutput, calls=%fused_computation.42 | convolution fusion | flops 67108864 | bytes 4726788 | tf_op jit(solution)/shard_map/nayz,yq->naqz/dot_general | solution.py:468
  70.5 7.0 %slab_moments.2 = f32[3,128,512]{2,1,0:T(8,128)} custom-call(f32[128,512]{1,0:T(8,128)} %get-tuple-element.84.x_ref.xv_ref, f32[128,512]{1,0:T(8,128)} %pad_maximum_fusion.2.xs_ref, f32[32,512]{1,0:T(8,128)} %get-tuple-element.86.yv_ref, f32[32,512]{1,0:T(8,128)} %get-tuple-element.39.ys_ref, bf16[128,32,128]{2,1,0:T(8,128)(2,1)} %get-tuple-element.29), custom_call_target="tpu_custom_call" | custom-call | flops 3221225472 | bytes 1048576 | tf_op jit(solution)/shard_map/slab_moments/pallas_call | solution.py:160
  77.4 7.0 %slab_moments.3 = f32[3,128,512]{2,1,0:T(8,128)} custom-call(f32[128,512]{1,0:T(8,128)} %get-tuple-element.84.x_ref.xv_ref, f32[128,512]{1,0:T(8,128)} %pad_maximum_fusion.2.xs_ref, f32[32,512]{1,0:T(8,128)} %get-tuple-element.87.yv_ref, f32[32,512]{1,0:T(8,128)} %get-tuple-element.38.ys_ref, bf16[128,32,128]{2,1,0:T(8,128)(2,1)} %get-tuple-element.37), custom_call_target="tpu_custom_call" | custom-call | flops 3221225472 | bytes 1048576 | tf_op jit(solution)/shard_map/slab_moments/pallas_call | solution.py:160
  84.5 1.3 %add_multiply_fusion = f32[3,128,512]{2,1,0:T(8,128)S(1)} fusion(f32[3,128,512]{2,1,0:T(8,128)S(1)} %copy-done.4, f32[3,128,512]{2,1,0:T(8,128)} %slab_moments.3, f32[]{:T(128)} %div.94), kind=kLoop, calls=%fused_computation.33 | loop fusion | flops 393216 | bytes 2359300 | tf_op jit(solution)/shard_map/add | solution.py:452
  85.9 0.7 fusion.41
  87.4 0.7 fusion.32
  88.1 1.4 %copy-done.2 = f32[128,64,128]{2,0,1:T(8,128)S(1)} copy-done((f32[128,64,128]{2,0,1:T(8,128)S(1)}, f32[128,64,128]{2,0,1:T(8,128)}, u32[]{:S(2)}) %copy-start.2) | copy-done | bytes 4194328
  89.6 3.6 %fusion.back_ref = bf16[1,64,128,128]{3,2,1,0:T(8,128)(2,1)S(1)} fusion(f32[128,64,128]{2,0,1:T(8,128)S(1)} %copy-done.2, f32[128,64,128]{2,0,1:T(8,128)S(1)} %fusion.32, f32[128,64,128]{2,0,1:T(8,128)} %fusion.30, bf16[64,32,128]{2,0,1:T(8,128)(2,1)S(1)} %bitcast.173, bf16[128,128]{1,0:T(8,128)(2,1)S(1)} %get-tuple-element.83.table_ref, s32[]{:T(128)S(6)} %select_n.111), kind=kOutput, calls=%fused_computation.3 | convolution fusion | flops 71303168 | bytes 15212548 | tf_op jit(solution)/shard_map/nayz,yq->naqz/dot_general | solution.py:468
  93.2 12.4 %tail.1 = (bf16[1,64,128,128]{3,2,1,0:T(8,128)(2,1)S(1)}, f32[32,8,128]{2,1,0:T(8,128)S(1)}) custom-call(bf16[1,64,128,128]{3,2,1,0:T(8,128)(2,1)S(1)} %fusion.back_ref, bf16[1,64,128,128]{3,2,1,0:T(8,128)(2,1)S(1)} %copy-done.1, bf16[128,128]{1,0:T(8,128)(2,1)S(1)} %get-tuple-element.83.table_ref, f32[1,128]{1,0:T(1,128)S(1)} %pad_bitcast_fusion.weight_ref, ...), custom_call_target="tpu_custom_call" | custom-call | tf_op jit(solution)/shard_map/tail/pallas_call | solution.py:332
  105.9 0.8 fusion.61
  107.3 0.6 fusion.114
  107.9 0.6 select_reduce_fusion
  109.2 0.6 pad_maximum_fusion.5
  109.8 1.3 %copy.154 = bf16[1,64,128,128]{3,2,1,0:T(8,128)(2,1)} copy(bf16[1,64,128,128]{3,2,1,0:T(8,128)(2,1)S(1)} %get-tuple-element.93) | data formatting | bytes 4194304
  (69 shorter events, 3.1 us)
Async XLA Ops:
  0.6 2.3 %copy-start = (f32[1024]{0:T(1024)S(1)}, f32[1024]{0:T(1024)}, u32[]{:S(2)}) copy-start(f32[1024]{0:T(1024)} %param.10) | copy-start | bytes 12292
  26.1 26.8 %collective-permute-start = (bf16[1,64,32,128]{3,2,1,0:T(8,128)(2,1)}, bf16[1,64,32,128]{3,2,1,0:T(8,128)(2,1)}, u32[]{:S(2)}, u32[]{:S(2)}) collective-permute-start(bf16[1,64,32,128]{3,2,1,0:T(8,128)(2,1)} %fusion.11), channel_id=1, source_target_pairs={{0,4},{4,0},{1,5},{5,1},{2,6},{6,2},{3,7},{7,3},{8,12},{12,8},{9,1... | collective-permute-start | bytes 1572872 | tf_op jit(solution)/shard_map/ppermute | solution.py:406
  28.5 22.8 %collective-permute-start.2 = (bf16[1,64,32,128]{3,2,1,0:T(8,128)(2,1)}, bf16[1,64,32,128]{3,2,1,0:T(8,128)(2,1)}, u32[]{:S(2)}, u32[]{:S(2)}) collective-permute-start(bf16[1,64,32,128]{3,2,1,0:T(8,128)(2,1)} %fusion.13), channel_id=1, source_target_pairs={{0,4},{4,0},{1,5},{5,1},{2,6},{6,2},{3,7},{7,3},{8,12},{12,8},{9,1... | collective-permute-start | bytes 1572872 | tf_op jit(solution)/shard_map/ppermute | solution.py:406
  29.5 0.8 copy-start.12
  43.0 0.9 copy-start.5
  51.3 3.2 %copy-start.3 = (f32[128,64,128]{2,1,0:T(8,128)S(1)}, f32[128,64,128]{2,1,0:T(8,128)}, u32[]{:S(2)}) copy-start(f32[128,64,128]{2,1,0:T(8,128)} %slab_potential.1) | copy-start | bytes 12582916
  63.0 25.1 %collective-permute-start.3 = (bf16[1,64,32,128]{3,1,2,0:T(8,128)(2,1)S(1)}, bf16[1,64,32,128]{3,1,2,0:T(8,128)(2,1)S(1)}, u32[]{:S(2)}, u32[]{:S(2)}) collective-permute-start(bf16[1,64,32,128]{3,1,2,0:T(8,128)(2,1)S(1)} %fusion.15), channel_id=1, source_target_pairs={{0,4},{4,0},{1,5},{5,1},{2,6},{6,2},{3,7},{7,3},{8,12},{12,8},{9,1... | collective-permute-start | bytes 1572872 | tf_op jit(solution)/shard_map/ppermute | solution.py:406
  64.5 22.9 %collective-permute-start.1 = (bf16[1,64,32,128]{3,1,2,0:T(8,128)(2,1)S(1)}, bf16[1,64,32,128]{3,1,2,0:T(8,128)(2,1)S(1)}, u32[]{:S(2)}, u32[]{:S(2)}) collective-permute-start(bf16[1,64,32,128]{3,1,2,0:T(8,128)(2,1)S(1)} %fusion.14), channel_id=1, source_target_pairs={{0,4},{4,0},{1,5},{5,1},{2,6},{6,2},{3,7},{7,3},{8,12},{12,8},{9,1... | collective-permute-start | bytes 1572872 | tf_op jit(solution)/shard_map/ppermute | solution.py:406
  77.4 7.0 %copy-start.4 = (f32[3,128,512]{2,1,0:T(8,128)S(1)}, f32[3,128,512]{2,1,0:T(8,128)}, u32[]{:S(2)}) copy-start(f32[3,128,512]{2,1,0:T(8,128)} %slab_moments.2) | copy-start | bytes 2359300
  84.4 1.4 %copy-start.6 = (bf16[128,512]{1,0:T(8,128)(2,1)S(1)}, bf16[128,512]{1,0:T(8,128)(2,1)}, u32[]{:S(2)}) copy-start(bf16[128,512]{1,0:T(8,128)(2,1)} %get-tuple-element.85.depth_ref) | copy-start | bytes 393220
  84.4 1.4 %copy-start.7 = (f32[128,128]{1,0:T(8,128)S(1)}, f32[128,128]{1,0:T(8,128)}, u32[]{:S(2)}) copy-start(f32[128,128]{1,0:T(8,128)} %get-tuple-element.51) | copy-start | bytes 196612
  84.5 1.4 %copy-start.8 = (f32[128,128]{1,0:T(8,128)S(1)}, f32[128,128]{1,0:T(8,128)}, u32[]{:S(2)}) copy-start(f32[128,128]{1,0:T(8,128)} %get-tuple-element.52) | copy-start | bytes 196612
  84.5 1.4 %copy-start.9 = (f32[128,128]{1,0:T(8,128)S(1)}, f32[128,128]{1,0:T(8,128)}, u32[]{:S(2)}) copy-start(f32[128,128]{1,0:T(8,128)} %get-tuple-element.53) | copy-start | bytes 196612
  84.5 1.4 %copy-start.10 = (f32[128,128]{1,0:T(8,128)S(1)}, f32[128,128]{1,0:T(8,128)}, u32[]{:S(2)}) copy-start(f32[128,128]{1,0:T(8,128)} %get-tuple-element.54) | copy-start | bytes 196612
  87.4 2.2 %copy-start.2 = (f32[128,64,128]{2,0,1:T(8,128)S(1)}, f32[128,64,128]{2,0,1:T(8,128)}, u32[]{:S(2)}) copy-start(f32[128,64,128]{2,0,1:T(8,128)} %fusion.20) | copy-start | bytes 12582916
  89.6 3.6 %copy-start.1 = (bf16[1,64,128,128]{3,2,1,0:T(8,128)(2,1)S(1)}, bf16[1,64,128,128]{3,2,1,0:T(8,128)(2,1)}, u32[]{:S(2)}) copy-start(bf16[1,64,128,128]{3,2,1,0:T(8,128)(2,1)} %coeff_ref) | copy-start | bytes 6291460
  93.2 12.7 %copy-start.11 = (s32[16]{0:T(128)S(1)}, s32[16]{0:T(128)}, u32[]{:S(2)}) copy-start(s32[16]{0:T(128)} %param.11) | copy-start | bytes 196

commit v5 on v4

--- a/solution.py
+++ b/solution.py
@@ -5,6 +5,7 @@
 from jax.experimental.pallas import tpu as pltpu
 from jax.sharding import PartitionSpec as P
 import functools
+
 
 sigma_fractions = (1.0 / 32.0, 1.0 / 16.0, 1.0 / 8.0, 1.0 / 4.0)
 kernel_weights = (1.0, 0.5, 0.25, 0.125)
@@ -88,13 +89,11 @@
         out_specs=pl.BlockSpec(memory_space=pltpu.VMEM),
         scratch_shapes=[pltpu.SemaphoreType.DMA((total,)), pltpu.SemaphoreType.DMA((total,))],
         compiler_params=pltpu.CompilerParams(collective_id=collective_id, has_side_effects=True),
-        name=f"gather_{collective_id}",
     )(block)
 
 
 def plane_rows(x_ref, y_ref):
-    rows, width = x_ref.shape
-    y_total = y_ref.shape[0]
+    rows, _ = x_ref.shape
     parts = []
     for row in range(rows):
         parts.append((x_ref[row : row + 1, :] * y_ref[...]).astype(jnp.bfloat16))
@@ -349,6 +348,10 @@
         ),
         name="tail",
     )(back_two, coeffs, cosines, weight, head)
+
+
+def step_body(sizes, *arrays):
+    return per_device(sizes, *arrays)
 
 
 def per_device(sizes, coeffs, v_local, atom_pos, atom_charge, near_list, live_count):
@@ -388,7 +391,6 @@
     weights = jnp.array(kernel_weights, jnp.float32)
     scaled = (weights[:, None] * charges[3][None, :]).reshape(-1)
     depth = (scaled[None, :] * z_value).astype(jnp.bfloat16)
-    field_total = slab_potential(x_value, y_value, depth, v_local)
 
     gvec_size = sizes[1]
     chunks = 2 if y_share % 32 == 0 else 1
@@ -416,10 +418,13 @@
             "naqz,yq->nayz", section_z, y_rows(step, part), preferred_element_type=jnp.float32
         ).astype(jnp.bfloat16)
 
-    arrived = [
-        [shift(section_y(-step, part), -step) for step in range(1, gvec_size)]
-        for part in range(chunks)
-    ]
+    arrived = []
+    for part in range(chunks):
+        leaving = [section_y(-step, part) for step in range(1, gvec_size)]
+        if part > 0:
+            leaving, arrived[-1], depth = lax.optimization_barrier((leaving, arrived[-1], depth))
+        arrived.append([shift(block, -step) for step, block in enumerate(leaving, 1)])
+    field_total = slab_potential(x_value, y_value, depth, v_local)
     moments = 0.0
     reals = []
     returned = []
@@ -443,9 +448,9 @@
             sent, reals = lax.optimization_barrier((sent, reals + [real_space]))
         else:
             reals.append(real_space)
-        returned.append(
-            [shift(block, step) for step, block in enumerate(sent, 1)] + [back_x(0)]
-        )
+            sent, arrived[part + 1] = lax.optimization_barrier((sent, arrived[part + 1]))
+        moved = [shift(block, step) for step, block in enumerate(sent, 1)]
+        returned.append(moved + [back_x(0)])
     for part in range(chunks):
         window = slice(part * chunk, (part + 1) * chunk)
         for band in range(local_bands):
@@ -505,7 +510,7 @@
 def solution(mesh):
     sizes = (mesh.shape["band"], mesh.shape["gvec"], mesh.shape["dom"])
     return jax.shard_map(
-        functools.partial(per_device, sizes),
+        functools.partial(step_body, sizes),
         mesh=mesh,
         in_specs=(
             P(("band", "dom"), "gvec", None, None),

time: 112 us -> 114 us (1.018)
  matrix products: 23 us -> 25.8 us
  waiting for transfers between devices: 6.7 us -> 4.24 us
  other arithmetic: 18.6 us -> 20.6 us
    convert_element_type x1 -> x2, other arithmetic: 6.38 us -> 9.22 us  [per_device(): (field_total[None, :, window] * real_space.astype(jnp.float32)).astype(jn...]
    dot_general x4, matrix products: 4.14 us -> 6.81 us  [per_device(): jnp.einsum('nayz,xa->nxyz', block, a_columns(step), preferred_element_typ...]
    ppermute x4, waiting for transfers between devices: 6.7 us -> 4.24 us  [shift(): lax.ppermute(value, 'gvec', [(at, (at + step) % gvec_size) for at in rang...]
    unnamed x32 -> x34, local copies, waits for them, and re-layouts: 4.59 us -> 2.99 us
    slice x1 -> x2, local copies, waits for them, and re-layouts: 0.07 us -> 1.59 us  [the longest x1 1.52 us: per_device(): y_value[window]]
    concatenate x4 -> x2, other arithmetic: 4.04 us -> 2.54 us  [kernels(): return (jnp.concatenate(values, axis=1), jnp.concatenate(slopes, axis=1))]
  transfers between devices with their start and end apart: 4 -> 4, of which waited for: 1 -> 2; matrix products, arithmetic and copies ran while one was open for 16% -> 25% of each run, Pallas kernels for 20% -> 19%
where the time goes in v5:
time: 114 us; the launch traced here: 113 us
  Pallas kernels  46.7 us (41%)
  matrix products  25.8 us (23%)
  other arithmetic  20.6 us (18%)
  local copies, waits for them, and re-layouts  7.98 us (7%)
  starting transfers between devices  4.62 us (4%)
  waiting for transfers between devices  4.24 us (4%)
  between operations  3.02 us (3%)
    pallas_call x2, Pallas kernels, slab_moments(): pl.pallas_call(force_kernel, grid=(x_total // rows,), out_shape=jax.Shape...  14 us
    pallas_call x1, Pallas kernels, gather_all(): pl.pallas_call(functools.partial(gather_kernel, sizes), out_shape=jax.Sha...  13.3 us
    pallas_call x1, Pallas kernels, tail(): pl.pallas_call(functools.partial(tail_kernel, sizes, base), out_shape=(ja...  11.6 us
    dot_general x4, matrix products, per_device(): jnp.einsum('nayz,yq->naqz', block, y_rows(step, part), preferred_element_...  9.89 us
    convert_element_type x2, other arithmetic, per_device(): (field_total[None, :, window] * real_space.astype(jnp.float32)).astype(jn...  9.22 us
    pallas_call x1, Pallas kernels, slab_potential(): pl.pallas_call(potential_kernel, grid=(x_total // rows,), out_shape=jax.S...  7.83 us
    dot_general x4, matrix products, per_device(): jnp.einsum('nayz,xa->nxyz', block, a_columns(step), preferred_element_typ...  6.81 us
    ppermute x4, starting transfers between devices, shift(): lax.ppermute(value, 'gvec', [(at, (at + step) % gvec_size) for at in rang...  4.62 us
  transfers between devices with their start and end apart: 4, of which 2 were waited for; matrix products, arithmetic and copies ran while one was open for 25% of the time, Pallas kernels for 19%

profile of v5, /device:TPU:0, one launch (start us, length us, event | category | flops | bytes accessed | tf_op | source)
XLA Modules:
  0.0 113.0 jit_solution(13246943147403729793)
XLA Ops:
  1.3 0.7 compare_select_fusion.2
  2.0 0.9 copy.55
  3.0 0.6 gather_fusion.1
  3.6 0.6 gather_fusion
  4.2 0.7 fusion.131
  4.9 0.6 select_maximum_fusion.2.x_ref
  5.5 13.3 %shard_map.110 = f32[32,8,128]{2,1,0:T(8,128)} custom-call(f32[8,128]{1,0:T(8,128)} %select_maximum_fusion.2.x_ref), custom_call_target="tpu_custom_call" | custom-call | tf_op jit(solution)/shard_map/pallas_call | solution.py:85
  18.8 0.9 slice_bitcast_fusion.3
  21.1 2.6 %fusion.7 = bf16[64,128,128]{2,1,0:T(8,128)(2,1)S(1)} fusion(bf16[1,64,128,128]{3,2,1,0:T(8,128)(2,1)} %coeff_ref, f32[128]{0:T(128)S(1)} %compare_select_fusion.4, f32[128]{0:T(128)S(1)} %iota_convert_fusion, f32[128]{0:T(128)S(1)} %add_multiply_fusion.1), kind=kOutput, calls=%fused_computation.14 | convolution fusion | flops 269549568 | bytes 4195840 | tf_op jit(solution)/shard_map/naql,zl->naqz/dot_general | solution.py:412
  23.6 1.2 %fusion.57 = (f32[128,128]{1,0:T(8,128)}, f32[128,128]{1,0:T(8,128)}, f32[128,128]{1,0:T(8,128)}, f32[128,128]{1,0:T(8,128)}, f32[128,128]{1,0:T(8,128)S(1)}, /*...) fusion(f32[128]{0:T(128)S(1)} %get-tuple-element.53, ...), kind=kLoop, calls=%fused_computation.119 | loop fusion | flops 622592 | bytes 1083904 | tf_op jit(solution)/shard_map/mul | solution.py:36
  24.9 1.2 %fusion.11 = bf16[1,64,32,128]{3,2,1,0:T(8,128)(2,1)} fusion(bf16[64,128,128]{2,1,0:T(8,128)(2,1)S(1)} %fusion.7, bf16[128,128]{1,0:T(8,128)(2,1)S(1)} %get-tuple-element.91.table_ref, s32[]{:T(128)S(6)} %select_n.104), kind=kOutput, calls=%fused_computation.24 | convolution fusion | flops 67371008 | bytes 2629636 | tf_op jit(solution)/shard_map/naqz,yq->nayz/dot_general | solution.py:417
  26.1 1.1 %collective-permute-start = (bf16[1,64,32,128]{3,2,1,0:T(8,128)(2,1)}, bf16[1,64,32,128]{3,2,1,0:T(8,128)(2,1)}, u32[]{:S(2)}, u32[]{:S(2)}) collective-permute-start(bf16[1,64,32,128]{3,2,1,0:T(8,128)(2,1)} %fusion.11), channel_id=1, source_target_pairs={{0,4},{4,0},{1,5},{5,1},{2,6},{6,2},{3,7},{7,3},{8,12},{12,8},{9,1... | collective-permute-start | bytes 1572872 | tf_op jit(solution)/shard_map/ppermute | solution.py:408
  27.4 0.7 pad_maximum_fusion.3
  28.1 0.7 fusion.137
  29.6 1.2 %fusion.10 = bf16[1,64,32,128]{3,2,1,0:T(8,128)(2,1)} fusion(bf16[64,128,128]{2,1,0:T(8,128)(2,1)S(1)} %fusion.7, bf16[128,128]{1,0:T(8,128)(2,1)S(1)} %get-tuple-element.91.table_ref, s32[]{:T(128)S(6)} %select_n.109), kind=kOutput, calls=%fused_computation.23 | convolution fusion | flops 67371008 | bytes 2629636 | tf_op jit(solution)/shard_map/naqz,yq->nayz/dot_general | solution.py:417
  30.9 0.5 fusion.36
  31.4 0.7 multiply_convert_fusion.depth_ref
  32.1 1.9 %pad_maximum_fusion = (f32[128,512]{1,0:T(8,128)}, f32[128,512]{1,0:T(8,128)}) fusion(f32[128,128]{1,0:T(8,128)} %get-tuple-element.86, f32[128,128]{1,0:T(8,128)} %get-tuple-element.84, f32[128,128]{1,0:T(8,128)} %get-tuple-element.85, f32[128,128]{1,0:T(8,128)S(1)} %get-tuple-element.83, f32[128,128]{1,0:T(8,128)} %get-tuple-element.89, ...), kind=kLoop, calls=%fused_computation.81 | loop fusion | flops 393216 | bytes 1048576 | tf_op jit(solution)/shard_map/concatenate | solution.py:37
  34.0 1.5 %fusion.138 = (f32[32,512]{1,0:T(8,128)}, f32[32,512]{1,0:T(8,128)}) fusion(f32[64,512]{1,0:T(8,128)} %get-tuple-element.94.y_ref), kind=kLoop, calls=%fused_computation.245 | loop fusion | bytes 262144 | tf_op jit(solution)/shard_map/slice | solution.py:458
  35.5 1.8 %fusion.28 = f32[128,32,128]{2,0,1:T(8,128)} fusion(bf16[64,32,128]{2,1,0:T(8,128)(2,1)S(1)} %fusion.13, bf16[128,128]{1,0:T(8,128)(2,1)S(1)} %get-tuple-element.91.table_ref, s32[]{:T(128)S(6)} %select_n.110), kind=kOutput, calls=%fused_computation.40 | convolution fusion | flops 67108864 | bytes 2654212 | tf_op jit(solution)/shard_map/nayz,xa->nxyz/dot_general | solution.py:436
  37.3 2.7 %collective-permute-done = bf16[1,64,32,128]{3,2,1,0:T(8,128)(2,1)} collective-permute-done((bf16[1,64,32,128]{3,2,1,0:T(8,128)(2,1)}, bf16[1,64,32,128]{3,2,1,0:T(8,128)(2,1)}, u32[]{:S(2)}, u32[]{:S(2)}) %collective-permute-start) | collective-permute-done | bytes 524320 | tf_op jit(solution)/shard_map/ppermute | solution.py:408
  40.0 1.4 %collective-permute-start.1 = (bf16[1,64,32,128]{3,2,1,0:T(8,128)(2,1)S(1)}, bf16[1,64,32,128]{3,2,1,0:T(8,128)(2,1)}, u32[]{:S(2)}, u32[]{:S(2)}) collective-permute-start(bf16[1,64,32,128]{3,2,1,0:T(8,128)(2,1)S(1)} %copy-done.6), channel_id=1, source_target_pairs={{0,4},{4,0},{1,5},{5,1},{2,6},{6,2},{3,7},{7,3},{8,12},{12,8},{9,1... | collective-permute-start | bytes 1572872 | tf_op jit(solution)/shard_map/ppermute | solution.py:408
  41.4 2.9 %fusion.34 = f32[128,32,128]{2,0,1:T(8,128)} fusion(bf16[64,32,128]{2,1,0:T(8,128)(2,1)} %bitcast.25, bf16[128,128]{1,0:T(8,128)(2,1)S(1)} %get-tuple-element.91.table_ref, s32[]{:T(128)S(6)} %select_n.104), kind=kOutput, calls=%fused_computation.46 | convolution fusion | flops 67108864 | bytes 2654212 | tf_op jit(solution)/shard_map/nayz,xa->nxyz/dot_general | solution.py:436
  44.3 7.8 %slab_potential.1 = f32[128,64,128]{2,1,0:T(8,128)} custom-call(f32[128,512]{1,0:T(8,128)} %get-tuple-element.92.x_ref.xv_ref, f32[64,512]{1,0:T(8,128)} %get-tuple-element.94.y_ref, bf16[128,512]{1,0:T(8,128)(2,1)} %multiply_convert_fusion.depth_ref, bf16[128,64,128]{2,1,0:T(8,128)(2,1)} %local_ref.1), custom_call_target="tpu_custom_call" | custom-call | flops 4294967296 | bytes 6291456 | tf_op jit(solution)/shard_map/slab_potential/pallas_call | solution.py:118
  52.1 5.8 %fusion.2 = (bf16[128,32,128]{2,1,0:T(8,128)(2,1)S(1)}, bf16[128,32,128]{2,1,0:T(8,128)(2,1)}) fusion(f32[128,64,128]{2,1,0:T(8,128)} %slab_potential.1, f32[128,32,128]{2,0,1:T(8,128)} %fusion.34, f32[128,32,128]{2,0,1:T(8,128)S(1)} %fusion.36), kind=kLoop, calls=%fused_computation.7 | loop fusion | flops 2621440 | bytes 8388608 | tf_op jit(solution)/shard_map/convert_element_type | solution.py:439
  57.9 0.5 convolution_convert_fusion.2
  58.4 0.5 fusion.14
  58.9 2.8 %fusion.30 = f32[128,64,128]{2,0,1:T(8,128)} fusion(bf16[64,32,128]{2,0,1:T(8,128)(2,1)S(1)} %convolution_convert_fusion.2, bf16[128,128]{1,0:T(8,128)(2,1)S(1)} %get-tuple-element.91.table_ref, s32[]{:T(128)S(6)} %select_n.111), kind=kOutput, calls=%fused_computation.42 | convolution fusion | flops 67108864 | bytes 4726788 | tf_op jit(solution)/shard_map/nayz,yq->naqz/dot_general | solution.py:473
  61.7 1.7 %fusion.26 = f32[128,32,128]{2,0,1:T(8,128)S(1)} fusion(bf16[64,32,128]{2,1,0:T(8,128)(2,1)} %bitcast.36, bf16[128,128]{1,0:T(8,128)(2,1)S(1)} %get-tuple-element.91.table_ref, s32[]{:T(128)S(6)} %select_n.104), kind=kOutput, calls=%fused_computation.38 | convolution fusion | flops 67108864 | bytes 2654212 | tf_op jit(solution)/shard_map/nayz,xa->nxyz/dot_general | solution.py:436
  63.6 3.5 %fusion.1 = (bf16[128,32,128]{2,1,0:T(8,128)(2,1)S(1)}, bf16[128,32,128]{2,1,0:T(8,128)(2,1)}) fusion(f32[128,64,128]{2,1,0:T(8,128)S(1)} %copy-done.4, f32[128,32,128]{2,0,1:T(8,128)S(1)} %fusion.26, f32[128,32,128]{2,0,1:T(8,128)S(1)} %copy-done.3), kind=kLoop, calls=%fused_computation.5 | loop fusion | flops 2621440 | bytes 8388608 | tf_op jit(solution)/shard_map/convert_element_type | solution.py:439
  67.1 0.5 convolution_convert_fusion
  67.6 0.5 fusion.15
  68.1 0.7 collective-permute-start.2
  68.8 1.4 %collective-permute-start.3 = (bf16[1,64,32,128]{3,1,2,0:T(8,128)(2,1)S(1)}, bf16[1,64,32,128]{3,1,2,0:T(8,128)(2,1)S(1)}, u32[]{:S(2)}, u32[]{:S(2)}) collective-permute-start(bf16[1,64,32,128]{3,1,2,0:T(8,128)(2,1)S(1)} %fusion.15), channel_id=1, source_target_pairs={{0,4},{4,0},{1,5},{5,1},{2,6},{6,2},{3,7},{7,3},{8,12},{12,8},{9,1... | collective-permute-start | bytes 1572872 | tf_op jit(solution)/shard_map/ppermute | solution.py:408
  70.2 2.7 %fusion.20 = f32[128,64,128]{2,0,1:T(8,128)} fusion(bf16[64,32,128]{2,0,1:T(8,128)(2,1)S(1)} %convolution_convert_fusion, bf16[128,128]{1,0:T(8,128)(2,1)S(1)} %get-tuple-element.91.table_ref, s32[]{:T(128)S(6)} %select_n.112), kind=kOutput, calls=%fused_computation.34 | convolution fusion | flops 67108864 | bytes 4726788 | tf_op jit(solution)/shard_map/nayz,yq->naqz/dot_general | solution.py:473
  72.9 7.0 %slab_moments.2 = f32[3,128,512]{2,1,0:T(8,128)} custom-call(f32[128,512]{1,0:T(8,128)} %get-tuple-element.92.x_ref.xv_ref, f32[128,512]{1,0:T(8,128)} %get-tuple-element.93.xs_ref, f32[32,512]{1,0:T(8,128)} %get-tuple-element.49.yv_ref, f32[32,512]{1,0:T(8,128)} %get-tuple-element.47.ys_ref, bf16[128,32,128]{2,1,0:T(8,128)(2,1)} %get-tuple-element.41), custom_call_target="tpu_custom_call" | custom-call | flops 3221225472 | bytes 1048576 | tf_op jit(solution)/shard_map/slab_moments/pallas_call | solution.py:159
  79.9 7.1 %slab_moments.3 = f32[3,128,512]{2,1,0:T(8,128)} custom-call(f32[128,512]{1,0:T(8,128)} %get-tuple-element.92.x_ref.xv_ref, f32[128,512]{1,0:T(8,128)} %get-tuple-element.93.xs_ref, f32[32,512]{1,0:T(8,128)} %get-tuple-element.48.yv_ref, f32[32,512]{1,0:T(8,128)} %get-tuple-element.46.ys_ref, bf16[128,32,128]{2,1,0:T(8,128)(2,1)} %get-tuple-element.39), custom_call_target="tpu_custom_call" | custom-call | flops 3221225472 | bytes 1048576 | tf_op jit(solution)/shard_map/slab_moments/pallas_call | solution.py:159
  87.0 1.3 %add_multiply_fusion = f32[3,128,512]{2,1,0:T(8,128)S(1)} fusion(f32[3,128,512]{2,1,0:T(8,128)S(1)} %copy-done.5, f32[3,128,512]{2,1,0:T(8,128)} %slab_moments.3, f32[]{:T(128)} %div.94), kind=kLoop, calls=%fused_computation.33 | loop fusion | flops 393216 | bytes 2359300 | tf_op jit(solution)/shard_map/add | solution.py:457
  88.4 0.7 fusion.41
  89.9 0.7 fusion.32
  90.6 1.6 %collective-permute-done.3 = bf16[1,64,32,128]{3,1,2,0:T(8,128)(2,1)S(1)} collective-permute-done((bf16[1,64,32,128]{3,1,2,0:T(8,128)(2,1)S(1)}, bf16[1,64,32,128]{3,1,2,0:T(8,128)(2,1)S(1)}, u32[]{:S(2)}, u32[]{:S(2)}) %collective-permute-start.3) | collective-permute-done | bytes 524320 | tf_op jit(solution)/shard_map/ppermute | solution.py:408
  92.2 3.7 %fusion.back_ref = bf16[1,64,128,128]{3,2,1,0:T(8,128)(2,1)S(1)} fusion(f32[128,64,128]{2,0,1:T(8,128)} %fusion.20, f32[128,64,128]{2,0,1:T(8,128)S(1)} %fusion.32, f32[128,64,128]{2,0,1:T(8,128)S(1)} %copy-done.2, bf16[64,32,128]{2,0,1:T(8,128)(2,1)S(1)} %bitcast.173, bf16[128,128]{1,0:T(8,128)(2,1)S(1)} %get-tuple-element.91.table_ref, s32[]{:T(128)S(6)} %select_n.109), kind=kOutput, calls=%fused_computation.3 | convolution fusion | flops 71303168 | bytes 15212548 | tf_op jit(solution)/shard_map/nayz,yq->naqz/dot_general | solution.py:473
  95.9 11.6 %tail.1 = (bf16[1,64,128,128]{3,2,1,0:T(8,128)(2,1)S(1)}, f32[32,8,128]{2,1,0:T(8,128)S(1)}) custom-call(bf16[1,64,128,128]{3,2,1,0:T(8,128)(2,1)S(1)} %fusion.back_ref, bf16[1,64,128,128]{3,2,1,0:T(8,128)(2,1)S(1)} %copy-done.1, bf16[128,128]{1,0:T(8,128)(2,1)S(1)} %get-tuple-element.91.table_ref, f32[1,128]{1,0:T(1,128)S(1)} %pad_bitcast_fusion.weight_ref, ...), custom_call_target="tpu_custom_call" | custom-call | tf_op jit(solution)/shard_map/tail/pallas_call | solution.py:331
  107.8 0.8 fusion.61
  109.2 0.6 fusion.114
  109.9 0.6 select_reduce_fusion
  111.1 0.6 pad_maximum_fusion.5
  111.7 1.3 %copy.154 = bf16[1,64,128,128]{3,2,1,0:T(8,128)(2,1)} copy(bf16[1,64,128,128]{3,2,1,0:T(8,128)(2,1)S(1)} %get-tuple-element.101) | data formatting | bytes 4194304
  (72 shorter events, 3.7 us)
Async XLA Ops:
  0.6 2.3 %copy-start = (f32[1024]{0:T(1024)S(1)}, f32[1024]{0:T(1024)}, u32[]{:S(2)}) copy-start(f32[1024]{0:T(1024)} %param.10) | copy-start | bytes 12292
  26.1 13.9 %collective-permute-start = (bf16[1,64,32,128]{3,2,1,0:T(8,128)(2,1)}, bf16[1,64,32,128]{3,2,1,0:T(8,128)(2,1)}, u32[]{:S(2)}, u32[]{:S(2)}) collective-permute-start(bf16[1,64,32,128]{3,2,1,0:T(8,128)(2,1)} %fusion.11), channel_id=1, source_target_pairs={{0,4},{4,0},{1,5},{5,1},{2,6},{6,2},{3,7},{7,3},{8,12},{12,8},{9,1... | collective-permute-start | bytes 1572872 | tf_op jit(solution)/shard_map/ppermute | solution.py:408
  29.2 1.7 %copy-start.13 = (f32[4]{0:T(128)S(1)}, f32[4]{0:T(128)}, u32[]{:S(2)}) copy-start(f32[4]{0:T(128)} %constant.154.clone) | copy-start | bytes 52
  31.4 8.6 %copy-start.6 = (bf16[1,64,32,128]{3,2,1,0:T(8,128)(2,1)S(1)}, bf16[1,64,32,128]{3,2,1,0:T(8,128)(2,1)}, u32[]{:S(2)}) copy-start(bf16[1,64,32,128]{3,2,1,0:T(8,128)(2,1)} %fusion.10) | copy-start | bytes 1572868
  40.0 21.7 %collective-permute-start.1 = (bf16[1,64,32,128]{3,2,1,0:T(8,128)(2,1)S(1)}, bf16[1,64,32,128]{3,2,1,0:T(8,128)(2,1)}, u32[]{:S(2)}, u32[]{:S(2)}) collective-permute-start(bf16[1,64,32,128]{3,2,1,0:T(8,128)(2,1)S(1)} %copy-done.6), channel_id=1, source_target_pairs={{0,4},{4,0},{1,5},{5,1},{2,6},{6,2},{3,7},{7,3},{8,12},{12,8},{9,1... | collective-permute-start | bytes 1572872 | tf_op jit(solution)/shard_map/ppermute | solution.py:408
  58.9 4.4 %copy-start.4 = (f32[128,64,128]{2,1,0:T(8,128)S(1)}, f32[128,64,128]{2,1,0:T(8,128)}, u32[]{:S(2)}) copy-start(f32[128,64,128]{2,1,0:T(8,128)} %slab_potential.1) | copy-start | bytes 12582916
  61.7 1.9 %copy-start.3 = (f32[128,32,128]{2,0,1:T(8,128)S(1)}, f32[128,32,128]{2,0,1:T(8,128)}, u32[]{:S(2)}) copy-start(f32[128,32,128]{2,0,1:T(8,128)} %fusion.28) | copy-start | bytes 6291460
  68.1 21.8 %collective-permute-start.2 = (bf16[1,64,32,128]{3,1,2,0:T(8,128)(2,1)S(1)}, bf16[1,64,32,128]{3,1,2,0:T(8,128)(2,1)S(1)}, u32[]{:S(2)}, u32[]{:S(2)}) collective-permute-start(bf16[1,64,32,128]{3,1,2,0:T(8,128)(2,1)S(1)} %fusion.14), channel_id=1, source_target_pairs={{0,4},{4,0},{1,5},{5,1},{2,6},{6,2},{3,7},{7,3},{8,12},{12,8},{9,1... | collective-permute-start | bytes 1572872 | tf_op jit(solution)/shard_map/ppermute | solution.py:408
  68.8 23.4 %collective-permute-start.3 = (bf16[1,64,32,128]{3,1,2,0:T(8,128)(2,1)S(1)}, bf16[1,64,32,128]{3,1,2,0:T(8,128)(2,1)S(1)}, u32[]{:S(2)}, u32[]{:S(2)}) collective-permute-start(bf16[1,64,32,128]{3,1,2,0:T(8,128)(2,1)S(1)} %fusion.15), channel_id=1, source_target_pairs={{0,4},{4,0},{1,5},{5,1},{2,6},{6,2},{3,7},{7,3},{8,12},{12,8},{9,1... | collective-permute-start | bytes 1572872 | tf_op jit(solution)/shard_map/ppermute | solution.py:408
  79.9 7.1 %copy-start.5 = (f32[3,128,512]{2,1,0:T(8,128)S(1)}, f32[3,128,512]{2,1,0:T(8,128)}, u32[]{:S(2)}) copy-start(f32[3,128,512]{2,1,0:T(8,128)} %slab_moments.2) | copy-start | bytes 2359300
  87.0 1.4 %copy-start.7 = (bf16[128,512]{1,0:T(8,128)(2,1)S(1)}, bf16[128,512]{1,0:T(8,128)(2,1)}, u32[]{:S(2)}) copy-start(bf16[128,512]{1,0:T(8,128)(2,1)} %multiply_convert_fusion.depth_ref) | copy-start | bytes 393220
  87.0 1.4 %copy-start.8 = (f32[128,128]{1,0:T(8,128)S(1)}, f32[128,128]{1,0:T(8,128)}, u32[]{:S(2)}) copy-start(f32[128,128]{1,0:T(8,128)} %get-tuple-element.59) | copy-start | bytes 196612
  87.0 1.4 %copy-start.9 = (f32[128,128]{1,0:T(8,128)S(1)}, f32[128,128]{1,0:T(8,128)}, u32[]{:S(2)}) copy-start(f32[128,128]{1,0:T(8,128)} %get-tuple-element.60) | copy-start | bytes 196612
  87.0 1.4 %copy-start.10 = (f32[128,128]{1,0:T(8,128)S(1)}, f32[128,128]{1,0:T(8,128)}, u32[]{:S(2)}) copy-start(f32[128,128]{1,0:T(8,128)} %get-tuple-element.61) | copy-start | bytes 196612
  87.0 1.4 %copy-start.11 = (f32[128,128]{1,0:T(8,128)S(1)}, f32[128,128]{1,0:T(8,128)}, u32[]{:S(2)}) copy-start(f32[128,128]{1,0:T(8,128)} %get-tuple-element.62) | copy-start | bytes 196612
  89.9 2.3 %copy-start.2 = (f32[128,64,128]{2,0,1:T(8,128)S(1)}, f32[128,64,128]{2,0,1:T(8,128)}, u32[]{:S(2)}) copy-start(f32[128,64,128]{2,0,1:T(8,128)} %fusion.30) | copy-start | bytes 12582916
  92.2 3.7 %copy-start.1 = (bf16[1,64,128,128]{3,2,1,0:T(8,128)(2,1)S(1)}, bf16[1,64,128,128]{3,2,1,0:T(8,128)(2,1)}, u32[]{:S(2)}) copy-start(bf16[1,64,128,128]{3,2,1,0:T(8,128)(2,1)} %coeff_ref) | copy-start | bytes 6291460
  95.9 11.9 %copy-start.12 = (s32[16]{0:T(128)S(1)}, s32[16]{0:T(128)}, u32[]{:S(2)}) copy-start(s32[16]{0:T(128)} %param.11) | copy-start | bytes 196
